TPU v7x, 32 devices: a whole 2x2x4 slice. The times are simulated.
32 devices in a mesh: parts: 2 (over y), blk: 4 (over z), sub: 4 (over x, core).
Axes of the slice: x: 2, y: 2, z: 4, core: 2. Of those that a mesh axis runs over, the one named last changes fastest.
Arguments:
- readings: float32 [2, 24576, 256], P(None, ('parts', 'blk', 'sub')), parts along dimension 1, may hold values from -6 to 6
- coverage: int32 [2, 24576, 256], P(None, ('parts', 'blk', 'sub')), parts along dimension 1, may hold values 0 or 1
- pixel_factors: float32 [24576, 256], P(('parts', 'blk', 'sub')), parts along dimension 0, may hold values from -1.5 to 1.5
- date_factors: float32 [2048, 256], P(('parts', 'blk', 'sub')), parts along dimension 0, may hold values from -1.5 to 1.5
Outputs:
- pixel_out: float32 [24576, 256], P(('parts', 'blk', 'sub')), parts along dimension 0
- date_out: float32 [2048, 256], P(('parts', 'blk', 'sub')), parts along dimension 0
There are 2 independent parts, one for each index of `parts`. A program takes and returns all parts, laid end to end along the dimension named above; each array names one. Nothing has to cross between parts.
All inputs are finite; a program needn't handle non-finite values. No bound on the sum of `coverage` on one device may be relied on, other than what follows from the above.
Results may differ from a plain program's by a relative error of at most 0.0001.
Values sent between devices are 32-bit elements; how exact they have to be, the bound alone decides.
No kernel may reach another device: no remote copies, remote signals or barrier semaphores. Data moves between devices by JAX's collectives and lax.ppermute only.
A program may use at most 64 MiB of HBM per device.

v0:
```python
import jax
import jax.numpy as jnp
from jax import lax
from jax.sharding import PartitionSpec as P

STRATA = 2


step_size = 0.05
ridge = 0.1
epsilon = 1e-06


def from_behind(value, axis, steps):
    count = lax.axis_size(axis)
    pairs = [(source, (source + steps) % count) for source in range(count)]
    return lax.ppermute(value, axis, pairs)


def local_terms(values, weights, strip, block):
    hp = lax.Precision.HIGHEST
    predicted = lax.dot_general(strip, block, (((1,), (1,)), ((), ())), precision=hp)
    errors = weights * (values - predicted)
    pixel_grad = -jnp.dot(errors, block, precision=hp) + ridge * strip
    date_part = -lax.dot_general(errors, strip, (((0,), (0,)), ((), ())), precision=hp)
    return (pixel_grad, date_part)


def on_device(readings, coverage, pixel_factors, date_factors):
    strip = pixel_factors
    share_rows = date_factors.shape[0]
    groups = lax.axis_size("sub")
    block_rows = share_rows * groups
    pixel_count = strip.shape[0] * groups * strip.shape[1]
    date_count = block_rows * strip.shape[1]
    share = date_factors
    for stratum in range(STRATA):
        block = lax.all_gather(share, "sub", axis=0, tiled=True)
        values = readings[stratum]
        weights = coverage[stratum].astype(jnp.float32)
        pixel_grad, date_part = local_terms(values, weights, strip, block)
        own_part = lax.psum_scatter(date_part, "sub", scatter_dimension=0, tiled=True)
        date_grad = own_part + ridge * share
        pixel_sq, date_sq = lax.psum(
            (jnp.sum(pixel_grad * pixel_grad), jnp.sum(date_grad * date_grad)), "sub"
        )
        strip = strip - step_size * pixel_grad / jnp.sqrt(pixel_sq / pixel_count + epsilon)
        share = share - step_size * date_grad / jnp.sqrt(date_sq / date_count + epsilon)
        share = from_behind(share, "blk", 1)
    return (strip, share)


def solution(mesh):
    in_specs = (
        P(None, ("parts", "blk", "sub"), None),
        P(None, ("parts", "blk", "sub"), None),
        P(("parts", "blk", "sub"), None),
        P(("parts", "blk", "sub"), None),
    )
    out_specs = (P(("parts", "blk", "sub"), None), P(("parts", "blk", "sub"), None))
    return jax.shard_map(
        on_device, mesh=mesh, in_specs=in_specs, out_specs=out_specs, check_vma=False
    )
```

profile of v0, /device:TPU:0, one launch (start us, length us, event | category | flops | bytes accessed | tf_op | source)
XLA Modules:
  0.0 109.8 jit_solution(7786691914013596123)
XLA Ops:
  7.2 7.4 %all_gather.6 = f32[256,256]{1,0:T(8,128)S(1)} all-gather(f32[64,256]{1,0:T(8,128)} %param.7), channel_id=1, replica_groups=mesh['parts'=2,'blk'=4,'sub'=4] {'sub'}, dimensions={0}, use_global_device_ids=true | all-gather | bytes 327680 | tf_op jit(solution)/shard_map/all_gather | solution.py:38
  14.6 2.5 %fusion.3 = f32[768,256]{1,0:T(8,128)S(1)} fusion(f32[768,256]{1,0:T(8,128)} %param.6, f32[256,256]{1,0:T(8,128)S(1)} %all_gather.6, f32[2,768,256]{2,1,0:T(8,128)} %param.4, s32[2,768,256]{2,1,0:T(8,128)} %param.5), kind=kOutput, calls=%fused_computation.7 | convolution fusion | flops 604569600 | bytes 3407872 | tf_op jit(solution)/shard_map/dot_general | solution.py:22
  17.2 2.1 %convolution_negate_fusion.3 = f32[256,256]{1,0:T(8,128)} fusion(f32[768,256]{1,0:T(8,128)S(1)} %fusion.3, f32[768,256]{1,0:T(8,128)S(1)} %copy-done), kind=kOutput, calls=%fused_computation.9 | convolution fusion | flops 604045312 | bytes 1835008 | tf_op jit(solution)/shard_map/dot_general | solution.py:25
  19.3 0.0 reduce-scatter.5.cloned.1.call-start
  19.4 1.4 %multiply_reduce_fusion.1 = (f32[]{:T(128)}, f32[768,256]{1,0:T(8,128)S(1)}) fusion(f32[768,256]{1,0:T(8,128)S(1)} %copy-done, f32[768,256]{1,0:T(8,128)S(1)} %fusion.3, f32[256,256]{1,0:T(8,128)S(1)} %all_gather.6), kind=kOutput, calls=%fused_computation.13 | convolution fusion | flops 604962816 | bytes 2621444 | tf_op jit(solution)/shard_map/dot_general | solution.py:24
  20.8 20.0 %reduce-scatter.3.cloned.1.call-done = f32[64,256]{1,0:T(8,128)} async-done(((f32[256,256]{1,0:T(8,128)}), f32[64,256]{1,0:T(8,128)}) %reduce-scatter.3.cloned.1.call-update) | async-done | bytes 65552 | tf_op jit(solution)/shard_map/reduce_scatter | solution.py:42
  40.8 1.5 %multiply_reduce_fusion.3 = f32[]{:T(128)} fusion(f32[64,256]{1,0:T(8,128)} %reduce-scatter.3.cloned.1.call-done, f32[64,256]{1,0:T(8,128)S(1)} %copy-done.1), kind=kLoop, calls=%fused_computation.18 | loop fusion | flops 65535 | bytes 131076 | tf_op jit(solution)/shard_map/reduce_sum | solution.py:45
  42.3 6.4 %all-reduce.1 = (f32[]{:T(128)}, f32[]{:T(128)}) all-reduce(f32[]{:T(128)} %get-tuple-element.6, f32[]{:T(128)} %multiply_reduce_fusion.3), channel_id=1, replica_groups=mesh['parts'=2,'blk'=4,'sub'=4] {'sub'}, use_global_device_ids=true, to_apply=%region_1.0 | all-reduce | flops 2 | bytes 16 | tf_op jit(solution)/shard_map/psum | solution.py:44
  50.0 0.9 divide_subtract_fusion.3
  50.9 1.7 %collective-permute-start = (f32[64,256]{1,0:T(8,128)S(1)}, f32[64,256]{1,0:T(8,128)S(1)}, u32[]{:S(2)}, u32[]{:S(2)}) collective-permute-start(f32[64,256]{1,0:T(8,128)S(1)} %divide_subtract_fusion.3), channel_id=1, source_target_pairs={{0,4},{4,8},{8,12},{12,0},{1,5},{5,9},{9,13},{13,1},{2,6},{6,10},{... | collective-permute-start | bytes 196616 | tf_op jit(solution)/shard_map/ppermute | solution.py:17
  52.6 0.1 divide_subtract_fusion.1
  52.7 4.3 %collective-permute-done = f32[64,256]{1,0:T(8,128)S(1)} collective-permute-done((f32[64,256]{1,0:T(8,128)S(1)}, f32[64,256]{1,0:T(8,128)S(1)}, u32[]{:S(2)}, u32[]{:S(2)}) %collective-permute-start) | collective-permute-done | bytes 65568 | tf_op jit(solution)/shard_map/ppermute | solution.py:17
  57.0 5.8 %all_gather.7 = f32[256,256]{1,0:T(8,128)S(1)} all-gather(f32[64,256]{1,0:T(8,128)S(1)} %collective-permute-done), channel_id=1, replica_groups=mesh['parts'=2,'blk'=4,'sub'=4] {'sub'}, dimensions={0}, use_global_device_ids=true | all-gather | bytes 327680 | tf_op jit(solution)/shard_map/all_gather | solution.py:38
  62.8 2.2 %fusion.2 = f32[768,256]{1,0:T(8,128)S(1)} fusion(f32[768,256]{1,0:T(8,128)S(1)} %divide_subtract_fusion.1, f32[256,256]{1,0:T(8,128)S(1)} %all_gather.7, f32[2,768,256]{2,1,0:T(8,128)} %param.4, s32[2,768,256]{2,1,0:T(8,128)} %param.5), kind=kOutput, calls=%fused_computation.5 | convolution fusion | flops 604569600 | bytes 3407872 | tf_op jit(solution)/shard_map/dot_general | solution.py:22
  65.0 2.1 %convolution_negate_fusion.2 = f32[256,256]{1,0:T(8,128)} fusion(f32[768,256]{1,0:T(8,128)S(1)} %fusion.2, f32[768,256]{1,0:T(8,128)S(1)} %divide_subtract_fusion.1), kind=kOutput, calls=%fused_computation.8 | convolution fusion | flops 604045312 | bytes 1835008 | tf_op jit(solution)/shard_map/dot_general | solution.py:25
  67.1 1.4 %multiply_reduce_fusion = (f32[]{:T(128)}, f32[768,256]{1,0:T(8,128)S(1)}) fusion(f32[768,256]{1,0:T(8,128)S(1)} %divide_subtract_fusion.1, f32[768,256]{1,0:T(8,128)S(1)} %fusion.2, f32[256,256]{1,0:T(8,128)S(1)} %all_gather.7), kind=kOutput, calls=%fused_computation.11 | convolution fusion | flops 604962816 | bytes 2621444 | tf_op jit(solution)/shard_map/dot_general | solution.py:24
  68.5 17.6 %reduce-scatter.5.cloned.1.call-done = f32[64,256]{1,0:T(8,128)} async-done(((f32[256,256]{1,0:T(8,128)}), f32[64,256]{1,0:T(8,128)}) %reduce-scatter.5.cloned.1.call-update) | async-done | bytes 65552 | tf_op jit(solution)/shard_map/reduce_scatter | solution.py:42
  86.1 1.5 %multiply_reduce_fusion.2 = f32[]{:T(128)} fusion(f32[64,256]{1,0:T(8,128)} %reduce-scatter.5.cloned.1.call-done, f32[64,256]{1,0:T(8,128)S(1)} %collective-permute-done), kind=kLoop, calls=%fused_computation.15 | loop fusion | flops 65535 | bytes 131076 | tf_op jit(solution)/shard_map/reduce_sum | solution.py:45
  87.6 6.4 %all-reduce = (f32[]{:T(128)}, f32[]{:T(128)}) all-reduce(f32[]{:T(128)} %get-tuple-element.8, f32[]{:T(128)} %multiply_reduce_fusion.2), channel_id=1, replica_groups=mesh['parts'=2,'blk'=4,'sub'=4] {'sub'}, use_global_device_ids=true, to_apply=%region_6.0 | all-reduce | flops 2 | bytes 16 | tf_op jit(solution)/shard_map/psum | solution.py:44
  95.3 0.9 divide_subtract_fusion.2
  96.2 1.7 %collective-permute-start.1 = (f32[64,256]{1,0:T(8,128)S(1)}, f32[64,256]{1,0:T(8,128)S(1)}, u32[]{:S(2)}, u32[]{:S(2)}) collective-permute-start(f32[64,256]{1,0:T(8,128)S(1)} %divide_subtract_fusion.2), channel_id=1, source_target_pairs={{0,4},{4,8},{8,12},{12,0},{1,5},{5,9},{9,13},{13,1},{2,6},{6,10},{... | collective-permute-start | bytes 196616 | tf_op jit(solution)/shard_map/ppermute | solution.py:17
  97.9 1.0 divide_subtract_fusion
  98.9 3.4 %collective-permute-done.1 = f32[64,256]{1,0:T(8,128)S(1)} collective-permute-done((f32[64,256]{1,0:T(8,128)S(1)}, f32[64,256]{1,0:T(8,128)S(1)}, u32[]{:S(2)}, u32[]{:S(2)}) %collective-permute-start.1) | collective-permute-done | bytes 65568 | tf_op jit(solution)/shard_map/ppermute | solution.py:17
  102.3 0.6 copy.7
  (7 shorter events, 0.1 us)
Async XLA Ops:
  7.2 33.6 %reduce-scatter.3.cloned.1.call-start = ((), (), s32[]{:S(2)}) async-start(), calls=%async_computation.2 | async-start | bytes 327680 | tf_op jit(solution)/shard_map/reduce_scatter | solution.py:42
  14.6 2.5 %copy-start = (f32[768,256]{1,0:T(8,128)S(1)}, f32[768,256]{1,0:T(8,128)}, u32[]{:S(2)}) copy-start(f32[768,256]{1,0:T(8,128)} %param.6) | copy-start | bytes 2359300
  19.3 21.5 %copy-start.1 = (f32[64,256]{1,0:T(8,128)S(1)}, f32[64,256]{1,0:T(8,128)}, u32[]{:S(2)}) copy-start(f32[64,256]{1,0:T(8,128)} %param.7) | copy-start | bytes 196612
  19.3 66.8 %reduce-scatter.5.cloned.1.call-start = ((), (), s32[]{:S(2)}) async-start(), calls=%async_computation.3 | async-start | bytes 327680 | tf_op jit(solution)/shard_map/reduce_scatter | solution.py:42
  50.9 6.1 %collective-permute-start = (f32[64,256]{1,0:T(8,128)S(1)}, f32[64,256]{1,0:T(8,128)S(1)}, u32[]{:S(2)}, u32[]{:S(2)}) collective-permute-start(f32[64,256]{1,0:T(8,128)S(1)} %divide_subtract_fusion.3), channel_id=1, source_target_pairs={{0,4},{4,8},{8,12},{12,0},{1,5},{5,9},{9,13},{13,1},{2,6},{6,10},{... | collective-permute-start | bytes 196616 | tf_op jit(solution)/shard_map/ppermute | solution.py:17
  96.2 6.1 %collective-permute-start.1 = (f32[64,256]{1,0:T(8,128)S(1)}, f32[64,256]{1,0:T(8,128)S(1)}, u32[]{:S(2)}, u32[]{:S(2)}) collective-permute-start(f32[64,256]{1,0:T(8,128)S(1)} %divide_subtract_fusion.2), channel_id=1, source_target_pairs={{0,4},{4,8},{8,12},{12,0},{1,5},{5,9},{9,13},{13,1},{2,6},{6,10},{... | collective-permute-start | bytes 196616 | tf_op jit(solution)/shard_map/ppermute | solution.py:17
Sparse Core Ops, SparseCore 0:
  19.4 21.3 reduce-scatter.2
  67.2 18.8 reduce-scatter.4
where the time goes:
time: 110 us
  waiting for transfers between devices  45.3 us (41%)
  blocking collectives  25.9 us (24%)
  between operations  16.8 us (15%)
  matrix products  11.7 us (11%)
  other arithmetic  5.73 us (5%)
  starting transfers between devices  3.54 us (3%)
    reduce_scatter x2, waiting for transfers between devices, on_device(): lax.psum_scatter(date_part, 'sub', scatter_dimension=0, tiled=True)  37.6 us
    all_gather x2, blocking collectives, on_device(): block = lax.all_gather(share, 'sub', axis=0, tiled=True)  13.2 us
    psum x2, blocking collectives, on_device(): lax.psum((jnp.sum(pixel_grad * pixel_grad), jnp.sum(date_grad * date_grad...  12.7 us
    ppermute x2, waiting for transfers between devices, from_behind(): return lax.ppermute(value, axis, pairs)  7.68 us
    dot_general x2, matrix products, local_terms(): lax.dot_general(strip, block, (((1,), (1,)), ((), ())), precision=hp)  4.68 us
    dot_general x2, matrix products, local_terms(): lax.dot_general(errors, strip, (((0,), (0,)), ((), ())), precision=hp)  4.24 us
    ppermute x2, starting transfers between devices, from_behind(): return lax.ppermute(value, axis, pairs)  3.46 us
    reduce_sum x2, other arithmetic, on_device(): jnp.sum(date_grad * date_grad)  2.92 us
  transfers between devices with their start and end apart: 4, of which 4 were waited for; matrix products, arithmetic and copies ran while one was open for 4% of the time, Pallas kernels for 0%

commit v1 on v0

v1 whole, which is shorter than its diff:
```python
import functools

import jax
import jax.numpy as jnp
from jax import lax
from jax.experimental import pallas as pl
from jax.experimental.pallas import tpu as pltpu
from jax.sharding import PartitionSpec as P

STRATA = 2

step_size = 0.05
ridge = 0.1
epsilon = 1e-06

CORES = 2
F32 = jnp.float32
BF16 = jnp.bfloat16

VMEM = pl.BlockSpec(memory_space=pltpu.VMEM)
SMEM = pl.BlockSpec(memory_space=pltpu.SMEM)

NT = (((1,), (1,)), ((), ()))
NN = (((1,), (0,)), ((), ()))
TN = (((0,), (0,)), ((), ()))


def split(value):
    high = value.astype(BF16)
    low = (value - high.astype(F32)).astype(BF16)
    return high, low


def product(a, b, dims):
    dot = functools.partial(
        lax.dot_general, dimension_numbers=dims, preferred_element_type=F32
    )
    (a_high, a_low), (b_high, b_low) = a, b
    return dot(a_high, b_high) + (dot(a_high, b_low) + dot(a_low, b_high))


def tile_squares(value):
    squares = value * value
    rows, columns = squares.shape
    folded = squares.reshape(rows // 8, 8, columns).sum(0)
    total = folded[:, :128]
    for start in range(128, columns, 128):
        total = total + folded[:, start : start + 128]
    return total


def step_of(tiles, count):
    total = tiles[0]
    for tile in tiles[1:]:
        total = total + tile
    mean = jnp.sum(total, axis=(0, 1), keepdims=True) / count
    return step_size / jnp.sqrt(mean + epsilon)


def call(kernel, outs, *args, scalars=0, flops=0):
    specs = [SMEM] * scalars + [VMEM] * (len(args) - scalars)
    size = sum(a.size * a.dtype.itemsize for a in list(args) + list(outs))
    return pl.pallas_call(
        kernel,
        out_shape=outs,
        in_specs=specs,
        out_specs=[VMEM] * len(outs),
        compiler_params=pltpu.CompilerParams(vmem_limit_bytes=16 << 20),
        cost_estimate=pl.CostEstimate(
            flops=flops, bytes_accessed=size, transcendentals=0
        ),
    )(*args)


def shape(rows, columns, dtype=F32):
    return jax.ShapeDtypeStruct((rows, columns), dtype)


def errors_and_part(place, nx, relative, values, weights, strip, block, outs):
    send_ref, keep_ref, high_ref, low_ref, part_ref = outs
    predicted = product(strip, block, NT)
    errors = weights * (values - predicted)
    errors = split(errors)
    high_ref[...], low_ref[...] = errors
    part_ref[...] = -product(errors, strip, TN)
    share = part_ref.shape[0] // (CORES * nx)
    chip, core = place
    for dx in range(nx):
        target = lax.rem(chip + dx, nx) if relative else dx
        rows = pl.ds(dx * share, share)
        for ref, owner in ((keep_ref, core), (send_ref, 1 - core)):
            start = pl.multiple_of((target * CORES + owner) * share, share)
            ref[rows, :] = part_ref[pl.ds(start, share), :]


def first_kernel(n, order, place_ref, *refs):
    shares, refs = refs[:n], refs[n:]
    values_ref, weights_ref, strip_ref = refs[:3]
    block_ref, part_ref = refs[-2], refs[-1]
    nx = n // CORES
    chip, core = place_ref[0], place_ref[1]
    share = shares[0].shape[0]
    for (dx, dc), ref in zip(order, shares):
        source = lax.rem(chip - dx + nx, nx) * CORES + lax.rem(core + dc, CORES)
        block_ref[pl.ds(pl.multiple_of(source * share, share), share), :] = ref[...]
    errors_and_part(
        (chip, core), nx, False, values_ref[...], weights_ref[...].astype(F32),
        split(strip_ref[...]), split(block_ref[...]), refs[3:7] + (part_ref,),
    )


def later_kernel(n, count, place_ref, *refs):
    own_ref, other_ref, own_block_ref, other_block_ref = refs[:4]
    values_ref, weights_ref, high_ref, low_ref = refs[4:8]
    block_ref, part_ref = refs[-2], refs[-1]
    nx = n // CORES
    chip, core = place_ref[0], place_ref[1]
    share = own_ref.shape[0] // nx
    step = step_of([tile_squares(own_ref[...]), tile_squares(other_ref[...])], count)
    for grad, block, owner in (
        (own_ref, own_block_ref, core), (other_ref, other_block_ref, 1 - core),
    ):
        updated = block[...] - step * grad[...]
        for at in range(nx):
            start = pl.multiple_of((at * CORES + owner) * share, share)
            block_ref[pl.ds(start, share), :] = updated[at * share : (at + 1) * share]
    own = pl.multiple_of((chip * CORES + core) * share, share)
    refs[12][...] = block_ref[pl.ds(own, share), :]
    errors_and_part(
        (chip, core), nx, True, values_ref[...], weights_ref[...].astype(F32),
        (high_ref[...], low_ref[...]), split(block_ref[...]), refs[8:12] + (part_ref,),
    )


def pixel_grad_kernel(high_ref, low_ref, block_ref, strip_ref, grad_ref, tile_ref):
    block = split(block_ref[...])
    grad = ridge * strip_ref[...] - product((high_ref[...], low_ref[...]), block, NN)
    grad_ref[...] = grad
    tile_ref[...] = tile_squares(grad)


def pixel_step_kernel(count, n, strip_ref, grad_ref, *refs):
    tiles, outs = refs[:n], refs[n:]
    strip = strip_ref[...] - step_of([t[...] for t in tiles], count) * grad_ref[...]
    outs[0][...] = strip
    if len(outs) > 1:
        outs[1][...], outs[2][...] = split(strip)


def gather_half_kernel(nx, place_ref, *refs):
    shares, out_ref = refs[:nx], refs[nx]
    share = shares[0].shape[0]
    for dx, ref in enumerate(shares):
        source = lax.rem(place_ref[0] - dx + nx, nx)
        out_ref[pl.ds(pl.multiple_of(source * share, share), share), :] = ref[...]


def last_grad_kernel(nx, block_ref, *refs):
    grad = ridge * block_ref[...]
    for ref in refs[:nx]:
        grad = grad + ref[...]
    refs[nx][...] = grad
    refs[nx + 1][...] = tile_squares(grad)


def on_device(readings, coverage, pixel_factors, date_factors):
    strip = pixel_factors
    pixels, rank = strip.shape
    share = date_factors.shape[0]
    n = lax.axis_size("sub")
    blocks = lax.axis_size("blk")
    nx = n // CORES
    dates = share * n
    half = share * nx
    pixel_count = pixels * n * rank
    date_count = dates * rank
    at = lax.axis_index("sub")
    place = jnp.stack([at // CORES, at % CORES]).astype(jnp.int32)
    order = [(dx, dc) for dx in range(nx) for dc in range(CORES)]

    def moved(a, dx, dc):
        return (a // CORES + dx) % nx * CORES + (a % CORES + dc) % CORES

    def within(value, dx, dc):
        return lax.ppermute(value, "sub", [(a, moved(a, dx, dc)) for a in range(n)])

    def onward(value, dx):
        pairs = [
            (b * n + a, (b + 1) % blocks * n + moved(a, dx, 0))
            for b in range(blocks) for a in range(n)
        ]
        return lax.ppermute(value, ("blk", "sub"), pairs)

    def everywhere(tile):
        return [tile] + [within(tile, *step) for step in order[1:]]

    work = 2 * pixels * dates * rank

    shares = [date_factors] + [within(date_factors, *step) for step in order[1:]]
    old = [onward(date_factors, dx) for dx in range(nx)]
    send, keep, high, low, block = call(
        functools.partial(first_kernel_out, n, order),
        [shape(half, rank), shape(half, rank), shape(pixels, dates, BF16),
         shape(pixels, dates, BF16), shape(dates, rank), shape(dates, rank)],
        place, *shares, readings[0], coverage[0], strip, scalars=1, flops=6 * work,
    )[:5]
    mine = keep + within(send, 0, 1)
    came = [onward(mine, dx) for dx in range(nx)]
    grad, tile = call(
        pixel_grad_kernel, [shape(pixels, rank), shape(8, 128)],
        high, low, block, strip, flops=3 * work,
    )
    strip, strip_high, strip_low = call(
        functools.partial(pixel_step_kernel, pixel_count, n),
        [shape(pixels, rank), shape(pixels, rank, BF16), shape(pixels, rank, BF16)],
        strip, grad, *everywhere(tile),
    )
    old_half, = call(
        functools.partial(gather_half_kernel, nx), [shape(half, rank)],
        place, *old, scalars=1,
    )
    old_other = within(old_half, 0, 1)
    date_half = sum(came[1:], came[0]) + ridge * old_half
    date_other = within(date_half, 0, 1)

    send, keep, high, low, own, block = call(
        functools.partial(later_kernel_out, n, date_count),
        [shape(half, rank), shape(half, rank), shape(pixels, dates, BF16),
         shape(pixels, dates, BF16), shape(share, rank), shape(dates, rank),
         shape(dates, rank)],
        place, date_half, date_other, old_half, old_other, readings[1], coverage[1],
        strip_high, strip_low, scalars=1, flops=6 * work,
    )[:6]
    got = within(send, 0, 1)
    came = [
        onward(keep[dx * share : (dx + 1) * share] + got[dx * share : (dx + 1) * share], dx)
        for dx in range(nx)
    ]
    old = onward(own, 0)
    grad, tile = call(
        pixel_grad_kernel, [shape(pixels, rank), shape(8, 128)],
        high, low, block, strip, flops=3 * work,
    )
    strip, = call(
        functools.partial(pixel_step_kernel, pixel_count, n), [shape(pixels, rank)],
        strip, grad, *everywhere(tile),
    )
    date_grad, tile = call(
        functools.partial(last_grad_kernel, nx), [shape(share, rank), shape(8, 128)],
        old, *came,
    )
    share_out, = call(
        functools.partial(pixel_step_kernel, date_count, n), [shape(share, rank)],
        old, date_grad, *everywhere(tile),
    )
    return strip, share_out


def first_kernel_out(n, order, *refs):
    first_kernel(n, order, *refs)


def later_kernel_out(n, count, *refs):
    later_kernel(n, count, *refs)


def solution(mesh):
    spec = P(("parts", "blk", "sub"), None)
    stacked = P(None, ("parts", "blk", "sub"), None)
    return jax.shard_map(
        on_device, mesh=mesh, in_specs=(stacked, stacked, spec, spec),
        out_specs=(spec, spec), check_vma=False,
    )
```

time: 110 us -> 50.8 us (0.46)
  waiting for transfers between devices: 45.3 us -> 18.9 us
  blocking collectives: 25.9 us -> 0 us
  between operations: 16.8 us -> 0.76 us
  starting transfers between devices: 3.54 us -> 17.3 us
  matrix products: 11.7 us -> 0 us
  Pallas kernels: 0 us -> 9.54 us
  other arithmetic: 5.73 us -> 0.14 us
  local copies, waits for them, and re-layouts: 0.64 us -> 3.99 us
    reduce_scatter x2 -> x0, waiting for transfers between devices: 37.6 us -> none  [on_device(): lax.psum_scatter(date_part, 'sub', scatter_dimension=0, tiled=True)]
    ppermute x2 -> x23, starting transfers between devices: 3.46 us -> 17.3 us  [the longest x16 8.98 us: within(): return lax.ppermute(value, 'sub', [(a, moved(a, dx, dc)) for a in range(n)])]
    all_gather x2 -> x0, blocking collectives: 13.2 us -> none  [on_device(): block = lax.all_gather(share, 'sub', axis=0, tiled=True)]
    psum x2 -> x0, blocking collectives: 12.7 us -> none  [on_device(): lax.psum((jnp.sum(pixel_grad * pixel_grad), jnp.sum(date_grad * date_grad...]
    dot_general x6 -> x0, matrix products: 11.7 us -> none  [the longest x2 4.68 us: local_terms(): lax.dot_general(strip, block, (((1,), (1,)), ((), ())), precision=hp)]
    ppermute x2 -> x23, waiting for transfers between devices: 7.68 us -> 18.9 us  [the longest x7 12.1 us: onward(): return lax.ppermute(value, ('blk', 'sub'), pairs)]
    pallas_call x0 -> x9, Pallas kernels: none -> 9.54 us  [call(): pl.pallas_call(kernel, out_shape=outs, in_specs=specs, out_specs=[VMEM] *...]
    reduce_sum x2 -> x0, other arithmetic: 2.92 us -> none  [on_device(): jnp.sum(date_grad * date_grad)]
  transfers between devices with their start and end apart: 4 -> 23, of which waited for: 4 -> 11; matrix products, arithmetic and copies ran while one was open for 4% -> 5% of each run, Pallas kernels for 0% -> 6%
where the time goes in v1:
time: 50.8 us; the launch traced here: 50.6 us
  waiting for transfers between devices  18.9 us (37%)
  starting transfers between devices  17.3 us (34%)
  Pallas kernels  9.54 us (19%)
  local copies, waits for them, and re-layouts  3.99 us (8%)
  between operations  0.76 us (1%)
    ppermute x7, waiting for transfers between devices, onward(): return lax.ppermute(value, ('blk', 'sub'), pairs)  12.1 us
    pallas_call x9, Pallas kernels, call(): pl.pallas_call(kernel, out_shape=outs, in_specs=specs, out_specs=[VMEM] *...  9.54 us
    ppermute x16, starting transfers between devices, within(): return lax.ppermute(value, 'sub', [(a, moved(a, dx, dc)) for a in range(n)])  8.98 us
    ppermute x7, starting transfers between devices, onward(): return lax.ppermute(value, ('blk', 'sub'), pairs)  8.31 us
    ppermute x16, waiting for transfers between devices, within(): return lax.ppermute(value, 'sub', [(a, moved(a, dx, dc)) for a in range(n)])  6.8 us
    squeeze x1, local copies, waits for them, and re-layouts, on_device(): readings[1]  1.59 us
    unnamed x8, local copies, waits for them, and re-layouts  1.42 us
  transfers between devices with their start and end apart: 23, of which 11 were waited for; matrix products, arithmetic and copies ran while one was open for 5% of the time, Pallas kernels for 6%

profile of v1, /device:TPU:0, one launch (start us, length us, event | category | flops | bytes accessed | tf_op | source)
XLA Modules:
  0.0 50.6 jit_solution(3766645361616943582)
XLA Ops:
  0.6 2.5 %collective-permute-start.2 = (f32[64,256]{1,0:T(8,128)}, f32[64,256]{1,0:T(8,128)S(1)}, u32[]{:S(2)}, u32[]{:S(2)}) collective-permute-start(f32[64,256]{1,0:T(8,128)} %refs_1_.1), channel_id=1, source_target_pairs={{0,3},{1,2},{2,1},{3,0},{4,7},{5,6},{6,5},{7,4},{8,11},{9,10},{10,... | collective-permute-start | bytes 196616 | tf_op jit(solution)/shard_map/ppermute | solution.py:185
  3.8 1.6 %slice_bitcast_fusion.1 = (f32[768,256]{1,0:T(8,128)S(1)}, f32[768,256]{1,0:T(8,128)S(1)}) fusion(f32[2,768,256]{2,1,0:T(8,128)} %param.4), kind=kLoop, calls=%fused_computation.1 | loop fusion | bytes 3145728 | tf_op jit(solution)/shard_map/squeeze | solution.py:231
  5.7 1.0 %slice_bitcast_fusion = (s32[768,256]{1,0:T(8,128)S(1)}, s32[768,256]{1,0:T(8,128)}) fusion(s32[2,768,256]{2,1,0:T(8,128)S(1)} %copy-done.3), kind=kLoop, calls=%fused_computation | loop fusion | bytes 3145728 | tf_op jit(solution)/shard_map/squeeze | solution.py:231
  6.7 1.3 %collective-permute-done.1.refs_3_ = f32[64,256]{1,0:T(8,128)S(1)} collective-permute-done((f32[64,256]{1,0:T(8,128)}, f32[64,256]{1,0:T(8,128)S(1)}, u32[]{:S(2)}, u32[]{:S(2)}) %collective-permute-start.1) | collective-permute-done | bytes 65568 | tf_op jit(solution)/shard_map/ppermute | solution.py:185
  8.0 1.1 %copy-done.1 = s32[768,256]{1,0:T(8,128)S(1)} copy-done((s32[768,256]{1,0:T(8,128)S(1)}, s32[768,256]{1,0:T(8,128)}, u32[]{:S(2)}) %copy-start.1) | copy-done | bytes 786456
  9.1 2.7 %shard_map.59 = (f32[128,256]{1,0:T(8,128)S(1)}, f32[128,256]{1,0:T(8,128)S(1)}, bf16[768,256]{1,0:T(8,128)(2,1)S(1)}, bf16[768,256]{1,0:T(8,128)(2,1)S(1)}, f32[256,256]{1,0:T(8,128)S(1)}, /*index=5*/f32[256,256]{1,0:T(8,128)}) custom-call(s32[2]{0:T(128)S(1)} %pad_add_fusion.refs_0_.place_ref, f32[64,256]{1,0:T(8,128)S(1)} %copy-done.2, ...), custom_call_target="tpu_custom_call" | custom-call | flops 603979776 | bytes 4194312 | tf_op jit(solution)/shard_map/pallas_call | solution.py:63
  11.9 1.3 %collective-permute-done.6 = f32[128,256]{1,0:T(8,128)S(1)} collective-permute-done((f32[128,256]{1,0:T(8,128)S(1)}, f32[128,256]{1,0:T(8,128)S(1)}, u32[]{:S(2)}, u32[]{:S(2)}) %collective-permute-start.6) | collective-permute-done | bytes 131104 | tf_op jit(solution)/shard_map/ppermute | solution.py:185
  13.2 2.7 %collective-permute-start.8 = (f32[128,256]{1,0:T(8,128)S(1)}, f32[128,256]{1,0:T(8,128)S(1)}, u32[]{:S(2)}, u32[]{:S(2)}) collective-permute-start(f32[128,256]{1,0:T(8,128)S(1)} %add.21), channel_id=1, source_target_pairs={{0,6},{1,7},{2,4},{3,5},{4,10},{5,11},{6,8},{7,9},{8,14},{9,15},{1... | collective-permute-start | bytes 393224 | tf_op jit(solution)/shard_map/ppermute | solution.py:192
  16.0 1.6 %collective-permute-start.7 = (f32[128,256]{1,0:T(8,128)S(1)}, f32[128,256]{1,0:T(8,128)S(1)}, u32[]{:S(2)}, u32[]{:S(2)}) collective-permute-start(f32[128,256]{1,0:T(8,128)S(1)} %add.21), channel_id=1, source_target_pairs={{0,4},{1,5},{2,6},{3,7},{4,8},{5,9},{6,10},{7,11},{8,12},{9,13},{1... | collective-permute-start | bytes 393224 | tf_op jit(solution)/shard_map/ppermute | solution.py:192
  17.5 1.5 %collective-permute-start.10 = (f32[64,256]{1,0:T(8,128)S(1)}, f32[64,256]{1,0:T(8,128)S(1)}, u32[]{:S(2)}, u32[]{:S(2)}) collective-permute-start(f32[64,256]{1,0:T(8,128)S(1)} %copy-done.2), channel_id=1, source_target_pairs={{0,6},{1,7},{2,4},{3,5},{4,10},{5,11},{6,8},{7,9},{8,14},{9,15},{1... | collective-permute-start | bytes 196616 | tf_op jit(solution)/shard_map/ppermute | solution.py:192
  19.2 7.4 %collective-permute-done.10.refs_1_ = f32[64,256]{1,0:T(8,128)S(1)} collective-permute-done((f32[64,256]{1,0:T(8,128)S(1)}, f32[64,256]{1,0:T(8,128)S(1)}, u32[]{:S(2)}, u32[]{:S(2)}) %collective-permute-start.10) | collective-permute-done | bytes 65568 | tf_op jit(solution)/shard_map/ppermute | solution.py:192
  26.6 0.8 %collective-permute-done.9.refs_0_ = f32[64,256]{1,0:T(8,128)S(1)} collective-permute-done((f32[64,256]{1,0:T(8,128)S(1)}, f32[64,256]{1,0:T(8,128)S(1)}, u32[]{:S(2)}, u32[]{:S(2)}) %collective-permute-start.9) | collective-permute-done | bytes 65568 | tf_op jit(solution)/shard_map/ppermute | solution.py:192
  29.6 1.3 %collective-permute-start.4 = (f32[8,128]{1,0:T(8,128)S(1)}, f32[8,128]{1,0:T(8,128)S(1)}, u32[]{:S(2)}, u32[]{:S(2)}) collective-permute-start(f32[8,128]{1,0:T(8,128)S(1)} %get-tuple-element.26.refs_0_), channel_id=1, source_target_pairs={{0,2},{1,3},{2,0},{3,1},{4,6},{5,7},{6,4},{7,5},{8,10},{9,11},{10,... | collective-permute-start | bytes 12296 | tf_op jit(solution)/shard_map/ppermute | solution.py:185
  31.0 1.2 %collective-permute-done.5.refs_3_ = f32[8,128]{1,0:T(8,128)S(1)} collective-permute-done((f32[8,128]{1,0:T(8,128)S(1)}, f32[8,128]{1,0:T(8,128)S(1)}, u32[]{:S(2)}, u32[]{:S(2)}) %collective-permute-start.5) | collective-permute-done | bytes 4128 | tf_op jit(solution)/shard_map/ppermute | solution.py:185
  32.2 1.0 %collective-permute-done.4.refs_2_ = f32[8,128]{1,0:T(8,128)S(1)} collective-permute-done((f32[8,128]{1,0:T(8,128)S(1)}, f32[8,128]{1,0:T(8,128)S(1)}, u32[]{:S(2)}, u32[]{:S(2)}) %collective-permute-start.4) | collective-permute-done | bytes 4128 | tf_op jit(solution)/shard_map/ppermute | solution.py:185
  33.7 2.9 %shard_map.63 = (f32[128,256]{1,0:T(8,128)S(1)}, f32[128,256]{1,0:T(8,128)S(1)}, bf16[768,256]{1,0:T(8,128)(2,1)S(1)}, bf16[768,256]{1,0:T(8,128)(2,1)S(1)}, f32...) custom-call(s32[2]{0:T(128)S(1)} %pad_add_fusion.refs_0_.place_ref, ...), custom_call_target="tpu_custom_call" | custom-call | flops 603979776 | bytes 4521992 | tf_op jit(solution)/shard_map/pallas_call | solution.py:63
  36.6 1.3 %collective-permute-done.17 = f32[128,256]{1,0:T(8,128)S(1)} collective-permute-done((f32[128,256]{1,0:T(8,128)S(1)}, f32[128,256]{1,0:T(8,128)S(1)}, u32[]{:S(2)}, u32[]{:S(2)}) %collective-permute-start.17) | collective-permute-done | bytes 131104 | tf_op jit(solution)/shard_map/ppermute | solution.py:185
  38.7 1.6 %collective-permute-start.18 = (f32[64,256]{1,0:T(8,128)S(1)}, f32[64,256]{1,0:T(8,128)S(1)}, u32[]{:S(2)}, u32[]{:S(2)}) collective-permute-start(f32[64,256]{1,0:T(8,128)S(1)} %get-tuple-element.47), channel_id=1, source_target_pairs={{0,4},{1,5},{2,6},{3,7},{4,8},{5,9},{6,10},{7,11},{8,12},{9,13},{1... | collective-permute-start | bytes 196616 | tf_op jit(solution)/shard_map/ppermute | solution.py:192
  40.9 1.3 %collective-permute-start.14 = (f32[8,128]{1,0:T(8,128)S(1)}, f32[8,128]{1,0:T(8,128)S(1)}, u32[]{:S(2)}, u32[]{:S(2)}) collective-permute-start(f32[8,128]{1,0:T(8,128)S(1)} %get-tuple-element.36.refs_0_), channel_id=1, source_target_pairs={{0,2},{1,3},{2,0},{3,1},{4,6},{5,7},{6,4},{7,5},{8,10},{9,11},{10,... | collective-permute-start | bytes 12296 | tf_op jit(solution)/shard_map/ppermute | solution.py:185
  42.9 2.8 %collective-permute-done.19.refs_1_ = f32[64,256]{1,0:T(8,128)S(1)} collective-permute-done((f32[64,256]{1,0:T(8,128)S(1)}, f32[64,256]{1,0:T(8,128)S(1)}, u32[]{:S(2)}, u32[]{:S(2)}) %collective-permute-start.19) | collective-permute-done | bytes 65568 | tf_op jit(solution)/shard_map/ppermute | solution.py:192
  46.1 1.0 %collective-permute-start.21 = (f32[8,128]{1,0:T(8,128)S(1)}, f32[8,128]{1,0:T(8,128)S(1)}, u32[]{:S(2)}, u32[]{:S(2)}) collective-permute-start(f32[8,128]{1,0:T(8,128)S(1)} %get-tuple-element.41.refs_0_), channel_id=1, source_target_pairs={{0,2},{1,3},{2,0},{3,1},{4,6},{5,7},{6,4},{7,5},{8,10},{9,11},{10,... | collective-permute-start | bytes 12296 | tf_op jit(solution)/shard_map/ppermute | solution.py:185
  47.1 0.9 %collective-permute-start.20 = (f32[8,128]{1,0:T(8,128)S(1)}, f32[8,128]{1,0:T(8,128)S(1)}, u32[]{:S(2)}, u32[]{:S(2)}) collective-permute-start(f32[8,128]{1,0:T(8,128)S(1)} %get-tuple-element.41.refs_0_), channel_id=1, source_target_pairs={{0,1},{1,0},{2,3},{3,2},{4,5},{5,4},{6,7},{7,6},{8,9},{9,8},{10,11... | collective-permute-start | bytes 12296 | tf_op jit(solution)/shard_map/ppermute | solution.py:185
  48.0 1.2 %shard_map.65 = f32[768,256]{1,0:T(8,128)} custom-call(f32[768,256]{1,0:T(8,128)S(1)} %get-tuple-element.27.strip_ref, f32[768,256]{1,0:T(8,128)S(1)} %get-tuple-element.35.grad_ref, f32[8,128]{1,0:T(8,128)S(1)} %get-tuple-element.36.refs_0_, f32[8,128]{1,0:T(8,128)S(1)} %collective-permute-done.13.refs_1_, f32[8,128]{1,0:T(8,128)S(1)} %collective-permute-done.14.refs_2_, ...), custom_call_target="tpu_custom_call" | custom-call | bytes 2375680 | tf_op jit(solution)/shard_map/pallas_call | solution.py:63
  49.8 0.8 %shard_map.67 = f32[64,256]{1,0:T(8,128)} custom-call(f32[64,256]{1,0:T(8,128)S(1)} %collective-permute-done.16.block_ref.strip_ref, f32[64,256]{1,0:T(8,128)S(1)} %get-tuple-element.40.grad_ref, f32[8,128]{1,0:T(8,128)S(1)} %get-tuple-element.41.refs_0_, f32[8,128]{1,0:T(8,128)S(1)} %collective-permute-done.20.refs_1_, ...), custom_call_target="tpu_custom_call" | custom-call | bytes 212992 | tf_op jit(solution)/shard_map/pallas_call | solution.py:63
  (45 shorter events, 7.3 us)
Async XLA Ops:
  0.6 6.1 %collective-permute-start.2 = (f32[64,256]{1,0:T(8,128)}, f32[64,256]{1,0:T(8,128)S(1)}, u32[]{:S(2)}, u32[]{:S(2)}) collective-permute-start(f32[64,256]{1,0:T(8,128)} %refs_1_.1), channel_id=1, source_target_pairs={{0,3},{1,2},{2,1},{3,0},{4,7},{5,6},{6,5},{7,4},{8,11},{9,10},{10,... | collective-permute-start | bytes 196616 | tf_op jit(solution)/shard_map/ppermute | solution.py:185
  3.1 4.9 %collective-permute-start.1 = (f32[64,256]{1,0:T(8,128)}, f32[64,256]{1,0:T(8,128)S(1)}, u32[]{:S(2)}, u32[]{:S(2)}) collective-permute-start(f32[64,256]{1,0:T(8,128)} %refs_1_.1), channel_id=1, source_target_pairs={{0,2},{1,3},{2,0},{3,1},{4,6},{5,7},{6,4},{7,5},{8,10},{9,11},{10,... | collective-permute-start | bytes 196616 | tf_op jit(solution)/shard_map/ppermute | solution.py:185
  3.7 4.2 %collective-permute-start = (f32[64,256]{1,0:T(8,128)}, f32[64,256]{1,0:T(8,128)S(1)}, u32[]{:S(2)}, u32[]{:S(2)}) collective-permute-start(f32[64,256]{1,0:T(8,128)} %refs_1_.1), channel_id=1, source_target_pairs={{0,1},{1,0},{2,3},{3,2},{4,5},{5,4},{6,7},{7,6},{8,9},{9,8},{10,11... | collective-permute-start | bytes 196616 | tf_op jit(solution)/shard_map/ppermute | solution.py:185
  5.7 2.3 %copy-start.2 = (f32[64,256]{1,0:T(8,128)S(1)}, f32[64,256]{1,0:T(8,128)}, u32[]{:S(2)}) copy-start(f32[64,256]{1,0:T(8,128)} %refs_1_.1) | copy-start | bytes 196612
  11.9 1.3 %collective-permute-start.6 = (f32[128,256]{1,0:T(8,128)S(1)}, f32[128,256]{1,0:T(8,128)S(1)}, u32[]{:S(2)}, u32[]{:S(2)}) collective-permute-start(f32[128,256]{1,0:T(8,128)S(1)} %get-tuple-element.29), channel_id=1, source_target_pairs={{0,1},{1,0},{2,3},{3,2},{4,5},{5,4},{6,7},{7,6},{8,9},{9,8},{10,11... | collective-permute-start | bytes 393224 | tf_op jit(solution)/shard_map/ppermute | solution.py:185
  13.2 14.8 %collective-permute-start.8 = (f32[128,256]{1,0:T(8,128)S(1)}, f32[128,256]{1,0:T(8,128)S(1)}, u32[]{:S(2)}, u32[]{:S(2)}) collective-permute-start(f32[128,256]{1,0:T(8,128)S(1)} %add.21), channel_id=1, source_target_pairs={{0,6},{1,7},{2,4},{3,5},{4,10},{5,11},{6,8},{7,9},{8,14},{9,15},{1... | collective-permute-start | bytes 393224 | tf_op jit(solution)/shard_map/ppermute | solution.py:192
  16.0 12.0 %collective-permute-start.7 = (f32[128,256]{1,0:T(8,128)S(1)}, f32[128,256]{1,0:T(8,128)S(1)}, u32[]{:S(2)}, u32[]{:S(2)}) collective-permute-start(f32[128,256]{1,0:T(8,128)S(1)} %add.21), channel_id=1, source_target_pairs={{0,4},{1,5},{2,6},{3,7},{4,8},{5,9},{6,10},{7,11},{8,12},{9,13},{1... | collective-permute-start | bytes 393224 | tf_op jit(solution)/shard_map/ppermute | solution.py:192
  17.5 9.0 %collective-permute-start.10 = (f32[64,256]{1,0:T(8,128)S(1)}, f32[64,256]{1,0:T(8,128)S(1)}, u32[]{:S(2)}, u32[]{:S(2)}) collective-permute-start(f32[64,256]{1,0:T(8,128)S(1)} %copy-done.2), channel_id=1, source_target_pairs={{0,6},{1,7},{2,4},{3,5},{4,10},{5,11},{6,8},{7,9},{8,14},{9,15},{1... | collective-permute-start | bytes 196616 | tf_op jit(solution)/shard_map/ppermute | solution.py:192
  19.1 8.3 %collective-permute-start.9 = (f32[64,256]{1,0:T(8,128)S(1)}, f32[64,256]{1,0:T(8,128)S(1)}, u32[]{:S(2)}, u32[]{:S(2)}) collective-permute-start(f32[64,256]{1,0:T(8,128)S(1)} %copy-done.2), channel_id=1, source_target_pairs={{0,4},{1,5},{2,6},{3,7},{4,8},{5,9},{6,10},{7,11},{8,12},{9,13},{1... | collective-permute-start | bytes 196616 | tf_op jit(solution)/shard_map/ppermute | solution.py:192
  27.9 5.7 %collective-permute-start.12 = (f32[128,256]{1,0:T(8,128)S(1)}, f32[128,256]{1,0:T(8,128)S(1)}, u32[]{:S(2)}, u32[]{:S(2)}) collective-permute-start(f32[128,256]{1,0:T(8,128)S(1)} %shard_map.62.refs_3_), channel_id=1, source_target_pairs={{0,1},{1,0},{2,3},{3,2},{4,5},{5,4},{6,7},{7,6},{8,9},{9,8},{10,11... | collective-permute-start | bytes 393224 | tf_op jit(solution)/shard_map/ppermute | solution.py:185
  28.1 5.6 %collective-permute-start.11 = (f32[128,256]{1,0:T(8,128)S(1)}, f32[128,256]{1,0:T(8,128)S(1)}, u32[]{:S(2)}, u32[]{:S(2)}) collective-permute-start(f32[128,256]{1,0:T(8,128)S(1)} %multiply_add_fusion.refs_1_), channel_id=1, source_target_pairs={{0,1},{1,0},{2,3},{3,2},{4,5},{5,4},{6,7},{7,6},{8,9},{9,8},{10,11... | collective-permute-start | bytes 393224 | tf_op jit(solution)/shard_map/ppermute | solution.py:185
  29.1 3.1 %collective-permute-start.5 = (f32[8,128]{1,0:T(8,128)S(1)}, f32[8,128]{1,0:T(8,128)S(1)}, u32[]{:S(2)}, u32[]{:S(2)}) collective-permute-start(f32[8,128]{1,0:T(8,128)S(1)} %get-tuple-element.26.refs_0_), channel_id=1, source_target_pairs={{0,3},{1,2},{2,1},{3,0},{4,7},{5,6},{6,5},{7,4},{8,11},{9,10},{10,... | collective-permute-start | bytes 12296 | tf_op jit(solution)/shard_map/ppermute | solution.py:185
  29.6 3.6 %collective-permute-start.4 = (f32[8,128]{1,0:T(8,128)S(1)}, f32[8,128]{1,0:T(8,128)S(1)}, u32[]{:S(2)}, u32[]{:S(2)}) collective-permute-start(f32[8,128]{1,0:T(8,128)S(1)} %get-tuple-element.26.refs_0_), channel_id=1, source_target_pairs={{0,2},{1,3},{2,0},{3,1},{4,6},{5,7},{6,4},{7,5},{8,10},{9,11},{10,... | collective-permute-start | bytes 12296 | tf_op jit(solution)/shard_map/ppermute | solution.py:185
  30.8 2.3 %collective-permute-start.3 = (f32[8,128]{1,0:T(8,128)S(1)}, f32[8,128]{1,0:T(8,128)S(1)}, u32[]{:S(2)}, u32[]{:S(2)}) collective-permute-start(f32[8,128]{1,0:T(8,128)S(1)} %get-tuple-element.26.refs_0_), channel_id=1, source_target_pairs={{0,1},{1,0},{2,3},{3,2},{4,5},{5,4},{6,7},{7,6},{8,9},{9,8},{10,11... | collective-permute-start | bytes 12296 | tf_op jit(solution)/shard_map/ppermute | solution.py:185
  36.6 1.3 %collective-permute-start.17 = (f32[128,256]{1,0:T(8,128)S(1)}, f32[128,256]{1,0:T(8,128)S(1)}, u32[]{:S(2)}, u32[]{:S(2)}) collective-permute-start(f32[128,256]{1,0:T(8,128)S(1)} %get-tuple-element.39), channel_id=1, source_target_pairs={{0,1},{1,0},{2,3},{3,2},{4,5},{5,4},{6,7},{7,6},{8,9},{9,8},{10,11... | collective-permute-start | bytes 393224 | tf_op jit(solution)/shard_map/ppermute | solution.py:185
  36.6 6.3 %collective-permute-start.16 = (f32[64,256]{1,0:T(8,128)S(1)}, f32[64,256]{1,0:T(8,128)S(1)}, u32[]{:S(2)}, u32[]{:S(2)}) collective-permute-start(f32[64,256]{1,0:T(8,128)S(1)} %get-tuple-element.37), channel_id=1, source_target_pairs={{0,4},{1,5},{2,6},{3,7},{4,8},{5,9},{6,10},{7,11},{8,12},{9,13},{1... | collective-permute-start | bytes 196616 | tf_op jit(solution)/shard_map/ppermute | solution.py:192
  37.9 7.7 %collective-permute-start.19 = (f32[64,256]{1,0:T(8,128)S(1)}, f32[64,256]{1,0:T(8,128)S(1)}, u32[]{:S(2)}, u32[]{:S(2)}) collective-permute-start(f32[64,256]{1,0:T(8,128)S(1)} %get-tuple-element.46), channel_id=1, source_target_pairs={{0,6},{1,7},{2,4},{3,5},{4,10},{5,11},{6,8},{7,9},{8,14},{9,15},{1... | collective-permute-start | bytes 196616 | tf_op jit(solution)/shard_map/ppermute | solution.py:192
  38.7 7.3 %collective-permute-start.18 = (f32[64,256]{1,0:T(8,128)S(1)}, f32[64,256]{1,0:T(8,128)S(1)}, u32[]{:S(2)}, u32[]{:S(2)}) collective-permute-start(f32[64,256]{1,0:T(8,128)S(1)} %get-tuple-element.47), channel_id=1, source_target_pairs={{0,4},{1,5},{2,6},{3,7},{4,8},{5,9},{6,10},{7,11},{8,12},{9,13},{1... | collective-permute-start | bytes 196616 | tf_op jit(solution)/shard_map/ppermute | solution.py:192
  40.8 6.3 %collective-permute-start.15 = (f32[8,128]{1,0:T(8,128)S(1)}, f32[8,128]{1,0:T(8,128)S(1)}, u32[]{:S(2)}, u32[]{:S(2)}) collective-permute-start(f32[8,128]{1,0:T(8,128)S(1)} %get-tuple-element.36.refs_0_), channel_id=1, source_target_pairs={{0,3},{1,2},{2,1},{3,0},{4,7},{5,6},{6,5},{7,4},{8,11},{9,10},{10,... | collective-permute-start | bytes 12296 | tf_op jit(solution)/shard_map/ppermute | solution.py:185
  40.9 7.1 %collective-permute-start.14 = (f32[8,128]{1,0:T(8,128)S(1)}, f32[8,128]{1,0:T(8,128)S(1)}, u32[]{:S(2)}, u32[]{:S(2)}) collective-permute-start(f32[8,128]{1,0:T(8,128)S(1)} %get-tuple-element.36.refs_0_), channel_id=1, source_target_pairs={{0,2},{1,3},{2,0},{3,1},{4,6},{5,7},{6,4},{7,5},{8,10},{9,11},{10,... | collective-permute-start | bytes 12296 | tf_op jit(solution)/shard_map/ppermute | solution.py:185
  42.9 5.1 %collective-permute-start.13 = (f32[8,128]{1,0:T(8,128)S(1)}, f32[8,128]{1,0:T(8,128)S(1)}, u32[]{:S(2)}, u32[]{:S(2)}) collective-permute-start(f32[8,128]{1,0:T(8,128)S(1)} %get-tuple-element.36.refs_0_), channel_id=1, source_target_pairs={{0,1},{1,0},{2,3},{3,2},{4,5},{5,4},{6,7},{7,6},{8,9},{9,8},{10,11... | collective-permute-start | bytes 12296 | tf_op jit(solution)/shard_map/ppermute | solution.py:185
  46.0 3.1 %collective-permute-start.22 = (f32[8,128]{1,0:T(8,128)S(1)}, f32[8,128]{1,0:T(8,128)S(1)}, u32[]{:S(2)}, u32[]{:S(2)}) collective-permute-start(f32[8,128]{1,0:T(8,128)S(1)} %get-tuple-element.41.refs_0_), channel_id=1, source_target_pairs={{0,3},{1,2},{2,1},{3,0},{4,7},{5,6},{6,5},{7,4},{8,11},{9,10},{10,... | collective-permute-start | bytes 12296 | tf_op jit(solution)/shard_map/ppermute | solution.py:185
  46.1 3.7 %collective-permute-start.21 = (f32[8,128]{1,0:T(8,128)S(1)}, f32[8,128]{1,0:T(8,128)S(1)}, u32[]{:S(2)}, u32[]{:S(2)}) collective-permute-start(f32[8,128]{1,0:T(8,128)S(1)} %get-tuple-element.41.refs_0_), channel_id=1, source_target_pairs={{0,2},{1,3},{2,0},{3,1},{4,6},{5,7},{6,4},{7,5},{8,10},{9,11},{10,... | collective-permute-start | bytes 12296 | tf_op jit(solution)/shard_map/ppermute | solution.py:185
  47.1 2.7 %collective-permute-start.20 = (f32[8,128]{1,0:T(8,128)S(1)}, f32[8,128]{1,0:T(8,128)S(1)}, u32[]{:S(2)}, u32[]{:S(2)}) collective-permute-start(f32[8,128]{1,0:T(8,128)S(1)} %get-tuple-element.41.refs_0_), channel_id=1, source_target_pairs={{0,1},{1,0},{2,3},{3,2},{4,5},{5,4},{6,7},{7,6},{8,9},{9,8},{10,11... | collective-permute-start | bytes 12296 | tf_op jit(solution)/shard_map/ppermute | solution.py:185
  (3 other events, 5.3 us)

commit v2 on v1

v2 whole, which is shorter than its diff:
```python
import functools

import jax
import jax.numpy as jnp
from jax import lax
from jax.experimental import pallas as pl
from jax.experimental.pallas import tpu as pltpu
from jax.sharding import PartitionSpec as P

step_size = 0.05
ridge = 0.1
epsilon = 1e-06

CORES = 2
CHUNK = 256
F32 = jnp.float32
BF16 = jnp.bfloat16

VMEM = pl.BlockSpec(memory_space=pltpu.VMEM)
ANY = pl.BlockSpec(memory_space=pl.ANY)

NN = (((1,), (0,)), ((), ()))
TN = (((0,), (0,)), ((), ()))


def split(value):
    high = value.astype(BF16)
    low = (value - high.astype(F32)).astype(BF16)
    return high, low


def product(a, b, dims):
    dot = functools.partial(
        lax.dot_general, dimension_numbers=dims, preferred_element_type=F32
    )
    (a_high, a_low), (b_high, b_low) = a, b
    return dot(a_high, b_high) + (dot(a_high, b_low) + dot(a_low, b_high))


def tile_squares(value):
    squares = value * value
    rows, columns = squares.shape
    folded = squares.reshape(rows // 8, 8, columns).sum(0)
    total = folded[:, :128]
    for start in range(128, columns, 128):
        total = total + folded[:, start : start + 128]
    return total


def step_of(tiles, count):
    total = tiles[0]
    for tile in tiles[1:]:
        total = total + tile
    mean = jnp.sum(total, axis=(0, 1), keepdims=True) / count
    return step_size / jnp.sqrt(mean + epsilon)


def call(kernel, outs, *args, where=VMEM, scratch=(), flops=0):
    size = sum(a.size * a.dtype.itemsize for a in list(args) + list(outs))
    return pl.pallas_call(
        kernel,
        out_shape=outs,
        in_specs=[where] * len(args),
        out_specs=[VMEM] * len(outs),
        scratch_shapes=list(scratch),
        compiler_params=pltpu.CompilerParams(vmem_limit_bytes=16 << 20),
        cost_estimate=pl.CostEstimate(
            flops=flops, bytes_accessed=size, transcendentals=0
        ),
    )(*args)


def shape(rows, columns, dtype=F32):
    return jax.ShapeDtypeStruct((rows, columns), dtype)


def chunks_of(pixels):
    size = CHUNK if pixels % CHUNK == 0 else pixels
    return [pl.ds(start, size) for start in range(0, pixels, size)]


def place():
    at = lax.axis_index("sub")
    return at // CORES, lax.rem(at, CORES)


def aligned(index, size):
    return pl.ds(pl.multiple_of(index * size, size), size)


def prepare_kernel(stratum, *refs):
    with_strip = stratum == 0
    sources = refs[: 2 + with_strip]
    outs = refs[2 + with_strip : 4 + 6 * with_strip]
    buffers, sem = refs[len(sources) + len(outs) : -1], refs[-1]
    chunks = chunks_of(buffers[0].shape[0])
    copies = []
    for at, chunk in enumerate(chunks):
        row = []
        for which, (source, buffer) in enumerate(zip(sources, buffers)):
            view = source.at[chunk] if which == 2 else source.at[stratum, chunk]
            copy = pltpu.make_async_copy(view, buffer.at[chunk], sem.at[at, which])
            copy.start()
            row.append(copy)
        copies.append(row)
    for chunk, row in zip(chunks, copies):
        for copy in row:
            copy.wait()
        outs[0][:, chunk] = buffers[0][chunk, :].T
        outs[1][:, chunk] = buffers[1][chunk, :].astype(F32).T
        if with_strip:
            strip = buffers[2][chunk, :]
            outs[2][chunk, :] = strip
            outs[3][chunk, :], outs[4][chunk, :] = split(strip)
            outs[5][:, chunk], outs[6][:, chunk] = split(strip.T)


def errors_and_part(nx, relative, problem, block, outs):
    values_ref, weights_ref, th_ref, tl_ref, h_ref, l_ref = problem
    send_ref, keep_ref, high_ref, low_ref, part_ref = outs
    total = None
    for chunk in chunks_of(values_ref.shape[1]):
        predicted = product(block, (th_ref[:, chunk], tl_ref[:, chunk]), NN)
        errors = weights_ref[:, chunk] * (values_ref[:, chunk] - predicted)
        errors = split(errors)
        high_ref[:, chunk], low_ref[:, chunk] = errors
        part = product(errors, (h_ref[chunk, :], l_ref[chunk, :]), NN)
        total = part if total is None else total + part
    part_ref[...] = -total
    share = part_ref.shape[0] // (CORES * nx)
    chip, core = place()
    for dx in range(nx):
        target = lax.rem(chip + dx, nx) if relative else dx
        rows = pl.ds(dx * share, share)
        for ref, owner in ((keep_ref, core), (send_ref, 1 - core)):
            ref[rows, :] = part_ref[aligned(target * CORES + owner, share), :]


def first_kernel(order, *refs):
    n = len(order)
    nx = n // CORES
    shares, problem, outs = refs[:n], refs[n : n + 6], refs[n + 6 :]
    block_ref = outs[4]
    share = shares[0].shape[0]
    chip, core = place()
    for (dx, dc), ref in zip(order, shares):
        source = lax.rem(chip - dx + nx, nx) * CORES + lax.rem(core + dc, CORES)
        block_ref[aligned(source, share), :] = ref[...]
    errors_and_part(nx, False, problem, split(block_ref[...]), outs[:4] + outs[5:])


def later_kernel(nx, count, own_ref, other_ref, old_ref, *refs):
    problem, outs = refs[:6], refs[6:]
    share_ref, block_ref = outs[4:6]
    chip, core = place()
    share = own_ref.shape[0] // nx
    step = step_of([tile_squares(own_ref[...]), tile_squares(other_ref[...])], count)
    for grad_ref, owner in ((own_ref, core), (other_ref, 1 - core)):
        for at in range(nx):
            rows = aligned(at * CORES + owner, share)
            grad = grad_ref[pl.ds(at * share, share), :]
            block_ref[rows, :] = old_ref[rows, :] - step * grad
    share_ref[...] = block_ref[aligned(chip * CORES + core, share), :]
    errors_and_part(nx, True, problem, split(block_ref[...]), outs[:4] + outs[6:])


def gradient(strip, high, low, block):
    return ridge * strip - product((high, low), split(block), TN)


def first_gradient_kernel(nx, high_ref, low_ref, block_ref, strip_ref, *refs):
    old, (grad_ref, tile_ref, half_ref) = refs[:nx], refs[nx:]
    grad = gradient(strip_ref[...], high_ref[...], low_ref[...], block_ref[...])
    grad_ref[...] = grad
    tile_ref[...] = tile_squares(grad)
    share = old[0].shape[0]
    chip, _ = place()
    for dx, ref in enumerate(old):
        half_ref[aligned(lax.rem(chip - dx + nx, nx), share), :] = ref[...]


def later_gradient_kernel(high_ref, low_ref, block_ref, strip_ref, grad_ref, tile_ref):
    grad = gradient(strip_ref[...], high_ref[...], low_ref[...], block_ref[...])
    grad_ref[...] = grad
    tile_ref[...] = tile_squares(grad)


def first_step_kernel(count, nx, own_ref, other_ref, strip_ref, grad_ref, *refs):
    n = nx * CORES
    tiles, (strip_out, h_ref, l_ref, th_ref, tl_ref, block_ref) = refs[:n], refs[n:]
    strip = strip_ref[...] - step_of([t[...] for t in tiles], count) * grad_ref[...]
    strip_out[...] = strip
    h_ref[...], l_ref[...] = split(strip)
    th_ref[...], tl_ref[...] = split(strip.T)
    share = own_ref.shape[0] // nx
    _, core = place()
    for ref, owner in ((own_ref, core), (other_ref, 1 - core)):
        for at in range(nx):
            rows = aligned(at * CORES + owner, share)
            block_ref[rows, :] = ref[pl.ds(at * share, share), :]


def step_kernel(count, held_ref, grad_ref, *refs):
    step = step_of([t[...] for t in refs[:-1]], count)
    refs[-1][...] = held_ref[...] - step * grad_ref[...]


def last_grad_kernel(nx, block_ref, *refs):
    grad = ridge * block_ref[...]
    for ref in refs[:nx]:
        grad = grad + ref[...]
    refs[nx][...] = grad
    refs[nx + 1][...] = tile_squares(grad)


def orders(n):
    return [(dx, dc) for dx in range(n // CORES) for dc in range(CORES)]


def on_device(readings, coverage, pixel_factors, date_factors):
    pixels, rank = pixel_factors.shape
    share = date_factors.shape[0]
    n = lax.axis_size("sub")
    blocks = lax.axis_size("blk")
    nx = n // CORES
    dates = share * n
    half = share * nx
    pixel_count = pixels * n * rank
    date_count = dates * rank
    order = orders(n)
    work = 2 * pixels * dates * rank

    def moved(a, dx, dc):
        return (a // CORES + dx) % nx * CORES + (a % CORES + dc) % CORES

    def within(value, dx, dc):
        pairs = [(a, moved(a, dx, dc)) for a in range(n)]
        return lax.ppermute(value, "sub", pairs)

    def onward(value, dx):
        pairs = [
            (b * n + a, (b + 1) % blocks * n + moved(a, dx, 0))
            for b in range(blocks) for a in range(n)
        ]
        return lax.ppermute(value, ("blk", "sub"), pairs)

    def everywhere(value):
        return [value] + [within(value, *step) for step in order[1:]]

    def pixel_shape(dtype=F32):
        return shape(pixels, rank, dtype)

    def date_shape(dtype=F32):
        return shape(dates, pixels, dtype)

    def prepared(stratum, *args):
        kinds = [F32, jnp.int32, F32][: len(args)]
        outs = [date_shape(), date_shape()]
        if len(args) == 3:
            outs += [pixel_shape(), pixel_shape(BF16), pixel_shape(BF16)]
            outs += [shape(rank, pixels, BF16)] * 2
        scratch = [pltpu.VMEM((pixels, args[0].shape[2]), kind) for kind in kinds]
        scratch.append(pltpu.SemaphoreType.DMA((len(chunks_of(pixels)), len(args))))
        return call(
            functools.partial(prepare_kernel, stratum), outs, *args,
            where=ANY, scratch=scratch,
        )

    part_outs = [shape(half, rank)] * 2 + [date_shape(BF16)] * 2
    part_scratch = [pltpu.VMEM((dates, rank), F32)]

    shares = everywhere(date_factors)
    old = [onward(date_factors, dx) for dx in range(nx)]
    values, weights, strip, high, low, t_high, t_low = prepared(
        0, readings, coverage, pixel_factors
    )
    values_1, weights_1 = prepared(1, readings, coverage)
    send, keep, err_high, err_low, block = call(
        functools.partial(first_kernel, order), part_outs + [shape(dates, rank)],
        *shares, values, weights, t_high, t_low, high, low,
        scratch=part_scratch, flops=6 * work,
    )
    mine = keep + within(send, 0, 1)
    came = [onward(mine, dx) for dx in range(nx)]
    grad, tile, old_half = call(
        functools.partial(first_gradient_kernel, nx),
        [pixel_shape(), shape(8, 128), shape(half, rank)],
        err_high, err_low, block, strip, *old, flops=3 * work,
    )
    old_other = within(old_half, 0, 1)
    strip, high, low, t_high, t_low, old_block = call(
        functools.partial(first_step_kernel, pixel_count, nx),
        [pixel_shape(), pixel_shape(BF16), pixel_shape(BF16)]
        + [shape(rank, pixels, BF16)] * 2 + [shape(dates, rank)],
        old_half, old_other, strip, grad, *everywhere(tile),
    )
    date_half = sum(came[1:], came[0]) + ridge * old_half
    date_other = within(date_half, 0, 1)

    send, keep, err_high, err_low, own, block = call(
        functools.partial(later_kernel, nx, date_count),
        part_outs + [shape(share, rank), shape(dates, rank)],
        date_half, date_other, old_block, values_1, weights_1,
        t_high, t_low, high, low, scratch=part_scratch, flops=6 * work,
    )
    got = within(send, 0, 1)
    came = []
    for dx in range(nx):
        rows = slice(dx * share, (dx + 1) * share)
        came.append(onward(keep[rows] + got[rows], dx))
    held = onward(own, 0)
    grad, tile = call(
        later_gradient_kernel, [pixel_shape(), shape(8, 128)],
        err_high, err_low, block, strip, flops=3 * work,
    )
    strip, = call(
        functools.partial(step_kernel, pixel_count), [pixel_shape()],
        strip, grad, *everywhere(tile),
    )
    date_grad, tile = call(
        functools.partial(last_grad_kernel, nx),
        [shape(share, rank), shape(8, 128)], held, *came,
    )
    date_out, = call(
        functools.partial(step_kernel, date_count), [shape(share, rank)],
        held, date_grad, *everywhere(tile),
    )
    return strip, date_out


def solution(mesh):
    spec = P(("parts", "blk", "sub"), None)
    stacked = P(None, ("parts", "blk", "sub"), None)

    return jax.shard_map(
        on_device, mesh=mesh, in_specs=(stacked, stacked, spec, spec),
        out_specs=(spec, spec), check_vma=False,
    )
```

time: 50.8 us -> 47.3 us (0.931)
  Pallas kernels: 9.54 us -> 7.53 us
  waiting for transfers between devices: 18.9 us -> 17.3 us
    ppermute x16, waiting for transfers between devices: 6.8 us -> 4.18 us  [within(): return lax.ppermute(value, 'sub', pairs)]
    squeeze x2 -> x0, local copies, waits for them, and re-layouts: 2.57 us -> none  [the longest x1 1.59 us: on_device(): readings[1]]
    unnamed x8 -> x12, local copies, waits for them, and re-layouts: 1.42 us -> 3.96 us
    pallas_call x9 -> x10, Pallas kernels: 9.54 us -> 7.53 us  [call(): pl.pallas_call(kernel, out_shape=outs, in_specs=[where] * len(args), out_...]
    ppermute x7, waiting for transfers between devices: 12.1 us -> 13.1 us  [onward(): return lax.ppermute(value, ('blk', 'sub'), pairs)]
  transfers between devices with their start and end apart: 23 -> 23, of which waited for: 11 -> 9; matrix products, arithmetic and copies ran while one was open for 5% -> 0% of each run, Pallas kernels for 6% -> 10%
where the time goes in v2:
time: 47.3 us; the launch traced here: 47.1 us
  starting transfers between devices  17.4 us (37%)
  waiting for transfers between devices  17.3 us (37%)
  Pallas kernels  7.53 us (16%)
  local copies, waits for them, and re-layouts  3.96 us (8%)
  between operations  0.82 us (2%)
    ppermute x7, waiting for transfers between devices, onward(): return lax.ppermute(value, ('blk', 'sub'), pairs)  13.1 us
    ppermute x16, starting transfers between devices, within(): return lax.ppermute(value, 'sub', pairs)  8.83 us
    ppermute x7, starting transfers between devices, onward(): return lax.ppermute(value, ('blk', 'sub'), pairs)  8.61 us
    pallas_call x10, Pallas kernels, call(): pl.pallas_call(kernel, out_shape=outs, in_specs=[where] * len(args), out_...  7.53 us
    ppermute x16, waiting for transfers between devices, within(): return lax.ppermute(value, 'sub', pairs)  4.18 us
    unnamed x12, local copies, waits for them, and re-layouts  3.96 us
  transfers between devices with their start and end apart: 23, of which 9 were waited for; matrix products, arithmetic and copies ran while one was open for 0% of the time, Pallas kernels for 10%

profile of v2, /device:TPU:0, one launch (start us, length us, event | category | flops | bytes accessed | tf_op | source)
XLA Modules:
  0.0 47.1 jit_solution(10410103506329832801)
XLA Ops:
  1.2 2.6 %collective-permute-start.1 = (f32[64,256]{1,0:T(8,128)}, f32[64,256]{1,0:T(8,128)S(1)}, u32[]{:S(2)}, u32[]{:S(2)}) collective-permute-start(f32[64,256]{1,0:T(8,128)} %refs_0_.4), channel_id=1, source_target_pairs={{0,2},{1,3},{2,0},{3,1},{4,6},{5,7},{6,4},{7,5},{8,10},{9,11},{10,... | collective-permute-start | bytes 196616 | tf_op jit(solution)/shard_map/ppermute | solution.py:238
  3.8 1.4 %copy-done = f32[2,768,256]{2,1,0:T(8,128)S(1)} copy-done((f32[2,768,256]{2,1,0:T(8,128)S(1)}, f32[2,768,256]{2,1,0:T(8,128)}, u32[]{:S(2)}) %copy-start) | copy-done | bytes 1572888
  5.2 1.4 %copy-done.2 = s32[2,768,256]{2,1,0:T(8,128)S(1)} copy-done((s32[2,768,256]{2,1,0:T(8,128)S(1)}, s32[2,768,256]{2,1,0:T(8,128)}, u32[]{:S(2)}) %copy-start.2) | copy-done | bytes 1572888
  6.6 1.1 %copy-done.4 = f32[768,256]{1,0:T(8,128)S(1)} copy-done((f32[768,256]{1,0:T(8,128)S(1)}, f32[768,256]{1,0:T(8,128)}, u32[]{:S(2)}) %copy-start.4) | copy-done | bytes 786456
  7.7 1.1 %shard_map.59 = (f32[256,768]{1,0:T(8,128)S(1)}, f32[256,768]{1,0:T(8,128)S(1)}, f32[768,256]{1,0:T(8,128)S(1)}, bf16[768,256]{1,0:T(8,128)(2,1)S(1)}, bf16[768,...) custom-call(f32[2,768,256]{2,1,0:T(8,128)S(1)} %copy-done, ...), custom_call_target="tpu_custom_call" | custom-call | bytes 7864320 | tf_op jit(solution)/shard_map/pallas_call | solution.py:60
  8.9 1.1 %shard_map.60 = (f32[128,256]{1,0:T(8,128)S(1)}, f32[128,256]{1,0:T(8,128)S(1)}, bf16[256,768]{1,0:T(8,128)(2,1)S(1)}, bf16[256,768]{1,0:T(8,128)(2,1)S(1)}, f32[256,256]{1,0:T(8,128)S(1)}) custom-call(f32[64,256]{1,0:T(8,128)S(1)} %copy-done.5, f32[64,256]{1,0:T(8,128)S(1)} %collective-permute-done.refs_1_, f32[64,256]{1,0:T(8,128)S(1)} %collective-permute-done.1.refs_2_, ...), custom_call_target="tpu_custom_call" | custom-call | flops 603979776 | bytes 4718592 | tf_op jit(solution)/shard_map/pallas_call | solution.py:60
  10.2 1.2 %collective-permute-done.9 = f32[128,256]{1,0:T(8,128)S(1)} collective-permute-done((f32[128,256]{1,0:T(8,128)S(1)}, f32[128,256]{1,0:T(8,128)S(1)}, u32[]{:S(2)}, u32[]{:S(2)}) %collective-permute-start.9) | collective-permute-done | bytes 131104 | tf_op jit(solution)/shard_map/ppermute | solution.py:238
  11.4 1.9 %collective-permute-start.10 = (f32[128,256]{1,0:T(8,128)S(1)}, f32[128,256]{1,0:T(8,128)S(1)}, u32[]{:S(2)}, u32[]{:S(2)}) collective-permute-start(f32[128,256]{1,0:T(8,128)S(1)} %add.15), channel_id=1, source_target_pairs={{0,4},{1,5},{2,6},{3,7},{4,8},{5,9},{6,10},{7,11},{8,12},{9,13},{1... | collective-permute-start | bytes 393224 | tf_op jit(solution)/shard_map/ppermute | solution.py:245
  13.3 2.5 %collective-permute-start.11 = (f32[128,256]{1,0:T(8,128)S(1)}, f32[128,256]{1,0:T(8,128)S(1)}, u32[]{:S(2)}, u32[]{:S(2)}) collective-permute-start(f32[128,256]{1,0:T(8,128)S(1)} %add.15), channel_id=1, source_target_pairs={{0,6},{1,7},{2,4},{3,5},{4,10},{5,11},{6,8},{7,9},{8,14},{9,15},{1... | collective-permute-start | bytes 393224 | tf_op jit(solution)/shard_map/ppermute | solution.py:245
  15.8 1.6 %collective-permute-start.3 = (f32[64,256]{1,0:T(8,128)S(1)}, f32[64,256]{1,0:T(8,128)S(1)}, u32[]{:S(2)}, u32[]{:S(2)}) collective-permute-start(f32[64,256]{1,0:T(8,128)S(1)} %copy-done.5), channel_id=1, source_target_pairs={{0,4},{1,5},{2,6},{3,7},{4,8},{5,9},{6,10},{7,11},{8,12},{9,13},{1... | collective-permute-start | bytes 196616 | tf_op jit(solution)/shard_map/ppermute | solution.py:245
  17.4 6.5 %collective-permute-done.3.refs_0_ = f32[64,256]{1,0:T(8,128)S(1)} collective-permute-done((f32[64,256]{1,0:T(8,128)S(1)}, f32[64,256]{1,0:T(8,128)S(1)}, u32[]{:S(2)}, u32[]{:S(2)}) %collective-permute-start.3) | collective-permute-done | bytes 65568 | tf_op jit(solution)/shard_map/ppermute | solution.py:245
  23.9 2.0 %collective-permute-done.4.refs_1_ = f32[64,256]{1,0:T(8,128)S(1)} collective-permute-done((f32[64,256]{1,0:T(8,128)S(1)}, f32[64,256]{1,0:T(8,128)S(1)}, u32[]{:S(2)}, u32[]{:S(2)}) %collective-permute-start.4) | collective-permute-done | bytes 65568 | tf_op jit(solution)/shard_map/ppermute | solution.py:245
  27.7 1.3 %collective-permute-start.8 = (f32[8,128]{1,0:T(8,128)S(1)}, f32[8,128]{1,0:T(8,128)S(1)}, u32[]{:S(2)}, u32[]{:S(2)}) collective-permute-start(f32[8,128]{1,0:T(8,128)S(1)} %get-tuple-element.47.refs_0_), channel_id=1, source_target_pairs={{0,3},{1,2},{2,1},{3,0},{4,7},{5,6},{6,5},{7,4},{8,11},{9,10},{10,... | collective-permute-start | bytes 12296 | tf_op jit(solution)/shard_map/ppermute | solution.py:238
  28.9 0.8 %shard_map.63 = (f32[256,768]{1,0:T(8,128)S(1)}, f32[256,768]{1,0:T(8,128)S(1)}) custom-call(f32[2,768,256]{2,1,0:T(8,128)S(1)} %copy-done.1, s32[2,768,256]{2,1,0:T(8,128)S(1)} %copy-done.3), custom_call_target="tpu_custom_call" | custom-call | bytes 4718592 | tf_op jit(solution)/shard_map/pallas_call | solution.py:60
  29.7 1.0 %collective-permute-done.7.refs_2_ = f32[8,128]{1,0:T(8,128)S(1)} collective-permute-done((f32[8,128]{1,0:T(8,128)S(1)}, f32[8,128]{1,0:T(8,128)S(1)}, u32[]{:S(2)}, u32[]{:S(2)}) %collective-permute-start.7) | collective-permute-done | bytes 4128 | tf_op jit(solution)/shard_map/ppermute | solution.py:238
  31.2 1.2 %shard_map.64 = (f32[128,256]{1,0:T(8,128)S(1)}, f32[128,256]{1,0:T(8,128)S(1)}, bf16[256,768]{1,0:T(8,128)(2,1)S(1)}, bf16[256,768]{1,0:T(8,128)(2,1)S(1)}, f32...) custom-call(f32[128,256]{1,0:T(8,128)S(1)} %multiply_add_fusion.own_ref, f32[128,256]{1,0:T(8,128)S(1)} %collective-permute-done.12.other_ref, ...), custom_call_target="tpu_custom_call" | custom-call | flops 603979776 | bytes 5046272 | tf_op jit(solution)/shard_map/pallas_call | solution.py:60
  32.6 1.2 %collective-permute-done.17 = f32[128,256]{1,0:T(8,128)S(1)} collective-permute-done((f32[128,256]{1,0:T(8,128)S(1)}, f32[128,256]{1,0:T(8,128)S(1)}, u32[]{:S(2)}, u32[]{:S(2)}) %collective-permute-start.17) | collective-permute-done | bytes 131104 | tf_op jit(solution)/shard_map/ppermute | solution.py:238
  34.0 2.5 %collective-permute-start.19 = (f32[64,256]{1,0:T(8,128)S(1)}, f32[64,256]{1,0:T(8,128)S(1)}, u32[]{:S(2)}, u32[]{:S(2)}) collective-permute-start(f32[64,256]{1,0:T(8,128)S(1)} %get-tuple-element.68), channel_id=1, source_target_pairs={{0,6},{1,7},{2,4},{3,5},{4,10},{5,11},{6,8},{7,9},{8,14},{9,15},{1... | collective-permute-start | bytes 196616 | tf_op jit(solution)/shard_map/ppermute | solution.py:245
  37.7 1.5 %collective-permute-done.16.block_ref.held_ref = f32[64,256]{1,0:T(8,128)S(1)} collective-permute-done((f32[64,256]{1,0:T(8,128)S(1)}, f32[64,256]{1,0:T(8,128)S(1)}, u32[]{:S(2)}, u32[]{:S(2)}) %collective-permute-start.16) | collective-permute-done | bytes 65568 | tf_op jit(solution)/shard_map/ppermute | solution.py:245
  39.4 1.3 %collective-permute-done.18.refs_0_ = f32[64,256]{1,0:T(8,128)S(1)} collective-permute-done((f32[64,256]{1,0:T(8,128)S(1)}, f32[64,256]{1,0:T(8,128)S(1)}, u32[]{:S(2)}, u32[]{:S(2)}) %collective-permute-start.18) | collective-permute-done | bytes 65568 | tf_op jit(solution)/shard_map/ppermute | solution.py:245
  40.7 1.9 %collective-permute-done.19.refs_1_ = f32[64,256]{1,0:T(8,128)S(1)} collective-permute-done((f32[64,256]{1,0:T(8,128)S(1)}, f32[64,256]{1,0:T(8,128)S(1)}, u32[]{:S(2)}, u32[]{:S(2)}) %collective-permute-start.19) | collective-permute-done | bytes 65568 | tf_op jit(solution)/shard_map/ppermute | solution.py:245
  43.3 1.2 %collective-permute-start.22 = (f32[8,128]{1,0:T(8,128)S(1)}, f32[8,128]{1,0:T(8,128)S(1)}, u32[]{:S(2)}, u32[]{:S(2)}) collective-permute-start(f32[8,128]{1,0:T(8,128)S(1)} %get-tuple-element.67.refs_0_), channel_id=1, source_target_pairs={{0,3},{1,2},{2,1},{3,0},{4,7},{5,6},{6,5},{7,4},{8,11},{9,10},{10,... | collective-permute-start | bytes 12296 | tf_op jit(solution)/shard_map/ppermute | solution.py:238
  44.5 1.1 %shard_map.66 = f32[768,256]{1,0:T(8,128)} custom-call(f32[768,256]{1,0:T(8,128)S(1)} %get-tuple-element.48.strip_ref.held_ref, f32[768,256]{1,0:T(8,128)S(1)} %get-tuple-element.61.grad_ref, f32[8,128]{1,0:T(8,128)S(1)} %get-tuple-element.62.refs_0_, f32[8,128]{1,0:T(8,128)S(1)} %collective-permute-done.13.refs_1_, ...), custom_call_target="tpu_custom_call" | custom-call | bytes 2375680 | tf_op jit(solution)/shard_map/pallas_call | solution.py:60
  46.3 0.8 %shard_map.68 = f32[64,256]{1,0:T(8,128)} custom-call(f32[64,256]{1,0:T(8,128)S(1)} %collective-permute-done.16.block_ref.held_ref, f32[64,256]{1,0:T(8,128)S(1)} %get-tuple-element.66.grad_ref, f32[8,128]{1,0:T(8,128)S(1)} %get-tuple-element.67.refs_0_, f32[8,128]{1,0:T(8,128)S(1)} %collective-permute-done.20.refs_1_, ...), custom_call_target="tpu_custom_call" | custom-call | bytes 212992 | tf_op jit(solution)/shard_map/pallas_call | solution.py:60
  (47 shorter events, 6.3 us)
Async XLA Ops:
  0.6 8.2 %collective-permute-start = (f32[64,256]{1,0:T(8,128)}, f32[64,256]{1,0:T(8,128)S(1)}, u32[]{:S(2)}, u32[]{:S(2)}) collective-permute-start(f32[64,256]{1,0:T(8,128)} %refs_0_.4), channel_id=1, source_target_pairs={{0,1},{1,0},{2,3},{3,2},{4,5},{5,4},{6,7},{7,6},{8,9},{9,8},{10,11... | collective-permute-start | bytes 196616 | tf_op jit(solution)/shard_map/ppermute | solution.py:238
  1.2 7.6 %collective-permute-start.1 = (f32[64,256]{1,0:T(8,128)}, f32[64,256]{1,0:T(8,128)S(1)}, u32[]{:S(2)}, u32[]{:S(2)}) collective-permute-start(f32[64,256]{1,0:T(8,128)} %refs_0_.4), channel_id=1, source_target_pairs={{0,2},{1,3},{2,0},{3,1},{4,6},{5,7},{6,4},{7,5},{8,10},{9,11},{10,... | collective-permute-start | bytes 196616 | tf_op jit(solution)/shard_map/ppermute | solution.py:238
  3.7 5.1 %collective-permute-start.2 = (f32[64,256]{1,0:T(8,128)}, f32[64,256]{1,0:T(8,128)S(1)}, u32[]{:S(2)}, u32[]{:S(2)}) collective-permute-start(f32[64,256]{1,0:T(8,128)} %refs_0_.4), channel_id=1, source_target_pairs={{0,3},{1,2},{2,1},{3,0},{4,7},{5,6},{6,5},{7,4},{8,11},{9,10},{10,... | collective-permute-start | bytes 196616 | tf_op jit(solution)/shard_map/ppermute | solution.py:238
  8.9 20.1 %copy-start.3 = (s32[2,768,256]{2,1,0:T(8,128)S(1)}, s32[2,768,256]{2,1,0:T(8,128)}, u32[]{:S(2)}) copy-start(s32[2,768,256]{2,1,0:T(8,128)} %refs_1_.3) | copy-start | bytes 4718596
  10.0 1.4 %collective-permute-start.9 = (f32[128,256]{1,0:T(8,128)S(1)}, f32[128,256]{1,0:T(8,128)S(1)}, u32[]{:S(2)}, u32[]{:S(2)}) collective-permute-start(f32[128,256]{1,0:T(8,128)S(1)} %get-tuple-element.50), channel_id=1, source_target_pairs={{0,1},{1,0},{2,3},{3,2},{4,5},{5,4},{6,7},{7,6},{8,9},{9,8},{10,11... | collective-permute-start | bytes 393224 | tf_op jit(solution)/shard_map/ppermute | solution.py:238
  11.4 15.1 %collective-permute-start.10 = (f32[128,256]{1,0:T(8,128)S(1)}, f32[128,256]{1,0:T(8,128)S(1)}, u32[]{:S(2)}, u32[]{:S(2)}) collective-permute-start(f32[128,256]{1,0:T(8,128)S(1)} %add.15), channel_id=1, source_target_pairs={{0,4},{1,5},{2,6},{3,7},{4,8},{5,9},{6,10},{7,11},{8,12},{9,13},{1... | collective-permute-start | bytes 393224 | tf_op jit(solution)/shard_map/ppermute | solution.py:245
  13.3 13.2 %collective-permute-start.11 = (f32[128,256]{1,0:T(8,128)S(1)}, f32[128,256]{1,0:T(8,128)S(1)}, u32[]{:S(2)}, u32[]{:S(2)}) collective-permute-start(f32[128,256]{1,0:T(8,128)S(1)} %add.15), channel_id=1, source_target_pairs={{0,6},{1,7},{2,4},{3,5},{4,10},{5,11},{6,8},{7,9},{8,14},{9,15},{1... | collective-permute-start | bytes 393224 | tf_op jit(solution)/shard_map/ppermute | solution.py:245
  15.8 8.1 %collective-permute-start.3 = (f32[64,256]{1,0:T(8,128)S(1)}, f32[64,256]{1,0:T(8,128)S(1)}, u32[]{:S(2)}, u32[]{:S(2)}) collective-permute-start(f32[64,256]{1,0:T(8,128)S(1)} %copy-done.5), channel_id=1, source_target_pairs={{0,4},{1,5},{2,6},{3,7},{4,8},{5,9},{6,10},{7,11},{8,12},{9,13},{1... | collective-permute-start | bytes 196616 | tf_op jit(solution)/shard_map/ppermute | solution.py:245
  17.4 8.5 %collective-permute-start.4 = (f32[64,256]{1,0:T(8,128)S(1)}, f32[64,256]{1,0:T(8,128)S(1)}, u32[]{:S(2)}, u32[]{:S(2)}) collective-permute-start(f32[64,256]{1,0:T(8,128)S(1)} %copy-done.5), channel_id=1, source_target_pairs={{0,6},{1,7},{2,4},{3,5},{4,10},{5,11},{6,8},{7,9},{8,14},{9,15},{1... | collective-permute-start | bytes 196616 | tf_op jit(solution)/shard_map/ppermute | solution.py:245
  26.4 4.4 %collective-permute-start.5 = (f32[128,256]{1,0:T(8,128)S(1)}, f32[128,256]{1,0:T(8,128)S(1)}, u32[]{:S(2)}, u32[]{:S(2)}) collective-permute-start(f32[128,256]{1,0:T(8,128)S(1)} %get-tuple-element.45.own_ref), channel_id=1, source_target_pairs={{0,1},{1,0},{2,3},{3,2},{4,5},{5,4},{6,7},{7,6},{8,9},{9,8},{10,11... | collective-permute-start | bytes 393224 | tf_op jit(solution)/shard_map/ppermute | solution.py:238
  26.5 4.7 %collective-permute-start.12 = (f32[128,256]{1,0:T(8,128)S(1)}, f32[128,256]{1,0:T(8,128)S(1)}, u32[]{:S(2)}, u32[]{:S(2)}) collective-permute-start(f32[128,256]{1,0:T(8,128)S(1)} %multiply_add_fusion.own_ref), channel_id=1, source_target_pairs={{0,1},{1,0},{2,3},{3,2},{4,5},{5,4},{6,7},{7,6},{8,9},{9,8},{10,11... | collective-permute-start | bytes 393224 | tf_op jit(solution)/shard_map/ppermute | solution.py:238
  27.1 2.7 %collective-permute-start.6 = (f32[8,128]{1,0:T(8,128)S(1)}, f32[8,128]{1,0:T(8,128)S(1)}, u32[]{:S(2)}, u32[]{:S(2)}) collective-permute-start(f32[8,128]{1,0:T(8,128)S(1)} %get-tuple-element.47.refs_0_), channel_id=1, source_target_pairs={{0,1},{1,0},{2,3},{3,2},{4,5},{5,4},{6,7},{7,6},{8,9},{9,8},{10,11... | collective-permute-start | bytes 12296 | tf_op jit(solution)/shard_map/ppermute | solution.py:238
  27.2 3.6 %collective-permute-start.7 = (f32[8,128]{1,0:T(8,128)S(1)}, f32[8,128]{1,0:T(8,128)S(1)}, u32[]{:S(2)}, u32[]{:S(2)}) collective-permute-start(f32[8,128]{1,0:T(8,128)S(1)} %get-tuple-element.47.refs_0_), channel_id=1, source_target_pairs={{0,2},{1,3},{2,0},{3,1},{4,6},{5,7},{6,4},{7,5},{8,10},{9,11},{10,... | collective-permute-start | bytes 12296 | tf_op jit(solution)/shard_map/ppermute | solution.py:238
  27.7 3.1 %collective-permute-start.8 = (f32[8,128]{1,0:T(8,128)S(1)}, f32[8,128]{1,0:T(8,128)S(1)}, u32[]{:S(2)}, u32[]{:S(2)}) collective-permute-start(f32[8,128]{1,0:T(8,128)S(1)} %get-tuple-element.47.refs_0_), channel_id=1, source_target_pairs={{0,3},{1,2},{2,1},{3,0},{4,7},{5,6},{6,5},{7,4},{8,11},{9,10},{10,... | collective-permute-start | bytes 12296 | tf_op jit(solution)/shard_map/ppermute | solution.py:238
  32.4 1.4 %collective-permute-start.17 = (f32[128,256]{1,0:T(8,128)S(1)}, f32[128,256]{1,0:T(8,128)S(1)}, u32[]{:S(2)}, u32[]{:S(2)}) collective-permute-start(f32[128,256]{1,0:T(8,128)S(1)} %get-tuple-element.65), channel_id=1, source_target_pairs={{0,1},{1,0},{2,3},{3,2},{4,5},{5,4},{6,7},{7,6},{8,9},{9,8},{10,11... | collective-permute-start | bytes 393224 | tf_op jit(solution)/shard_map/ppermute | solution.py:238
  32.6 6.5 %collective-permute-start.16 = (f32[64,256]{1,0:T(8,128)S(1)}, f32[64,256]{1,0:T(8,128)S(1)}, u32[]{:S(2)}, u32[]{:S(2)}) collective-permute-start(f32[64,256]{1,0:T(8,128)S(1)} %get-tuple-element.63), channel_id=1, source_target_pairs={{0,4},{1,5},{2,6},{3,7},{4,8},{5,9},{6,10},{7,11},{8,12},{9,13},{1... | collective-permute-start | bytes 196616 | tf_op jit(solution)/shard_map/ppermute | solution.py:245
  33.9 6.8 %collective-permute-start.18 = (f32[64,256]{1,0:T(8,128)S(1)}, f32[64,256]{1,0:T(8,128)S(1)}, u32[]{:S(2)}, u32[]{:S(2)}) collective-permute-start(f32[64,256]{1,0:T(8,128)S(1)} %get-tuple-element.69), channel_id=1, source_target_pairs={{0,4},{1,5},{2,6},{3,7},{4,8},{5,9},{6,10},{7,11},{8,12},{9,13},{1... | collective-permute-start | bytes 196616 | tf_op jit(solution)/shard_map/ppermute | solution.py:245
  34.0 8.6 %collective-permute-start.19 = (f32[64,256]{1,0:T(8,128)S(1)}, f32[64,256]{1,0:T(8,128)S(1)}, u32[]{:S(2)}, u32[]{:S(2)}) collective-permute-start(f32[64,256]{1,0:T(8,128)S(1)} %get-tuple-element.68), channel_id=1, source_target_pairs={{0,6},{1,7},{2,4},{3,5},{4,10},{5,11},{6,8},{7,9},{8,14},{9,15},{1... | collective-permute-start | bytes 196616 | tf_op jit(solution)/shard_map/ppermute | solution.py:245
  37.0 6.3 %collective-permute-start.13 = (f32[8,128]{1,0:T(8,128)S(1)}, f32[8,128]{1,0:T(8,128)S(1)}, u32[]{:S(2)}, u32[]{:S(2)}) collective-permute-start(f32[8,128]{1,0:T(8,128)S(1)} %get-tuple-element.62.refs_0_), channel_id=1, source_target_pairs={{0,1},{1,0},{2,3},{3,2},{4,5},{5,4},{6,7},{7,6},{8,9},{9,8},{10,11... | collective-permute-start | bytes 12296 | tf_op jit(solution)/shard_map/ppermute | solution.py:238
  37.1 7.4 %collective-permute-start.14 = (f32[8,128]{1,0:T(8,128)S(1)}, f32[8,128]{1,0:T(8,128)S(1)}, u32[]{:S(2)}, u32[]{:S(2)}) collective-permute-start(f32[8,128]{1,0:T(8,128)S(1)} %get-tuple-element.62.refs_0_), channel_id=1, source_target_pairs={{0,2},{1,3},{2,0},{3,1},{4,6},{5,7},{6,4},{7,5},{8,10},{9,11},{10,... | collective-permute-start | bytes 12296 | tf_op jit(solution)/shard_map/ppermute | solution.py:238
  39.2 5.3 %collective-permute-start.15 = (f32[8,128]{1,0:T(8,128)S(1)}, f32[8,128]{1,0:T(8,128)S(1)}, u32[]{:S(2)}, u32[]{:S(2)}) collective-permute-start(f32[8,128]{1,0:T(8,128)S(1)} %get-tuple-element.62.refs_0_), channel_id=1, source_target_pairs={{0,3},{1,2},{2,1},{3,0},{4,7},{5,6},{6,5},{7,4},{8,11},{9,10},{10,... | collective-permute-start | bytes 12296 | tf_op jit(solution)/shard_map/ppermute | solution.py:238
  42.6 3.1 %collective-permute-start.20 = (f32[8,128]{1,0:T(8,128)S(1)}, f32[8,128]{1,0:T(8,128)S(1)}, u32[]{:S(2)}, u32[]{:S(2)}) collective-permute-start(f32[8,128]{1,0:T(8,128)S(1)} %get-tuple-element.67.refs_0_), channel_id=1, source_target_pairs={{0,1},{1,0},{2,3},{3,2},{4,5},{5,4},{6,7},{7,6},{8,9},{9,8},{10,11... | collective-permute-start | bytes 12296 | tf_op jit(solution)/shard_map/ppermute | solution.py:238
  42.6 3.7 %collective-permute-start.21 = (f32[8,128]{1,0:T(8,128)S(1)}, f32[8,128]{1,0:T(8,128)S(1)}, u32[]{:S(2)}, u32[]{:S(2)}) collective-permute-start(f32[8,128]{1,0:T(8,128)S(1)} %get-tuple-element.67.refs_0_), channel_id=1, source_target_pairs={{0,2},{1,3},{2,0},{3,1},{4,6},{5,7},{6,4},{7,5},{8,10},{9,11},{10,... | collective-permute-start | bytes 12296 | tf_op jit(solution)/shard_map/ppermute | solution.py:238
  43.3 3.1 %collective-permute-start.22 = (f32[8,128]{1,0:T(8,128)S(1)}, f32[8,128]{1,0:T(8,128)S(1)}, u32[]{:S(2)}, u32[]{:S(2)}) collective-permute-start(f32[8,128]{1,0:T(8,128)S(1)} %get-tuple-element.67.refs_0_), channel_id=1, source_target_pairs={{0,3},{1,2},{2,1},{3,0},{4,7},{5,6},{6,5},{7,4},{8,11},{9,10},{10,... | collective-permute-start | bytes 12296 | tf_op jit(solution)/shard_map/ppermute | solution.py:238
  (5 other events, 24.1 us)

commit v3 on v2

v3 whole, which is shorter than its diff:
```python
import functools

import jax
import jax.numpy as jnp
from jax import lax
from jax.experimental import pallas as pl
from jax.experimental.pallas import tpu as pltpu
from jax.sharding import PartitionSpec as P


step_size = 0.05
ridge = 0.1
epsilon = 1e-06

CORES = 2
CHUNK = 256
F32 = jnp.float32
BF16 = jnp.bfloat16

VMEM = pl.BlockSpec(memory_space=pltpu.VMEM)
HBM = pl.BlockSpec(memory_space=pltpu.HBM)

NN = (((1,), (0,)), ((), ()))
TN = (((0,), (0,)), ((), ()))


def split(value):
    high = value.astype(BF16)
    low = (value - high.astype(F32)).astype(BF16)
    return high, low


def product(a, b, dims):
    dot = functools.partial(
        lax.dot_general, dimension_numbers=dims, preferred_element_type=F32
    )
    (a_high, a_low), (b_high, b_low) = a, b
    return dot(a_high, b_high) + (dot(a_high, b_low) + dot(a_low, b_high))


def tile_squares(value):
    squares = value * value
    rows, columns = squares.shape
    folded = squares.reshape(rows // 8, 8, columns).sum(0)
    total = folded[:, :128]
    for start in range(128, columns, 128):
        total = total + folded[:, start : start + 128]
    return total


def step_of(tiles, count):
    total = tiles[0]
    for tile in tiles[1:]:
        total = total + tile
    mean = jnp.sum(total, axis=(0, 1), keepdims=True) / count
    return step_size / jnp.sqrt(mean + epsilon)


def call(kernel, outs, *args, where=VMEM, scratch=(), flops=0):
    size = sum(a.size * a.dtype.itemsize for a in list(args) + list(outs))
    return pl.pallas_call(
        kernel,
        out_shape=outs,
        in_specs=[where] * len(args),
        out_specs=[VMEM] * len(outs),
        scratch_shapes=list(scratch),
        compiler_params=pltpu.CompilerParams(vmem_limit_bytes=16 << 20),
        cost_estimate=pl.CostEstimate(
            flops=flops, bytes_accessed=size, transcendentals=0
        ),
    )(*args)


def shape(rows, columns, dtype=F32):
    return jax.ShapeDtypeStruct((rows, columns), dtype)


def chunks_of(pixels):
    size = CHUNK if pixels % CHUNK == 0 else pixels
    return [pl.ds(start, size) for start in range(0, pixels, size)]


def place():
    at = lax.axis_index("sub")
    return at // CORES, lax.rem(at, CORES)


def aligned(index, size):
    return pl.ds(pl.multiple_of(index * size, size), size)


def prepare_kernel(stratum, share, *refs):
    with_strip = stratum == 0
    sources = refs[: 2 + with_strip]
    outs = refs[2 + with_strip : 4 + 6 * with_strip]
    buffers, sem = refs[len(sources) + len(outs) : -1], refs[-1]
    pixels, dates = buffers[0].shape
    nx = dates // share // CORES
    chunks = chunks_of(pixels)
    copies = []
    for at, chunk in enumerate(chunks):
        row = []
        for which, (source, buffer) in enumerate(zip(sources, buffers)):
            view = source.at[chunk] if which == 2 else source.at[stratum, chunk]
            copy = pltpu.make_async_copy(view, buffer.at[chunk], sem.at[at, which])
            copy.start()
            row.append(copy)
        copies.append(row)
    _, core = place()
    for chunk, row in zip(chunks, copies):
        for copy in row:
            copy.wait()
        for out, buffer in zip(outs[:2], buffers[:2]):
            turned = buffer[chunk, :].astype(F32).T
            for at in range(nx * CORES):
                own = jnp.where(core == at % CORES, nx, 0)
                rows = aligned(own + at // CORES, share)
                out[rows, chunk] = turned[at * share : (at + 1) * share]
        if with_strip:
            strip = buffers[2][chunk, :]
            outs[2][chunk, :] = strip
            outs[3][chunk, :], outs[4][chunk, :] = split(strip)
            outs[5][:, chunk], outs[6][:, chunk] = split(strip.T)


def errors_and_part(side, problem, block, high_ref, low_ref):
    values_ref, weights_ref, th_ref, tl_ref, h_ref, l_ref = problem
    half = block.shape[0]
    rows = slice(side * half, (side + 1) * half)
    block = split(block)
    total = None
    for chunk in chunks_of(values_ref.shape[1]):
        predicted = product(block, (th_ref[:, chunk], tl_ref[:, chunk]), NN)
        errors = weights_ref[rows, chunk] * (values_ref[rows, chunk] - predicted)
        errors = split(errors)
        high_ref[:, chunk], low_ref[:, chunk] = errors
        part = product(errors, (h_ref[chunk, :], l_ref[chunk, :]), NN)
        total = part if total is None else total + part
    return -total


def with_ridge(part, block):
    chip, _ = place()
    return part + jnp.where(chip == 0, ridge, 0.0) * block


def first_send_kernel(order, *refs):
    n = len(order)
    nx = n // CORES
    shares, problem = refs[:n], refs[n : n + 6]
    send_ref, high_ref, low_ref, other_ref, own_ref = refs[n + 6 :]
    share = shares[0].shape[0]
    chip, _ = place()
    for (dx, dc), ref in zip(order, shares):
        rows = aligned(lax.rem(chip - dx + nx, nx), share)
        (other_ref if dc else own_ref)[rows, :] = ref[...]
    send_ref[...] = errors_and_part(0, problem, other_ref[...], high_ref, low_ref)


def first_keep_kernel(block_ref, *refs):
    problem, (keep_ref, high_ref, low_ref) = refs[:6], refs[6:]
    block = block_ref[...]
    part = errors_and_part(1, problem, block, high_ref, low_ref)
    keep_ref[...] = with_ridge(part, block)


def later_step(count, own_ref, other_ref):
    return step_of([tile_squares(own_ref[...]), tile_squares(other_ref[...])], count)


def later_send_kernel(count, own_ref, other_ref, message_ref, *refs):
    problem, (send_ref, high_ref, low_ref, block_ref) = refs[:6], refs[6:]
    step = later_step(count, own_ref, other_ref)
    block = message_ref[: other_ref.shape[0], :] - step * other_ref[...]
    block_ref[...] = block
    send_ref[...] = errors_and_part(0, problem, block, high_ref, low_ref)


def later_keep_kernel(count, share, own_ref, other_ref, message_ref, *refs):
    problem, (keep_ref, high_ref, low_ref, block_ref, share_ref) = refs[:6], refs[6:]
    step = later_step(count, own_ref, other_ref)
    block = message_ref[: own_ref.shape[0], :] - step * own_ref[...]
    block_ref[...] = block
    chip, _ = place()
    share_ref[...] = block_ref[aligned(chip, share), :]
    part = errors_and_part(1, problem, block, high_ref, low_ref)
    keep_ref[...] = with_ridge(part, block)


def pixel_gradient(strip_ref, errors, blocks):
    joined = [jnp.concatenate([ref[...] for ref in part], 0) for part in errors]
    block = jnp.concatenate([ref[...] for ref in blocks], 0)
    return ridge * strip_ref[...] - product(joined, split(block), TN)


def first_gradient_kernel(strip_ref, old_ref, h0, l0, h1, l1, b0, b1, grad_ref, out_ref):
    grad = pixel_gradient(strip_ref, ((h0, h1), (l0, l1)), (b0, b1))
    grad_ref[...] = grad
    share, rank = old_ref.shape
    out_ref[:share, :] = old_ref[...]
    out_ref[share:, :128] = tile_squares(grad)
    if rank > 128:
        out_ref[share:, 128:] = jnp.zeros((8, rank - 128), F32)


def later_gradient_kernel(strip_ref, h0, l0, h1, l1, b0, b1, grad_ref, tile_ref):
    grad = pixel_gradient(strip_ref, ((h0, h1), (l0, l1)), (b0, b1))
    grad_ref[...] = grad
    tile_ref[...] = tile_squares(grad)


def join_kernel(*refs):
    messages, out_ref = refs[:-1], refs[-1]
    nx = len(messages)
    share = messages[0].shape[0] - 8
    chip, _ = place()
    total = None
    for dx, ref in enumerate(messages):
        out_ref[aligned(lax.rem(chip - dx + nx, nx), share), :] = ref[:share, :]
        tile = ref[share:, :]
        total = tile if total is None else total + tile
    out_ref[nx * share :, :] = total


def first_step_kernel(count, own_ref, other_ref, strip_ref, grad_ref, *outs):
    strip_out, h_ref, l_ref, th_ref, tl_ref = outs
    half = own_ref.shape[0] - 8
    step = step_of([own_ref[half:, :128], other_ref[half:, :128]], count)
    strip = strip_ref[...] - step * grad_ref[...]
    strip_out[...] = strip
    h_ref[...], l_ref[...] = split(strip)
    th_ref[...], tl_ref[...] = split(strip.T)


def step_kernel(count, held_ref, grad_ref, *refs):
    step = step_of([t[...] for t in refs[:-1]], count)
    refs[-1][...] = held_ref[...] - step * grad_ref[...]


def last_gradient_kernel(share, *refs):
    parts, (grad_ref, tile_ref), sum_ref = refs[:-3], refs[-3:-1], refs[-1]
    total = parts[0][...]
    for ref in parts[1:]:
        total = total + ref[...]
    sum_ref[...] = total
    tile_ref[...] = tile_squares(total)
    chip, _ = place()
    grad_ref[...] = sum_ref[aligned(chip, share), :]


def orders(n):
    return [(dx, dc) for dx in range(n // CORES) for dc in range(CORES)]


def on_device(readings, coverage, pixel_factors, date_factors):
    pixels, rank = pixel_factors.shape
    share = date_factors.shape[0]
    n = lax.axis_size("sub")
    blocks = lax.axis_size("blk")
    nx = n // CORES
    dates = share * n
    half = share * nx
    pixel_count = pixels * n * rank
    date_count = dates * rank
    order = orders(n)
    work = pixels * dates * rank

    def moved(a, dx, dc):
        return (a // CORES + dx) % nx * CORES + (a % CORES + dc) % CORES

    def within(value, dx, dc):
        pairs = [(a, moved(a, dx, dc)) for a in range(n)]
        return lax.ppermute(value, "sub", pairs)

    def onward(value, dx):
        pairs = [
            (b * n + a, (b + 1) % blocks * n + moved(a, dx, 0))
            for b in range(blocks) for a in range(n)
        ]
        return lax.ppermute(value, ("blk", "sub"), pairs)

    def chips(value):
        return [value] + [within(value, dx, 0) for dx in range(1, nx)]

    strip_shapes = [shape(pixels, rank)] + [shape(pixels, rank, BF16)] * 2
    strip_shapes += [shape(rank, pixels, BF16)] * 2
    part_shapes = [shape(half, rank)] + [shape(half, pixels, BF16)] * 2

    def prepared(stratum, *args):
        kinds = [F32, jnp.int32, F32][: len(args)]
        outs = [shape(dates, pixels)] * 2
        if len(args) == 3:
            outs += strip_shapes
        scratch = [pltpu.VMEM((pixels, args[0].shape[2]), kind) for kind in kinds]
        scratch.append(pltpu.SemaphoreType.DMA((len(chunks_of(pixels)), len(args))))
        return call(
            functools.partial(prepare_kernel, stratum, share), outs, *args,
            where=HBM, scratch=scratch,
        )

    shares = [date_factors]
    shares += [within(date_factors, *step) for step in order[1:]]
    old = onward(date_factors, 0)
    values, weights, strip, *halves = prepared(0, readings, coverage, pixel_factors)
    values_1, weights_1 = prepared(1, readings, coverage)
    problem = (values, weights, halves[2], halves[3], halves[0], halves[1])
    send, h0, l0, b0, b1 = call(
        functools.partial(first_send_kernel, order),
        part_shapes + [shape(half, rank)] * 2, *shares, *problem, flops=6 * work,
    )
    got = within(send, 0, 1)
    keep, h1, l1 = call(first_keep_kernel, part_shapes, b1, *problem, flops=6 * work)
    mine = keep + got
    came = [onward(mine, dx) for dx in range(nx)]
    grad, message = call(
        first_gradient_kernel, [shape(pixels, rank), shape(share + 8, rank)],
        strip, old, h0, l0, h1, l1, b0, b1, flops=6 * work,
    )
    messages = chips(message)
    own_message, = call(join_kernel, [shape(half + 8, rank)], *messages)
    other_message = within(own_message, 0, 1)
    strip, *halves = call(
        functools.partial(first_step_kernel, pixel_count), strip_shapes,
        own_message, other_message, strip, grad,
    )
    own_grad = sum(came[1:], came[0])
    other_grad = within(own_grad, 0, 1)

    problem = (values_1, weights_1, halves[2], halves[3], halves[0], halves[1])
    send, h0, l0, b0 = call(
        functools.partial(later_send_kernel, date_count),
        part_shapes + [shape(half, rank)],
        own_grad, other_grad, other_message, *problem, flops=6 * work,
    )
    got = within(send, 0, 1)
    keep, h1, l1, b1, own = call(
        functools.partial(later_keep_kernel, date_count, share),
        part_shapes + [shape(half, rank), shape(share, rank)],
        own_grad, other_grad, own_message, *problem, flops=6 * work,
    )
    mine = keep + got
    came = [onward(mine, dx) for dx in range(nx)]
    held = onward(own, 0)
    grad, tile = call(
        later_gradient_kernel, [shape(pixels, rank), shape(8, 128)],
        strip, h0, l0, h1, l1, b0, b1, flops=6 * work,
    )
    tiles = chips(tile)
    tile = sum(tiles[1:], tiles[0])
    strip, = call(
        functools.partial(step_kernel, pixel_count), [shape(pixels, rank)],
        strip, grad, tile, within(tile, 0, 1),
    )
    date_grad, tile = call(
        functools.partial(last_gradient_kernel, share),
        [shape(share, rank), shape(8, 128)], *came,
        scratch=[pltpu.VMEM((half, rank), F32)],
    )
    date_out, = call(
        functools.partial(step_kernel, date_count), [shape(share, rank)],
        held, date_grad, tile, within(tile, 0, 1),
    )
    return strip, date_out


def solution(mesh):
    spec = P(("parts", "blk", "sub"), None)
    stacked = P(None, ("parts", "blk", "sub"), None)

    return jax.shard_map(
        on_device, mesh=mesh, in_specs=(stacked, stacked, spec, spec),
        out_specs=(spec, spec), check_vma=False,
    )
```

time: 47.3 us -> 41.5 us (0.88)
  waiting for transfers between devices: 17.3 us -> 11.8 us
  starting transfers between devices: 17.4 us -> 16.3 us
  Pallas kernels: 7.53 us -> 8.21 us
    ppermute x7 -> x6, waiting for transfers between devices: 13.1 us -> 3.86 us  [onward(): return lax.ppermute(value, ('blk', 'sub'), pairs)]
    ppermute x16 -> x11, waiting for transfers between devices: 4.18 us -> 7.98 us  [within(): return lax.ppermute(value, 'sub', pairs)]
    ppermute x16 -> x11, starting transfers between devices: 8.83 us -> 6.97 us  [within(): return lax.ppermute(value, 'sub', pairs)]
    ppermute x7 -> x6, starting transfers between devices: 8.61 us -> 9.37 us  [onward(): return lax.ppermute(value, ('blk', 'sub'), pairs)]
    pallas_call x10 -> x13, Pallas kernels: 7.53 us -> 8.21 us  [call(): pl.pallas_call(kernel, out_shape=outs, in_specs=[where] * len(args), out_...]
  transfers between devices with their start and end apart: 23 -> 17, of which waited for: 9 -> 5; matrix products, arithmetic and copies ran while one was open for 0% -> 0% of each run, Pallas kernels for 10% -> 15%
where the time goes in v3:
time: 41.5 us; the launch traced here: 41.3 us
  starting transfers between devices  16.3 us (39%)
  waiting for transfers between devices  11.8 us (28%)
  Pallas kernels  8.21 us (20%)
  local copies, waits for them, and re-layouts  3.96 us (10%)
  between operations  0.84 us (2%)
    ppermute x6, starting transfers between devices, onward(): return lax.ppermute(value, ('blk', 'sub'), pairs)  9.37 us
    pallas_call x13, Pallas kernels, call(): pl.pallas_call(kernel, out_shape=outs, in_specs=[where] * len(args), out_...  8.21 us
    ppermute x11, waiting for transfers between devices, within(): return lax.ppermute(value, 'sub', pairs)  7.98 us
    ppermute x11, starting transfers between devices, within(): return lax.ppermute(value, 'sub', pairs)  6.97 us
    unnamed x12, local copies, waits for them, and re-layouts  3.96 us
    ppermute x6, waiting for transfers between devices, onward(): return lax.ppermute(value, ('blk', 'sub'), pairs)  3.86 us
  transfers between devices with their start and end apart: 17, of which 5 were waited for; matrix products, arithmetic and copies ran while one was open for 0% of the time, Pallas kernels for 15%

profile of v3, /device:TPU:0, one launch (start us, length us, event | category | flops | bytes accessed | tf_op | source)
XLA Modules:
  0.0 41.3 jit_solution(592917705751844711)
XLA Ops:
  0.6 0.6 %collective-permute-start.1 = (f32[64,256]{1,0:T(8,128)}, f32[64,256]{1,0:T(8,128)S(1)}, u32[]{:S(2)}, u32[]{:S(2)}) collective-permute-start(f32[64,256]{1,0:T(8,128)} %refs_0_.4), channel_id=1, source_target_pairs={{0,1},{1,0},{2,3},{3,2},{4,5},{5,4},{6,7},{7,6},{8,9},{9,8},{10,11... | collective-permute-start | bytes 196616 | tf_op jit(solution)/shard_map/ppermute | solution.py:273
  1.2 2.6 %collective-permute-start.2 = (f32[64,256]{1,0:T(8,128)}, f32[64,256]{1,0:T(8,128)S(1)}, u32[]{:S(2)}, u32[]{:S(2)}) collective-permute-start(f32[64,256]{1,0:T(8,128)} %refs_0_.4), channel_id=1, source_target_pairs={{0,2},{1,3},{2,0},{3,1},{4,6},{5,7},{6,4},{7,5},{8,10},{9,11},{10,... | collective-permute-start | bytes 196616 | tf_op jit(solution)/shard_map/ppermute | solution.py:273
  3.8 1.4 %copy-done = f32[2,768,256]{2,1,0:T(8,128)S(1)} copy-done((f32[2,768,256]{2,1,0:T(8,128)S(1)}, f32[2,768,256]{2,1,0:T(8,128)}, u32[]{:S(2)}) %copy-start) | copy-done | bytes 1572888
  5.2 1.4 %copy-done.2 = s32[2,768,256]{2,1,0:T(8,128)S(1)} copy-done((s32[2,768,256]{2,1,0:T(8,128)S(1)}, s32[2,768,256]{2,1,0:T(8,128)}, u32[]{:S(2)}) %copy-start.2) | copy-done | bytes 1572888
  6.6 1.1 %copy-done.4 = f32[768,256]{1,0:T(8,128)S(1)} copy-done((f32[768,256]{1,0:T(8,128)S(1)}, f32[768,256]{1,0:T(8,128)}, u32[]{:S(2)}) %copy-start.4) | copy-done | bytes 786456
  7.7 1.1 %shard_map.59 = (f32[256,768]{1,0:T(8,128)S(1)}, f32[256,768]{1,0:T(8,128)S(1)}, f32[768,256]{1,0:T(8,128)S(1)}, bf16[768,256]{1,0:T(8,128)(2,1)S(1)}, bf16[768,...) custom-call(f32[2,768,256]{2,1,0:T(8,128)S(1)} %copy-done, ...), custom_call_target="tpu_custom_call" | custom-call | bytes 7864320 | tf_op jit(solution)/shard_map/pallas_call | solution.py:61
  8.9 0.7 %shard_map.60 = (f32[128,256]{1,0:T(8,128)S(1)}, bf16[128,768]{1,0:T(8,128)(2,1)S(1)}, bf16[128,768]{1,0:T(8,128)(2,1)S(1)}, f32[128,256]{1,0:T(8,128)S(1)}, f32[128,256]{1,0:T(8,128)S(1)}) custom-call(f32[64,256]{1,0:T(8,128)S(1)} %copy-done.5, f32[64,256]{1,0:T(8,128)S(1)} %collective-permute-done.1.refs_1_, f32[64,256]{1,0:T(8,128)S(1)} %collective-permute-done.2.refs_2_, ...), custom_call_target="tpu_custom_call" | custom-call | flops 301989888 | bytes 4194304 | tf_op jit(solution)/shard_map/pallas_call | solution.py:61
  9.8 2.0 %collective-permute-start = (f32[64,256]{1,0:T(8,128)S(1)}, f32[64,256]{1,0:T(8,128)S(1)}, u32[]{:S(2)}, u32[]{:S(2)}) collective-permute-start(f32[64,256]{1,0:T(8,128)S(1)} %copy-done.5), channel_id=1, source_target_pairs={{0,4},{1,5},{2,6},{3,7},{4,8},{5,9},{6,10},{7,11},{8,12},{9,13},{1... | collective-permute-start | bytes 196616 | tf_op jit(solution)/shard_map/ppermute | solution.py:280
  11.8 0.6 %shard_map.61 = (f32[128,256]{1,0:T(8,128)S(1)}, bf16[128,768]{1,0:T(8,128)(2,1)S(1)}, bf16[128,768]{1,0:T(8,128)(2,1)S(1)}) custom-call(f32[128,256]{1,0:T(8,128)S(1)} %get-tuple-element.48.block_ref.b1, f32[256,768]{1,0:T(8,128)S(1)} %get-tuple-element.40.refs_4_.refs_0_, f32[256,768]{1,0:T(8,128)S(1)} %get-tuple-element.41.refs_5_.refs_1_, ...), custom_call_target="tpu_custom_call" | custom-call | flops 301989888 | bytes 3801088 | tf_op jit(solution)/shard_map/pallas_call | solution.py:61
  12.5 1.6 %collective-permute-start.7 = (f32[128,256]{1,0:T(8,128)S(1)}, f32[128,256]{1,0:T(8,128)S(1)}, u32[]{:S(2)}, u32[]{:S(2)}) collective-permute-start(f32[128,256]{1,0:T(8,128)S(1)} %add.12), channel_id=1, source_target_pairs={{0,4},{1,5},{2,6},{3,7},{4,8},{5,9},{6,10},{7,11},{8,12},{9,13},{1... | collective-permute-start | bytes 393224 | tf_op jit(solution)/shard_map/ppermute | solution.py:280
  14.1 2.5 %collective-permute-start.8 = (f32[128,256]{1,0:T(8,128)S(1)}, f32[128,256]{1,0:T(8,128)S(1)}, u32[]{:S(2)}, u32[]{:S(2)}) collective-permute-start(f32[128,256]{1,0:T(8,128)S(1)} %add.12), channel_id=1, source_target_pairs={{0,6},{1,7},{2,4},{3,5},{4,10},{5,11},{6,8},{7,9},{8,14},{9,15},{1... | collective-permute-start | bytes 393224 | tf_op jit(solution)/shard_map/ppermute | solution.py:280
  17.2 1.2 %collective-permute-start.4 = (f32[72,256]{1,0:T(8,128)S(1)}, f32[72,256]{1,0:T(8,128)S(1)}, u32[]{:S(2)}, u32[]{:S(2)}) collective-permute-start(f32[72,256]{1,0:T(8,128)S(1)} %get-tuple-element.52.refs_0_), channel_id=1, source_target_pairs={{0,2},{1,3},{2,0},{3,1},{4,6},{5,7},{6,4},{7,5},{8,10},{9,11},{10,... | collective-permute-start | bytes 221192 | tf_op jit(solution)/shard_map/ppermute | solution.py:273
  18.4 5.3 %collective-permute-done.4.refs_1_ = f32[72,256]{1,0:T(8,128)S(1)} collective-permute-done((f32[72,256]{1,0:T(8,128)S(1)}, f32[72,256]{1,0:T(8,128)S(1)}, u32[]{:S(2)}, u32[]{:S(2)}) %collective-permute-start.4) | collective-permute-done | bytes 73760 | tf_op jit(solution)/shard_map/ppermute | solution.py:273
  24.4 0.8 %shard_map.65 = (f32[256,768]{1,0:T(8,128)S(1)}, f32[256,768]{1,0:T(8,128)S(1)}) custom-call(f32[2,768,256]{2,1,0:T(8,128)S(1)} %copy-done.1, s32[2,768,256]{2,1,0:T(8,128)S(1)} %copy-done.3), custom_call_target="tpu_custom_call" | custom-call | bytes 4718592 | tf_op jit(solution)/shard_map/pallas_call | solution.py:61
  25.7 0.8 %shard_map.66 = (f32[128,256]{1,0:T(8,128)S(1)}, bf16[128,768]{1,0:T(8,128)(2,1)S(1)}, bf16[128,768]{1,0:T(8,128)(2,1)S(1)}, f32[128,256]{1,0:T(8,128)S(1)}) custom-call(f32[128,256]{1,0:T(8,128)S(1)} %add.13.own_ref, f32[128,256]{1,0:T(8,128)S(1)} %collective-permute-done.9.other_ref, f32[136,256]{1,0:T(8,128)S(1)} %collective-permute-done.5.other_ref.message_ref, ...), custom_call_target="tpu_custom_call" | custom-call | flops 301989888 | bytes 4202496 | tf_op jit(solution)/shard_map/pallas_call | solution.py:61
  26.6 0.8 %shard_map.67 = (f32[128,256]{1,0:T(8,128)S(1)}, bf16[128,768]{1,0:T(8,128)(2,1)S(1)}, bf16[128,768]{1,0:T(8,128)(2,1)S(1)}, f32[128,256]{1,0:T(8,128)S(1)}, f32[64,256]{1,0:T(8,128)S(1)}) custom-call(f32[128,256]{1,0:T(8,128)S(1)} %add.13.own_ref, f32[128,256]{1,0:T(8,128)S(1)} %collective-permute-done.9.other_ref, ...), custom_call_target="tpu_custom_call" | custom-call | flops 301989888 | bytes 4268032 | tf_op jit(solution)/shard_map/pallas_call | solution.py:61
  28.2 1.4 %collective-permute-start.15 = (f32[128,256]{1,0:T(8,128)S(1)}, f32[128,256]{1,0:T(8,128)S(1)}, u32[]{:S(2)}, u32[]{:S(2)}) collective-permute-start(f32[128,256]{1,0:T(8,128)S(1)} %add.15), channel_id=1, source_target_pairs={{0,6},{1,7},{2,4},{3,5},{4,10},{5,11},{6,8},{7,9},{8,14},{9,15},{1... | collective-permute-start | bytes 393224 | tf_op jit(solution)/shard_map/ppermute | solution.py:280
  29.6 1.5 %collective-permute-start.12 = (f32[64,256]{1,0:T(8,128)S(1)}, f32[64,256]{1,0:T(8,128)S(1)}, u32[]{:S(2)}, u32[]{:S(2)}) collective-permute-start(f32[64,256]{1,0:T(8,128)S(1)} %get-tuple-element.71), channel_id=1, source_target_pairs={{0,4},{1,5},{2,6},{3,7},{4,8},{5,9},{6,10},{7,11},{8,12},{9,13},{1... | collective-permute-start | bytes 196616 | tf_op jit(solution)/shard_map/ppermute | solution.py:280
  31.6 1.6 %collective-permute-start.10 = (f32[8,128]{1,0:T(8,128)S(1)}, f32[8,128]{1,0:T(8,128)S(1)}, u32[]{:S(2)}, u32[]{:S(2)}) collective-permute-start(f32[8,128]{1,0:T(8,128)S(1)} %get-tuple-element.70), channel_id=1, source_target_pairs={{0,2},{1,3},{2,0},{3,1},{4,6},{5,7},{6,4},{7,5},{8,10},{9,11},{10,... | collective-permute-start | bytes 12296 | tf_op jit(solution)/shard_map/ppermute | solution.py:273
  33.2 2.2 %collective-permute-done.10 = f32[8,128]{1,0:T(8,128)S(1)} collective-permute-done((f32[8,128]{1,0:T(8,128)S(1)}, f32[8,128]{1,0:T(8,128)S(1)}, u32[]{:S(2)}, u32[]{:S(2)}) %collective-permute-start.10) | collective-permute-done | bytes 4128 | tf_op jit(solution)/shard_map/ppermute | solution.py:273
  35.3 0.8 %collective-permute-done.14.refs_0_ = f32[128,256]{1,0:T(8,128)S(1)} collective-permute-done((f32[128,256]{1,0:T(8,128)S(1)}, f32[128,256]{1,0:T(8,128)S(1)}, u32[]{:S(2)}, u32[]{:S(2)}) %collective-permute-start.14) | collective-permute-done | bytes 131104 | tf_op jit(solution)/shard_map/ppermute | solution.py:280
  36.1 3.1 %collective-permute-done.15.refs_1_ = f32[128,256]{1,0:T(8,128)S(1)} collective-permute-done((f32[128,256]{1,0:T(8,128)S(1)}, f32[128,256]{1,0:T(8,128)S(1)}, u32[]{:S(2)}, u32[]{:S(2)}) %collective-permute-start.15) | collective-permute-done | bytes 131104 | tf_op jit(solution)/shard_map/ppermute | solution.py:280
  39.3 1.2 %shard_map.69 = f32[768,256]{1,0:T(8,128)} custom-call(f32[768,256]{1,0:T(8,128)S(1)} %get-tuple-element.54.strip_ref.held_ref, f32[768,256]{1,0:T(8,128)S(1)} %get-tuple-element.69.grad_ref, f32[8,128]{1,0:T(8,128)S(1)} %add.14.refs_0_, f32[8,128]{1,0:T(8,128)S(1)} %collective-permute-done.11.refs_1_), custom_call_target="tpu_custom_call" | custom-call | bytes 2367488 | tf_op jit(solution)/shard_map/pallas_call | solution.py:61
  40.5 0.8 %shard_map.71 = f32[64,256]{1,0:T(8,128)} custom-call(f32[64,256]{1,0:T(8,128)S(1)} %collective-permute-done.12.held_ref, f32[64,256]{1,0:T(8,128)S(1)} %get-tuple-element.74.grad_ref, f32[8,128]{1,0:T(8,128)S(1)} %get-tuple-element.75.refs_0_, f32[8,128]{1,0:T(8,128)S(1)} %collective-permute-done.16.refs_1_), custom_call_target="tpu_custom_call" | custom-call | bytes 204800 | tf_op jit(solution)/shard_map/pallas_call | solution.py:61
  (39 shorter events, 3.5 us)
Async XLA Ops:
  0.6 8.2 %collective-permute-start.1 = (f32[64,256]{1,0:T(8,128)}, f32[64,256]{1,0:T(8,128)S(1)}, u32[]{:S(2)}, u32[]{:S(2)}) collective-permute-start(f32[64,256]{1,0:T(8,128)} %refs_0_.4), channel_id=1, source_target_pairs={{0,1},{1,0},{2,3},{3,2},{4,5},{5,4},{6,7},{7,6},{8,9},{9,8},{10,11... | collective-permute-start | bytes 196616 | tf_op jit(solution)/shard_map/ppermute | solution.py:273
  1.2 7.7 %collective-permute-start.2 = (f32[64,256]{1,0:T(8,128)}, f32[64,256]{1,0:T(8,128)S(1)}, u32[]{:S(2)}, u32[]{:S(2)}) collective-permute-start(f32[64,256]{1,0:T(8,128)} %refs_0_.4), channel_id=1, source_target_pairs={{0,2},{1,3},{2,0},{3,1},{4,6},{5,7},{6,4},{7,5},{8,10},{9,11},{10,... | collective-permute-start | bytes 196616 | tf_op jit(solution)/shard_map/ppermute | solution.py:273
  3.7 5.1 %collective-permute-start.3 = (f32[64,256]{1,0:T(8,128)}, f32[64,256]{1,0:T(8,128)S(1)}, u32[]{:S(2)}, u32[]{:S(2)}) collective-permute-start(f32[64,256]{1,0:T(8,128)} %refs_0_.4), channel_id=1, source_target_pairs={{0,3},{1,2},{2,1},{3,0},{4,7},{5,6},{6,5},{7,4},{8,11},{9,10},{10,... | collective-permute-start | bytes 196616 | tf_op jit(solution)/shard_map/ppermute | solution.py:273
  3.8 1.4 %copy-start = (f32[2,768,256]{2,1,0:T(8,128)S(1)}, f32[2,768,256]{2,1,0:T(8,128)}, u32[]{:S(2)}) copy-start(f32[2,768,256]{2,1,0:T(8,128)} %refs_0_.5) | copy-start | bytes 4718596
  5.2 1.4 %copy-start.2 = (s32[2,768,256]{2,1,0:T(8,128)S(1)}, s32[2,768,256]{2,1,0:T(8,128)}, u32[]{:S(2)}) copy-start(s32[2,768,256]{2,1,0:T(8,128)} %refs_1_.3) | copy-start | bytes 4718596
  6.6 1.1 %copy-start.4 = (f32[768,256]{1,0:T(8,128)S(1)}, f32[768,256]{1,0:T(8,128)}, u32[]{:S(2)}) copy-start(f32[768,256]{1,0:T(8,128)} %refs_2_.1) | copy-start | bytes 2359300
  7.7 1.1 %copy-start.5 = (f32[64,256]{1,0:T(8,128)S(1)}, f32[64,256]{1,0:T(8,128)}, u32[]{:S(2)}) copy-start(f32[64,256]{1,0:T(8,128)} %refs_0_.4) | copy-start | bytes 196612
  9.5 2.9 %collective-permute-start.6 = (f32[128,256]{1,0:T(8,128)S(1)}, f32[128,256]{1,0:T(8,128)S(1)}, u32[]{:S(2)}, u32[]{:S(2)}) collective-permute-start(f32[128,256]{1,0:T(8,128)S(1)} %get-tuple-element.56), channel_id=1, source_target_pairs={{0,1},{1,0},{2,3},{3,2},{4,5},{5,4},{6,7},{7,6},{8,9},{9,8},{10,11... | collective-permute-start | bytes 393224 | tf_op jit(solution)/shard_map/ppermute | solution.py:273
  9.8 6.9 %collective-permute-start = (f32[64,256]{1,0:T(8,128)S(1)}, f32[64,256]{1,0:T(8,128)S(1)}, u32[]{:S(2)}, u32[]{:S(2)}) collective-permute-start(f32[64,256]{1,0:T(8,128)S(1)} %copy-done.5), channel_id=1, source_target_pairs={{0,4},{1,5},{2,6},{3,7},{4,8},{5,9},{6,10},{7,11},{8,12},{9,13},{1... | collective-permute-start | bytes 196616 | tf_op jit(solution)/shard_map/ppermute | solution.py:280
  11.8 12.6 %copy-start.3 = (s32[2,768,256]{2,1,0:T(8,128)S(1)}, s32[2,768,256]{2,1,0:T(8,128)}, u32[]{:S(2)}) copy-start(s32[2,768,256]{2,1,0:T(8,128)} %refs_1_.3) | copy-start | bytes 4718596
  12.4 12.0 %copy-start.1 = (f32[2,768,256]{2,1,0:T(8,128)S(1)}, f32[2,768,256]{2,1,0:T(8,128)}, u32[]{:S(2)}) copy-start(f32[2,768,256]{2,1,0:T(8,128)} %refs_0_.5) | copy-start | bytes 4718596
  12.5 11.3 %collective-permute-start.7 = (f32[128,256]{1,0:T(8,128)S(1)}, f32[128,256]{1,0:T(8,128)S(1)}, u32[]{:S(2)}, u32[]{:S(2)}) collective-permute-start(f32[128,256]{1,0:T(8,128)S(1)} %add.12), channel_id=1, source_target_pairs={{0,4},{1,5},{2,6},{3,7},{4,8},{5,9},{6,10},{7,11},{8,12},{9,13},{1... | collective-permute-start | bytes 393224 | tf_op jit(solution)/shard_map/ppermute | solution.py:280
  14.1 9.7 %collective-permute-start.8 = (f32[128,256]{1,0:T(8,128)S(1)}, f32[128,256]{1,0:T(8,128)S(1)}, u32[]{:S(2)}, u32[]{:S(2)}) collective-permute-start(f32[128,256]{1,0:T(8,128)S(1)} %add.12), channel_id=1, source_target_pairs={{0,6},{1,7},{2,4},{3,5},{4,10},{5,11},{6,8},{7,9},{8,14},{9,15},{1... | collective-permute-start | bytes 393224 | tf_op jit(solution)/shard_map/ppermute | solution.py:280
  17.2 6.6 %collective-permute-start.4 = (f32[72,256]{1,0:T(8,128)S(1)}, f32[72,256]{1,0:T(8,128)S(1)}, u32[]{:S(2)}, u32[]{:S(2)}) collective-permute-start(f32[72,256]{1,0:T(8,128)S(1)} %get-tuple-element.52.refs_0_), channel_id=1, source_target_pairs={{0,2},{1,3},{2,0},{3,1},{4,6},{5,7},{6,4},{7,5},{8,10},{9,11},{10,... | collective-permute-start | bytes 221192 | tf_op jit(solution)/shard_map/ppermute | solution.py:273
  23.7 1.5 %collective-permute-start.5 = (f32[136,256]{1,0:T(8,128)S(1)}, f32[136,256]{1,0:T(8,128)S(1)}, u32[]{:S(2)}, u32[]{:S(2)}) collective-permute-start(f32[136,256]{1,0:T(8,128)S(1)} %shard_map.63.own_ref.message_ref), channel_id=1, source_target_pairs={{0,1},{1,0},{2,3},{3,2},{4,5},{5,4},{6,7},{7,6},{8,9},{9,8},{10,11... | collective-permute-start | bytes 417800 | tf_op jit(solution)/shard_map/ppermute | solution.py:273
  23.9 1.8 %collective-permute-start.9 = (f32[128,256]{1,0:T(8,128)S(1)}, f32[128,256]{1,0:T(8,128)S(1)}, u32[]{:S(2)}, u32[]{:S(2)}) collective-permute-start(f32[128,256]{1,0:T(8,128)S(1)} %add.13.own_ref), channel_id=1, source_target_pairs={{0,1},{1,0},{2,3},{3,2},{4,5},{5,4},{6,7},{7,6},{8,9},{9,8},{10,11... | collective-permute-start | bytes 393224 | tf_op jit(solution)/shard_map/ppermute | solution.py:273
  26.5 1.4 %collective-permute-start.13 = (f32[128,256]{1,0:T(8,128)S(1)}, f32[128,256]{1,0:T(8,128)S(1)}, u32[]{:S(2)}, u32[]{:S(2)}) collective-permute-start(f32[128,256]{1,0:T(8,128)S(1)} %get-tuple-element.73), channel_id=1, source_target_pairs={{0,1},{1,0},{2,3},{3,2},{4,5},{5,4},{6,7},{7,6},{8,9},{9,8},{10,11... | collective-permute-start | bytes 393224 | tf_op jit(solution)/shard_map/ppermute | solution.py:273
  27.9 8.2 %collective-permute-start.14 = (f32[128,256]{1,0:T(8,128)S(1)}, f32[128,256]{1,0:T(8,128)S(1)}, u32[]{:S(2)}, u32[]{:S(2)}) collective-permute-start(f32[128,256]{1,0:T(8,128)S(1)} %add.15), channel_id=1, source_target_pairs={{0,4},{1,5},{2,6},{3,7},{4,8},{5,9},{6,10},{7,11},{8,12},{9,13},{1... | collective-permute-start | bytes 393224 | tf_op jit(solution)/shard_map/ppermute | solution.py:280
  28.2 11.0 %collective-permute-start.15 = (f32[128,256]{1,0:T(8,128)S(1)}, f32[128,256]{1,0:T(8,128)S(1)}, u32[]{:S(2)}, u32[]{:S(2)}) collective-permute-start(f32[128,256]{1,0:T(8,128)S(1)} %add.15), channel_id=1, source_target_pairs={{0,6},{1,7},{2,4},{3,5},{4,10},{5,11},{6,8},{7,9},{8,14},{9,15},{1... | collective-permute-start | bytes 393224 | tf_op jit(solution)/shard_map/ppermute | solution.py:280
  29.6 10.9 %collective-permute-start.12 = (f32[64,256]{1,0:T(8,128)S(1)}, f32[64,256]{1,0:T(8,128)S(1)}, u32[]{:S(2)}, u32[]{:S(2)}) collective-permute-start(f32[64,256]{1,0:T(8,128)S(1)} %get-tuple-element.71), channel_id=1, source_target_pairs={{0,4},{1,5},{2,6},{3,7},{4,8},{5,9},{6,10},{7,11},{8,12},{9,13},{1... | collective-permute-start | bytes 196616 | tf_op jit(solution)/shard_map/ppermute | solution.py:280
  31.6 3.7 %collective-permute-start.10 = (f32[8,128]{1,0:T(8,128)S(1)}, f32[8,128]{1,0:T(8,128)S(1)}, u32[]{:S(2)}, u32[]{:S(2)}) collective-permute-start(f32[8,128]{1,0:T(8,128)S(1)} %get-tuple-element.70), channel_id=1, source_target_pairs={{0,2},{1,3},{2,0},{3,1},{4,6},{5,7},{6,4},{7,5},{8,10},{9,11},{10,... | collective-permute-start | bytes 12296 | tf_op jit(solution)/shard_map/ppermute | solution.py:273
  35.3 4.0 %collective-permute-start.11 = (f32[8,128]{1,0:T(8,128)S(1)}, f32[8,128]{1,0:T(8,128)S(1)}, u32[]{:S(2)}, u32[]{:S(2)}) collective-permute-start(f32[8,128]{1,0:T(8,128)S(1)} %add.14.refs_0_), channel_id=1, source_target_pairs={{0,1},{1,0},{2,3},{3,2},{4,5},{5,4},{6,7},{7,6},{8,9},{9,8},{10,11... | collective-permute-start | bytes 12296 | tf_op jit(solution)/shard_map/ppermute | solution.py:273
  39.2 1.2 %collective-permute-start.16 = (f32[8,128]{1,0:T(8,128)S(1)}, f32[8,128]{1,0:T(8,128)S(1)}, u32[]{:S(2)}, u32[]{:S(2)}) collective-permute-start(f32[8,128]{1,0:T(8,128)S(1)} %get-tuple-element.75.refs_0_), channel_id=1, source_target_pairs={{0,1},{1,0},{2,3},{3,2},{4,5},{5,4},{6,7},{7,6},{8,9},{9,8},{10,11... | collective-permute-start | bytes 12296 | tf_op jit(solution)/shard_map/ppermute | solution.py:273

commit v4 on v3

v4 whole, which is shorter than its diff:
```python
import functools

import jax
import jax.numpy as jnp
from jax import lax
from jax.experimental import pallas as pl
from jax.experimental.pallas import tpu as pltpu
from jax.sharding import PartitionSpec as P


step_size = 0.05
ridge = 0.1
epsilon = 1e-06

CORES = 2
CHUNK = 256
HIDDEN = 1e9
GRANT = 16 << 20
WIDE = 54_000_000
F32 = jnp.float32
BF16 = jnp.bfloat16

VMEM = pl.BlockSpec(memory_space=pltpu.VMEM)
HBM = pl.BlockSpec(memory_space=pltpu.HBM)

NT = (((1,), (1,)), ((), ()))
NN = (((1,), (0,)), ((), ()))
TN = (((0,), (0,)), ((), ()))


def split(value):
    high = value.astype(BF16)
    low = (value - high.astype(F32)).astype(BF16)
    return high, low


def product(a, b, dims):
    dot = functools.partial(
        lax.dot_general, dimension_numbers=dims, preferred_element_type=F32
    )
    (a_high, a_low), (b_high, b_low) = a, b
    return dot(a_high, b_high) + (dot(a_high, b_low) + dot(a_low, b_high))


def tile_squares(value):
    squares = value * value
    rows, columns = squares.shape
    folded = squares.reshape(rows // 8, 8, columns).sum(0)
    total = folded[:, :128]
    for start in range(128, columns, 128):
        total = total + folded[:, start : start + 128]
    return total


def step_of(tiles, count):
    total = tiles[0]
    for tile in tiles[1:]:
        total = total + tile
    mean = jnp.sum(total, axis=(0, 1), keepdims=True) / count
    return step_size / jnp.sqrt(mean + epsilon)


def call(kernel, outs, *args, where=VMEM, scratch=(), flops=0, grant=GRANT):
    size = sum(a.size * a.dtype.itemsize for a in list(args) + list(outs))
    return pl.pallas_call(
        kernel,
        out_shape=outs,
        in_specs=[where] * len(args),
        out_specs=[VMEM] * len(outs),
        scratch_shapes=list(scratch),
        compiler_params=pltpu.CompilerParams(vmem_limit_bytes=grant),
        cost_estimate=pl.CostEstimate(
            flops=flops, bytes_accessed=size, transcendentals=0
        ),
    )(*args)


def shape(rows, columns, dtype=F32):
    return jax.ShapeDtypeStruct((rows, columns), dtype)


def chunks_of(pixels):
    size = CHUNK if pixels % CHUNK == 0 else pixels
    return [pl.ds(start, size) for start in range(0, pixels, size)]


def place():
    at = lax.axis_index("sub")
    return at // CORES, lax.rem(at, CORES)


def aligned(index, size):
    return pl.ds(pl.multiple_of(index * size, size), size)


def prepare_kernel(stratum, share, *refs):
    with_strip = stratum == 0
    sources = refs[: 2 + with_strip]
    outs = refs[len(sources) : len(sources) + 1 + 3 * with_strip]
    buffers, sem = refs[len(sources) + len(outs) : -1], refs[-1]
    pixels, dates = buffers[0].shape
    nx = dates // share // CORES
    chunks = chunks_of(pixels)
    copies = []
    for at, chunk in enumerate(chunks):
        row = []
        for which, (source, buffer) in enumerate(zip(sources, buffers)):
            view = source.at[chunk] if which == 2 else source.at[stratum, chunk]
            copy = pltpu.make_async_copy(view, buffer.at[chunk], sem.at[at, which])
            copy.start()
            row.append(copy)
        copies.append(row)
    _, core = place()
    for chunk, row in zip(chunks, copies):
        for copy in row:
            copy.wait()
        seen = jnp.where(buffers[1][chunk, :] != 0, buffers[0][chunk, :], HIDDEN)
        turned = seen.T
        for at in range(nx * CORES):
            own = jnp.where(core == at % CORES, nx, 0)
            rows = aligned(own + at // CORES, share)
            outs[0][rows, chunk] = turned[at * share : (at + 1) * share]
        if with_strip:
            strip = buffers[2][chunk, :]
            outs[1][chunk, :] = strip
            outs[2][chunk, :], outs[3][chunk, :] = split(strip)


def errors_and_part(side, problem, block, high_ref, low_ref):
    values_ref, h_ref, l_ref = problem
    half = block.shape[0]
    rows = slice(side * half, (side + 1) * half)
    block = split(block)
    total = None
    for chunk in chunks_of(values_ref.shape[1]):
        strip = (h_ref[chunk, :], l_ref[chunk, :])
        values = values_ref[rows, chunk]
        errors = jnp.where(values < HIDDEN, values - product(block, strip, NT), 0.0)
        errors = split(errors)
        high_ref[:, chunk], low_ref[:, chunk] = errors
        part = product(errors, strip, NN)
        total = part if total is None else total + part
    return -total


def with_ridge(part, block):
    chip, _ = place()
    return part + jnp.where(chip == 0, ridge, 0.0) * block


def assemble(shares, block_ref):
    nx = len(shares)
    share = shares[0].shape[0]
    chip, _ = place()
    for dx, ref in enumerate(shares):
        block_ref[aligned(lax.rem(chip - dx + nx, nx), share), :] = ref[...]


def first_send_kernel(nx, *refs):
    problem, (send_ref, high_ref, low_ref, block_ref) = refs[nx : nx + 3], refs[nx + 3 :]
    assemble(refs[:nx], block_ref)
    send_ref[...] = errors_and_part(0, problem, block_ref[...], high_ref, low_ref)


def first_keep_kernel(nx, *refs):
    problem, (keep_ref, high_ref, low_ref, block_ref) = refs[nx : nx + 3], refs[nx + 3 :]
    assemble(refs[:nx], block_ref)
    block = block_ref[...]
    part = errors_and_part(1, problem, block, high_ref, low_ref)
    keep_ref[...] = with_ridge(part, block)


def later_step(count, own_ref, other_ref):
    return step_of([tile_squares(own_ref[...]), tile_squares(other_ref[...])], count)


def later_send_kernel(count, own_ref, other_ref, message_ref, *refs):
    problem, (send_ref, high_ref, low_ref, block_ref) = refs[:3], refs[3:]
    step = later_step(count, own_ref, other_ref)
    block = message_ref[: other_ref.shape[0], :] - step * other_ref[...]
    block_ref[...] = block
    send_ref[...] = errors_and_part(0, problem, block, high_ref, low_ref)


def later_keep_kernel(count, share, own_ref, other_ref, message_ref, *refs):
    problem, (keep_ref, high_ref, low_ref, block_ref, share_ref) = refs[:3], refs[3:]
    step = later_step(count, own_ref, other_ref)
    block = message_ref[: own_ref.shape[0], :] - step * own_ref[...]
    block_ref[...] = block
    chip, _ = place()
    share_ref[...] = block_ref[aligned(chip, share), :]
    part = errors_and_part(1, problem, block, high_ref, low_ref)
    keep_ref[...] = with_ridge(part, block)


def pixel_gradient(strip_ref, errors, blocks):
    joined = [jnp.concatenate([ref[...] for ref in part], 0) for part in errors]
    block = jnp.concatenate([ref[...] for ref in blocks], 0)
    return ridge * strip_ref[...] - product(joined, split(block), TN)


def gradient_kernel(strip_ref, h0, l0, h1, l1, b0, b1, grad_ref, tile_ref):
    grad = pixel_gradient(strip_ref, ((h0, h1), (l0, l1)), (b0, b1))
    grad_ref[...] = grad
    tile = tile_squares(grad)
    columns = tile_ref.shape[1]
    tile_ref[:, :128] = tile
    if columns > 128:
        tile_ref[:, 128:] = jnp.zeros((8, columns - 128), F32)


def join_kernel(*refs):
    messages, out_ref = refs[:-1], refs[-1]
    nx = len(messages)
    share = messages[0].shape[0] - 8
    chip, _ = place()
    total = None
    for dx, ref in enumerate(messages):
        out_ref[aligned(lax.rem(chip - dx + nx, nx), share), :] = ref[:share, :]
        tile = ref[share:, :]
        total = tile if total is None else total + tile
    out_ref[nx * share :, :] = total


def first_step_kernel(count, own_ref, other_ref, strip_ref, grad_ref, *outs):
    strip_out, h_ref, l_ref = outs
    half = own_ref.shape[0] - 8
    step = step_of([own_ref[half:, :128], other_ref[half:, :128]], count)
    strip = strip_ref[...] - step * grad_ref[...]
    strip_out[...] = strip
    h_ref[...], l_ref[...] = split(strip)


def step_kernel(count, held_ref, grad_ref, *refs):
    step = step_of([t[...] for t in refs[:-1]], count)
    refs[-1][...] = held_ref[...] - step * grad_ref[...]


def last_gradient_kernel(share, *refs):
    parts, (grad_ref, tile_ref), sum_ref = refs[:-3], refs[-3:-1], refs[-1]
    half = sum_ref.shape[0]
    total = parts[0][:half, :]
    for ref in parts[1:]:
        total = total + ref[...]
    sum_ref[...] = total
    tile_ref[...] = tile_squares(total)
    chip, _ = place()
    grad_ref[...] = sum_ref[aligned(chip, share), :]


def last_step_kernel(count, message_ref, grad_ref, own_ref, other_ref, out_ref):
    step = step_of([own_ref[...], other_ref[...]], count)
    held = message_ref[message_ref.shape[0] - grad_ref.shape[0] :, :]
    out_ref[...] = held - step * grad_ref[...]


def on_device(readings, coverage, pixel_factors, date_factors):
    pixels, rank = pixel_factors.shape
    share = date_factors.shape[0]
    n = lax.axis_size("sub")
    blocks = lax.axis_size("blk")
    nx = n // CORES
    dates = share * n
    half = share * nx
    pixel_count = pixels * n * rank
    date_count = dates * rank
    work = pixels * dates * rank

    def moved(a, dx, dc):
        return (a // CORES + dx) % nx * CORES + (a % CORES + dc) % CORES

    def within(value, dx, dc):
        pairs = [(a, moved(a, dx, dc)) for a in range(n)]
        return lax.ppermute(value, "sub", pairs)

    def onward(value, dx):
        pairs = [
            (b * n + a, (b + 1) % blocks * n + moved(a, dx, 0))
            for b in range(blocks) for a in range(n)
        ]
        return lax.ppermute(value, ("blk", "sub"), pairs)

    def chips(value):
        return [value] + [within(value, dx, 0) for dx in range(1, nx)]

    strip_shapes = [shape(pixels, rank)] + [shape(pixels, rank, BF16)] * 2
    part_shapes = [shape(half, rank)] + [shape(half, pixels, BF16)] * 2
    part_shapes += [shape(half, rank)]

    def prepared(stratum, grant, *args):
        kinds = [F32, jnp.int32, F32][: len(args)]
        outs = [shape(dates, pixels)]
        if len(args) == 3:
            outs += strip_shapes
        scratch = [pltpu.VMEM((pixels, args[0].shape[2]), kind) for kind in kinds]
        scratch.append(pltpu.SemaphoreType.DMA((len(chunks_of(pixels)), len(args))))
        return call(
            functools.partial(prepare_kernel, stratum, share), outs, *args,
            where=HBM, scratch=scratch, grant=grant,
        )

    others = [within(date_factors, dx, 1) for dx in range(nx)]
    owns = chips(date_factors)
    old = onward(date_factors, 0)
    values, strip, *halves = prepared(0, WIDE, readings, coverage, pixel_factors)
    values_1, = prepared(1, GRANT, readings, coverage)
    send, h0, l0, b0 = call(
        functools.partial(first_send_kernel, nx), part_shapes,
        *others, values, *halves, flops=6 * work,
    )
    got = within(send, 0, 1)
    keep, h1, l1, b1 = call(
        functools.partial(first_keep_kernel, nx), part_shapes,
        *owns, values, *halves, flops=6 * work,
    )
    mine = keep + got
    came = [onward(mine, dx) for dx in range(nx)]
    grad, tile = call(
        gradient_kernel, [shape(pixels, rank), shape(8, rank)],
        strip, h0, l0, h1, l1, b0, b1, flops=6 * work,
    )
    messages = chips(jnp.concatenate([old, tile], 0))
    own_message, = call(join_kernel, [shape(half + 8, rank)], *messages)
    other_message = within(own_message, 0, 1)
    strip, *halves = call(
        functools.partial(first_step_kernel, pixel_count), strip_shapes,
        own_message, other_message, strip, grad,
    )
    own_grad = sum(came[1:], came[0])
    other_grad = within(own_grad, 0, 1)

    send, h0, l0, b0 = call(
        functools.partial(later_send_kernel, date_count), part_shapes,
        own_grad, other_grad, other_message, values_1, *halves, flops=6 * work,
    )
    got = within(send, 0, 1)
    keep, h1, l1, b1, own = call(
        functools.partial(later_keep_kernel, date_count, share),
        part_shapes + [shape(share, rank)],
        own_grad, other_grad, own_message, values_1, *halves, flops=6 * work,
    )
    mine = keep + got
    came = [onward(jnp.concatenate([mine, own], 0), 0)]
    came += [onward(mine, dx) for dx in range(1, nx)]
    grad, tile = call(
        gradient_kernel, [shape(pixels, rank), shape(8, 128)],
        strip, h0, l0, h1, l1, b0, b1, flops=6 * work,
    )
    tiles = chips(tile)
    tile = sum(tiles[1:], tiles[0])
    other_tile = within(tile, 0, 1)
    strip, = call(
        functools.partial(step_kernel, pixel_count), [shape(pixels, rank)],
        strip, grad, tile, other_tile,
    )
    date_grad, tile = call(
        functools.partial(last_gradient_kernel, share),
        [shape(share, rank), shape(8, 128)], *came,
        scratch=[pltpu.VMEM((half, rank), F32)],
    )
    other_tile = within(tile, 0, 1)
    date_out, = call(
        functools.partial(last_step_kernel, date_count), [shape(share, rank)],
        came[0], date_grad, tile, other_tile,
    )
    return strip, date_out


def solution(mesh):
    spec = P(("parts", "blk", "sub"), None)
    stacked = P(None, ("parts", "blk", "sub"), None)

    return jax.shard_map(
        on_device, mesh=mesh, in_specs=(stacked, stacked, spec, spec),
        out_specs=(spec, spec), check_vma=False,
    )
```

time: 41.5 us -> 40 us (0.964)
  local copies, waits for them, and re-layouts: 3.96 us -> 0.03 us
  waiting for transfers between devices: 11.8 us -> 14.4 us
  starting transfers between devices: 16.3 us -> 14.2 us
  Pallas kernels: 8.21 us -> 10.2 us
    ppermute x6 -> x5, waiting for transfers between devices: 3.86 us -> 7.81 us  [onward(): return lax.ppermute(value, ('blk', 'sub'), pairs)]
    unnamed x12 -> x7, local copies, waits for them, and re-layouts: 3.96 us -> 0.03 us
    pallas_call x13, Pallas kernels: 8.21 us -> 10.2 us  [call(): pl.pallas_call(kernel, out_shape=outs, in_specs=[where] * len(args), out_...]
    ppermute x11, waiting for transfers between devices: 7.98 us -> 6.56 us  [within(): return lax.ppermute(value, 'sub', pairs)]
    ppermute x6 -> x5, starting transfers between devices: 9.37 us -> 8.31 us  [onward(): return lax.ppermute(value, ('blk', 'sub'), pairs)]
    ppermute x11, starting transfers between devices: 6.97 us -> 5.93 us  [within(): return lax.ppermute(value, 'sub', pairs)]
  transfers between devices with their start and end apart: 17 -> 16, of which waited for: 5 -> 5; matrix products, arithmetic and copies ran while one was open for 0% -> 0% of each run, Pallas kernels for 15% -> 21%
where the time goes in v4:
time: 40 us; the launch traced here: 39.8 us
  waiting for transfers between devices  14.4 us (36%)
  starting transfers between devices  14.2 us (36%)
  Pallas kernels  10.2 us (25%)
  between operations  0.9 us (2%)
    pallas_call x13, Pallas kernels, call(): pl.pallas_call(kernel, out_shape=outs, in_specs=[where] * len(args), out_...  10.2 us
    ppermute x5, starting transfers between devices, onward(): return lax.ppermute(value, ('blk', 'sub'), pairs)  8.31 us
    ppermute x5, waiting for transfers between devices, onward(): return lax.ppermute(value, ('blk', 'sub'), pairs)  7.81 us
    ppermute x11, waiting for transfers between devices, within(): return lax.ppermute(value, 'sub', pairs)  6.56 us
    ppermute x11, starting transfers between devices, within(): return lax.ppermute(value, 'sub', pairs)  5.93 us
  transfers between devices with their start and end apart: 16, of which 5 were waited for; matrix products, arithmetic and copies ran while one was open for 0% of the time, Pallas kernels for 21%

profile of v4, /device:TPU:0, one launch (start us, length us, event | category | flops | bytes accessed | tf_op | source)
XLA Modules:
  0.0 39.8 jit_solution(11072404845367158013)
XLA Ops:
  0.6 0.6 %collective-permute-start.1 = (f32[64,256]{1,0:T(8,128)}, f32[64,256]{1,0:T(8,128)S(1)}, u32[]{:S(2)}, u32[]{:S(2)}) collective-permute-start(f32[64,256]{1,0:T(8,128)} %refs_0_.4), channel_id=1, source_target_pairs={{0,1},{1,0},{2,3},{3,2},{4,5},{5,4},{6,7},{7,6},{8,9},{9,8},{10,11... | collective-permute-start | bytes 196616 | tf_op jit(solution)/shard_map/ppermute | solution.py:274
  1.2 2.6 %collective-permute-start.2 = (f32[64,256]{1,0:T(8,128)}, f32[64,256]{1,0:T(8,128)S(1)}, u32[]{:S(2)}, u32[]{:S(2)}) collective-permute-start(f32[64,256]{1,0:T(8,128)} %refs_0_.4), channel_id=1, source_target_pairs={{0,3},{1,2},{2,1},{3,0},{4,7},{5,6},{6,5},{7,4},{8,11},{9,10},{10,... | collective-permute-start | bytes 196616 | tf_op jit(solution)/shard_map/ppermute | solution.py:274
  3.8 2.1 %collective-permute-start = (f32[64,256]{1,0:T(8,128)}, f32[64,256]{1,0:T(8,128)S(1)}, u32[]{:S(2)}, u32[]{:S(2)}) collective-permute-start(f32[64,256]{1,0:T(8,128)} %refs_0_.4), channel_id=1, source_target_pairs={{0,4},{1,5},{2,6},{3,7},{4,8},{5,9},{6,10},{7,11},{8,12},{9,13},{1... | collective-permute-start | bytes 196616 | tf_op jit(solution)/shard_map/ppermute | solution.py:281
  5.9 1.9 %shard_map.59 = (f32[256,768]{1,0:T(8,128)S(1)}, f32[768,256]{1,0:T(8,128)S(1)}, bf16[768,256]{1,0:T(8,128)(2,1)S(1)}, bf16[768,256]{1,0:T(8,128)(2,1)S(1)}) custom-call(f32[2,768,256]{2,1,0:T(8,128)} %refs_0_.5, s32[2,768,256]{2,1,0:T(8,128)} %refs_1_.3, f32[768,256]{1,0:T(8,128)} %refs_2_.1), custom_call_target="tpu_custom_call" | custom-call | bytes 6291456 | tf_op jit(solution)/shard_map/pallas_call | solution.py:65
  7.8 1.0 %shard_map.60 = (f32[128,256]{1,0:T(8,128)S(1)}, bf16[128,768]{1,0:T(8,128)(2,1)S(1)}, bf16[128,768]{1,0:T(8,128)(2,1)S(1)}, f32[128,256]{1,0:T(8,128)S(1)}) custom-call(f32[64,256]{1,0:T(8,128)S(1)} %collective-permute-done.1.refs_0_, f32[64,256]{1,0:T(8,128)S(1)} %collective-permute-done.2.refs_1_, f32[256,768]{1,0:T(8,128)S(1)} %get-tuple-element.33.refs_2_, ...), custom_call_target="tpu_custom_call" | custom-call | flops 301989888 | bytes 2359296 | tf_op jit(solution)/shard_map/pallas_call | solution.py:65
  8.9 1.0 %shard_map.61 = (f32[128,256]{1,0:T(8,128)S(1)}, bf16[128,768]{1,0:T(8,128)(2,1)S(1)}, bf16[128,768]{1,0:T(8,128)(2,1)S(1)}, f32[128,256]{1,0:T(8,128)S(1)}) custom-call(f32[64,256]{1,0:T(8,128)S(1)} %copy-done.2, f32[64,256]{1,0:T(8,128)S(1)} %collective-permute-done.3.refs_1_, f32[256,768]{1,0:T(8,128)S(1)} %get-tuple-element.33.refs_2_, ...), custom_call_target="tpu_custom_call" | custom-call | flops 301989888 | bytes 2359296 | tf_op jit(solution)/shard_map/pallas_call | solution.py:65
  10.0 0.5 %shard_map.62 = (f32[768,256]{1,0:T(8,128)S(1)}, f32[8,256]{1,0:T(8,128)S(1)}) custom-call(f32[768,256]{1,0:T(8,128)S(1)} %get-tuple-element.32.strip_ref, bf16[128,768]{1,0:T(8,128)(2,1)S(1)} %get-tuple-element.36.h0, bf16[128,768]{1,0:T(8,128)(2,1)S(1)} %get-tuple-element.37.l0, bf16[128,768]{1,0:T(8,128)(2,1)S(1)} %get-tuple-element.38.h1, ...), custom_call_target="tpu_custom_call" | custom-call | flops 301989888 | bytes 2629632 | tf_op jit(solution)/shard_map/pallas_call | solution.py:65
  10.6 1.6 %collective-permute-start.7 = (f32[128,256]{1,0:T(8,128)S(1)}, f32[128,256]{1,0:T(8,128)S(1)}, u32[]{:S(2)}, u32[]{:S(2)}) collective-permute-start(f32[128,256]{1,0:T(8,128)S(1)} %add.12), channel_id=1, source_target_pairs={{0,4},{1,5},{2,6},{3,7},{4,8},{5,9},{6,10},{7,11},{8,12},{9,13},{1... | collective-permute-start | bytes 393224 | tf_op jit(solution)/shard_map/ppermute | solution.py:281
  12.2 2.5 %collective-permute-start.8 = (f32[128,256]{1,0:T(8,128)S(1)}, f32[128,256]{1,0:T(8,128)S(1)}, u32[]{:S(2)}, u32[]{:S(2)}) collective-permute-start(f32[128,256]{1,0:T(8,128)S(1)} %add.12), channel_id=1, source_target_pairs={{0,6},{1,7},{2,4},{3,5},{4,10},{5,11},{6,8},{7,9},{8,14},{9,15},{1... | collective-permute-start | bytes 393224 | tf_op jit(solution)/shard_map/ppermute | solution.py:281
  14.7 0.5 %collective-permute-start.4 = (f32[72,256]{1,0:T(8,128)S(1)}, f32[72,256]{1,0:T(8,128)S(1)}, u32[]{:S(2)}, u32[]{:S(2)}) collective-permute-start(f32[72,256]{1,0:T(8,128)S(1)} %constant_dynamic-update-slice_fusion.refs_0_), channel_id=1, source_target_pairs={{0,2},{1,3},{2,0},{3,1},{4,6},{5,7},{6,4},{7,5},{8,10},{9,11},{10,... | collective-permute-start | bytes 221192 | tf_op jit(solution)/shard_map/ppermute | solution.py:274
  15.2 4.2 %collective-permute-done.4.refs_1_ = f32[72,256]{1,0:T(8,128)S(1)} collective-permute-done((f32[72,256]{1,0:T(8,128)S(1)}, f32[72,256]{1,0:T(8,128)S(1)}, u32[]{:S(2)}, u32[]{:S(2)}) %collective-permute-start.4) | collective-permute-done | bytes 73760 | tf_op jit(solution)/shard_map/ppermute | solution.py:274
  19.6 2.4 %collective-permute-done.8 = f32[128,256]{1,0:T(8,128)S(1)} collective-permute-done((f32[128,256]{1,0:T(8,128)S(1)}, f32[128,256]{1,0:T(8,128)S(1)}, u32[]{:S(2)}, u32[]{:S(2)}) %collective-permute-start.8) | collective-permute-done | bytes 131104 | tf_op jit(solution)/shard_map/ppermute | solution.py:281
  22.1 0.6 %shard_map.65.refs_0_ = f32[256,768]{1,0:T(8,128)S(1)} custom-call(f32[2,768,256]{2,1,0:T(8,128)S(1)} %copy-done, s32[2,768,256]{2,1,0:T(8,128)S(1)} %copy-done.1), custom_call_target="tpu_custom_call" | custom-call | bytes 3932160 | tf_op jit(solution)/shard_map/pallas_call | solution.py:65
  22.7 0.5 %shard_map.64 = (f32[768,256]{1,0:T(8,128)S(1)}, bf16[768,256]{1,0:T(8,128)(2,1)S(1)}, bf16[768,256]{1,0:T(8,128)(2,1)S(1)}) custom-call(f32[136,256]{1,0:T(8,128)S(1)} %shard_map.63.own_ref.message_ref, f32[136,256]{1,0:T(8,128)S(1)} %collective-permute-done.5.other_ref.message_ref, f32[768,256]{1,0:T(8,128)S(1)} %get-tuple-element.32.strip_ref, ...), custom_call_target="tpu_custom_call" | custom-call | bytes 3424256 | tf_op jit(solution)/shard_map/pallas_call | solution.py:65
  23.4 1.1 %shard_map.66 = (f32[128,256]{1,0:T(8,128)S(1)}, bf16[128,768]{1,0:T(8,128)(2,1)S(1)}, bf16[128,768]{1,0:T(8,128)(2,1)S(1)}, f32[128,256]{1,0:T(8,128)S(1)}) custom-call(f32[128,256]{1,0:T(8,128)S(1)} %add.13.own_ref, f32[128,256]{1,0:T(8,128)S(1)} %collective-permute-done.9.other_ref, f32[136,256]{1,0:T(8,128)S(1)} %collective-permute-done.5.other_ref.message_ref, ...), custom_call_target="tpu_custom_call" | custom-call | flops 301989888 | bytes 2629632 | tf_op jit(solution)/shard_map/pallas_call | solution.py:65
  24.9 1.1 %shard_map.67 = (f32[128,256]{1,0:T(8,128)S(1)}, bf16[128,768]{1,0:T(8,128)(2,1)S(1)}, bf16[128,768]{1,0:T(8,128)(2,1)S(1)}, f32[128,256]{1,0:T(8,128)S(1)}, f32[64,256]{1,0:T(8,128)S(1)}) custom-call(f32[128,256]{1,0:T(8,128)S(1)} %add.13.own_ref, f32[128,256]{1,0:T(8,128)S(1)} %collective-permute-done.9.other_ref, ...), custom_call_target="tpu_custom_call" | custom-call | flops 301989888 | bytes 2695168 | tf_op jit(solution)/shard_map/pallas_call | solution.py:65
  26.1 1.0 %collective-permute-start.13 = (f32[192,256]{1,0:T(8,128)S(1)}, f32[192,256]{1,0:T(8,128)S(1)}, u32[]{:S(2)}, u32[]{:S(2)}) collective-permute-start(f32[192,256]{1,0:T(8,128)S(1)} %pad_maximum_fusion), channel_id=1, source_target_pairs={{0,4},{1,5},{2,6},{3,7},{4,8},{5,9},{6,10},{7,11},{8,12},{9,13},{1... | collective-permute-start | bytes 589832 | tf_op jit(solution)/shard_map/ppermute | solution.py:281
  27.0 1.1 %collective-permute-start.14 = (f32[128,256]{1,0:T(8,128)S(1)}, f32[128,256]{1,0:T(8,128)S(1)}, u32[]{:S(2)}, u32[]{:S(2)}) collective-permute-start(f32[128,256]{1,0:T(8,128)S(1)} %add.15), channel_id=1, source_target_pairs={{0,6},{1,7},{2,4},{3,5},{4,10},{5,11},{6,8},{7,9},{8,14},{9,15},{1... | collective-permute-start | bytes 393224 | tf_op jit(solution)/shard_map/ppermute | solution.py:281
  28.2 0.5 %shard_map.68 = (f32[768,256]{1,0:T(8,128)S(1)}, f32[8,128]{1,0:T(8,128)S(1)}) custom-call(f32[768,256]{1,0:T(8,128)S(1)} %get-tuple-element.44.strip_ref.held_ref, bf16[128,768]{1,0:T(8,128)(2,1)S(1)} %get-tuple-element.49.h0, bf16[128,768]{1,0:T(8,128)(2,1)S(1)} %get-tuple-element.50.l0, bf16[128,768]{1,0:T(8,128)(2,1)S(1)} %get-tuple-element.51.h1, ...), custom_call_target="tpu_custom_call" | custom-call | flops 301989888 | bytes 2625536 | tf_op jit(solution)/shard_map/pallas_call | solution.py:65
  28.7 1.6 %collective-permute-start.10 = (f32[8,128]{1,0:T(8,128)S(1)}, f32[8,128]{1,0:T(8,128)S(1)}, u32[]{:S(2)}, u32[]{:S(2)}) collective-permute-start(f32[8,128]{1,0:T(8,128)S(1)} %get-tuple-element.56), channel_id=1, source_target_pairs={{0,2},{1,3},{2,0},{3,1},{4,6},{5,7},{6,4},{7,5},{8,10},{9,11},{10,... | collective-permute-start | bytes 12296 | tf_op jit(solution)/shard_map/ppermute | solution.py:274
  30.3 2.1 %collective-permute-done.10 = f32[8,128]{1,0:T(8,128)S(1)} collective-permute-done((f32[8,128]{1,0:T(8,128)S(1)}, f32[8,128]{1,0:T(8,128)S(1)}, u32[]{:S(2)}, u32[]{:S(2)}) %collective-permute-start.10) | collective-permute-done | bytes 4128 | tf_op jit(solution)/shard_map/ppermute | solution.py:274
  32.4 5.4 %collective-permute-done.14.refs_1_ = f32[128,256]{1,0:T(8,128)S(1)} collective-permute-done((f32[128,256]{1,0:T(8,128)S(1)}, f32[128,256]{1,0:T(8,128)S(1)}, u32[]{:S(2)}, u32[]{:S(2)}) %collective-permute-start.14) | collective-permute-done | bytes 131104 | tf_op jit(solution)/shard_map/ppermute | solution.py:281
  37.9 1.1 %shard_map.69 = f32[768,256]{1,0:T(8,128)} custom-call(f32[768,256]{1,0:T(8,128)S(1)} %get-tuple-element.44.strip_ref.held_ref, f32[768,256]{1,0:T(8,128)S(1)} %get-tuple-element.55.grad_ref, f32[8,128]{1,0:T(8,128)S(1)} %add.14.refs_0_, f32[8,128]{1,0:T(8,128)S(1)} %collective-permute-done.11.refs_1_), custom_call_target="tpu_custom_call" | custom-call | bytes 2367488 | tf_op jit(solution)/shard_map/pallas_call | solution.py:65
  39.0 0.8 %shard_map.71 = f32[64,256]{1,0:T(8,128)} custom-call(f32[192,256]{1,0:T(8,128)S(1)} %collective-permute-done.13.refs_0_.message_ref, f32[64,256]{1,0:T(8,128)S(1)} %get-tuple-element.60.grad_ref, f32[8,128]{1,0:T(8,128)S(1)} %get-tuple-element.61.own_ref, f32[8,128]{1,0:T(8,128)S(1)} %collective-permute-done.15.other_ref), custom_call_target="tpu_custom_call" | custom-call | bytes 335872 | tf_op jit(solution)/shard_map/pallas_call | solution.py:65
  (34 shorter events, 1.1 us)
Async XLA Ops:
  0.6 7.1 %collective-permute-start.1 = (f32[64,256]{1,0:T(8,128)}, f32[64,256]{1,0:T(8,128)S(1)}, u32[]{:S(2)}, u32[]{:S(2)}) collective-permute-start(f32[64,256]{1,0:T(8,128)} %refs_0_.4), channel_id=1, source_target_pairs={{0,1},{1,0},{2,3},{3,2},{4,5},{5,4},{6,7},{7,6},{8,9},{9,8},{10,11... | collective-permute-start | bytes 196616 | tf_op jit(solution)/shard_map/ppermute | solution.py:274
  1.2 6.6 %collective-permute-start.2 = (f32[64,256]{1,0:T(8,128)}, f32[64,256]{1,0:T(8,128)S(1)}, u32[]{:S(2)}, u32[]{:S(2)}) collective-permute-start(f32[64,256]{1,0:T(8,128)} %refs_0_.4), channel_id=1, source_target_pairs={{0,3},{1,2},{2,1},{3,0},{4,7},{5,6},{6,5},{7,4},{8,11},{9,10},{10,... | collective-permute-start | bytes 196616 | tf_op jit(solution)/shard_map/ppermute | solution.py:274
  3.8 5.1 %collective-permute-start.3 = (f32[64,256]{1,0:T(8,128)}, f32[64,256]{1,0:T(8,128)S(1)}, u32[]{:S(2)}, u32[]{:S(2)}) collective-permute-start(f32[64,256]{1,0:T(8,128)} %refs_0_.4), channel_id=1, source_target_pairs={{0,2},{1,3},{2,0},{3,1},{4,6},{5,7},{6,4},{7,5},{8,10},{9,11},{10,... | collective-permute-start | bytes 196616 | tf_op jit(solution)/shard_map/ppermute | solution.py:274
  3.8 6.7 %collective-permute-start = (f32[64,256]{1,0:T(8,128)}, f32[64,256]{1,0:T(8,128)S(1)}, u32[]{:S(2)}, u32[]{:S(2)}) collective-permute-start(f32[64,256]{1,0:T(8,128)} %refs_0_.4), channel_id=1, source_target_pairs={{0,4},{1,5},{2,6},{3,7},{4,8},{5,9},{6,10},{7,11},{8,12},{9,13},{1... | collective-permute-start | bytes 196616 | tf_op jit(solution)/shard_map/ppermute | solution.py:281
  7.8 1.1 %copy-start.2 = (f32[64,256]{1,0:T(8,128)S(1)}, f32[64,256]{1,0:T(8,128)}, u32[]{:S(2)}) copy-start(f32[64,256]{1,0:T(8,128)} %refs_0_.4) | copy-start | bytes 196612
  8.8 1.7 %collective-permute-start.6 = (f32[128,256]{1,0:T(8,128)S(1)}, f32[128,256]{1,0:T(8,128)S(1)}, u32[]{:S(2)}, u32[]{:S(2)}) collective-permute-start(f32[128,256]{1,0:T(8,128)S(1)} %get-tuple-element.46), channel_id=1, source_target_pairs={{0,1},{1,0},{2,3},{3,2},{4,5},{5,4},{6,7},{7,6},{8,9},{9,8},{10,11... | collective-permute-start | bytes 393224 | tf_op jit(solution)/shard_map/ppermute | solution.py:274
  8.9 13.2 %copy-start.1 = (s32[2,768,256]{2,1,0:T(8,128)S(1)}, s32[2,768,256]{2,1,0:T(8,128)}, u32[]{:S(2)}) copy-start(s32[2,768,256]{2,1,0:T(8,128)} %refs_1_.3) | copy-start | bytes 4718596
  9.9 12.2 %copy-start = (f32[2,768,256]{2,1,0:T(8,128)S(1)}, f32[2,768,256]{2,1,0:T(8,128)}, u32[]{:S(2)}) copy-start(f32[2,768,256]{2,1,0:T(8,128)} %refs_0_.5) | copy-start | bytes 4718596
  10.6 9.0 %collective-permute-start.7 = (f32[128,256]{1,0:T(8,128)S(1)}, f32[128,256]{1,0:T(8,128)S(1)}, u32[]{:S(2)}, u32[]{:S(2)}) collective-permute-start(f32[128,256]{1,0:T(8,128)S(1)} %add.12), channel_id=1, source_target_pairs={{0,4},{1,5},{2,6},{3,7},{4,8},{5,9},{6,10},{7,11},{8,12},{9,13},{1... | collective-permute-start | bytes 393224 | tf_op jit(solution)/shard_map/ppermute | solution.py:281
  12.2 9.8 %collective-permute-start.8 = (f32[128,256]{1,0:T(8,128)S(1)}, f32[128,256]{1,0:T(8,128)S(1)}, u32[]{:S(2)}, u32[]{:S(2)}) collective-permute-start(f32[128,256]{1,0:T(8,128)S(1)} %add.12), channel_id=1, source_target_pairs={{0,6},{1,7},{2,4},{3,5},{4,10},{5,11},{6,8},{7,9},{8,14},{9,15},{1... | collective-permute-start | bytes 393224 | tf_op jit(solution)/shard_map/ppermute | solution.py:281
  14.7 4.8 %collective-permute-start.4 = (f32[72,256]{1,0:T(8,128)S(1)}, f32[72,256]{1,0:T(8,128)S(1)}, u32[]{:S(2)}, u32[]{:S(2)}) collective-permute-start(f32[72,256]{1,0:T(8,128)S(1)} %constant_dynamic-update-slice_fusion.refs_0_), channel_id=1, source_target_pairs={{0,2},{1,3},{2,0},{3,1},{4,6},{5,7},{6,4},{7,5},{8,10},{9,11},{10,... | collective-permute-start | bytes 221192 | tf_op jit(solution)/shard_map/ppermute | solution.py:274
  19.5 3.3 %collective-permute-start.5 = (f32[136,256]{1,0:T(8,128)S(1)}, f32[136,256]{1,0:T(8,128)S(1)}, u32[]{:S(2)}, u32[]{:S(2)}) collective-permute-start(f32[136,256]{1,0:T(8,128)S(1)} %shard_map.63.own_ref.message_ref), channel_id=1, source_target_pairs={{0,1},{1,0},{2,3},{3,2},{4,5},{5,4},{6,7},{7,6},{8,9},{9,8},{10,11... | collective-permute-start | bytes 417800 | tf_op jit(solution)/shard_map/ppermute | solution.py:274
  22.0 1.4 %collective-permute-start.9 = (f32[128,256]{1,0:T(8,128)S(1)}, f32[128,256]{1,0:T(8,128)S(1)}, u32[]{:S(2)}, u32[]{:S(2)}) collective-permute-start(f32[128,256]{1,0:T(8,128)S(1)} %add.13.own_ref), channel_id=1, source_target_pairs={{0,1},{1,0},{2,3},{3,2},{4,5},{5,4},{6,7},{7,6},{8,9},{9,8},{10,11... | collective-permute-start | bytes 393224 | tf_op jit(solution)/shard_map/ppermute | solution.py:274
  24.6 1.5 %collective-permute-start.12 = (f32[128,256]{1,0:T(8,128)S(1)}, f32[128,256]{1,0:T(8,128)S(1)}, u32[]{:S(2)}, u32[]{:S(2)}) collective-permute-start(f32[128,256]{1,0:T(8,128)S(1)} %get-tuple-element.58), channel_id=1, source_target_pairs={{0,1},{1,0},{2,3},{3,2},{4,5},{5,4},{6,7},{7,6},{8,9},{9,8},{10,11... | collective-permute-start | bytes 393224 | tf_op jit(solution)/shard_map/ppermute | solution.py:274
  26.1 11.7 %collective-permute-start.13 = (f32[192,256]{1,0:T(8,128)S(1)}, f32[192,256]{1,0:T(8,128)S(1)}, u32[]{:S(2)}, u32[]{:S(2)}) collective-permute-start(f32[192,256]{1,0:T(8,128)S(1)} %pad_maximum_fusion), channel_id=1, source_target_pairs={{0,4},{1,5},{2,6},{3,7},{4,8},{5,9},{6,10},{7,11},{8,12},{9,13},{1... | collective-permute-start | bytes 589832 | tf_op jit(solution)/shard_map/ppermute | solution.py:281
  27.0 10.7 %collective-permute-start.14 = (f32[128,256]{1,0:T(8,128)S(1)}, f32[128,256]{1,0:T(8,128)S(1)}, u32[]{:S(2)}, u32[]{:S(2)}) collective-permute-start(f32[128,256]{1,0:T(8,128)S(1)} %add.15), channel_id=1, source_target_pairs={{0,6},{1,7},{2,4},{3,5},{4,10},{5,11},{6,8},{7,9},{8,14},{9,15},{1... | collective-permute-start | bytes 393224 | tf_op jit(solution)/shard_map/ppermute | solution.py:281
  28.7 3.7 %collective-permute-start.10 = (f32[8,128]{1,0:T(8,128)S(1)}, f32[8,128]{1,0:T(8,128)S(1)}, u32[]{:S(2)}, u32[]{:S(2)}) collective-permute-start(f32[8,128]{1,0:T(8,128)S(1)} %get-tuple-element.56), channel_id=1, source_target_pairs={{0,2},{1,3},{2,0},{3,1},{4,6},{5,7},{6,4},{7,5},{8,10},{9,11},{10,... | collective-permute-start | bytes 12296 | tf_op jit(solution)/shard_map/ppermute | solution.py:274
  32.4 5.5 %collective-permute-start.11 = (f32[8,128]{1,0:T(8,128)S(1)}, f32[8,128]{1,0:T(8,128)S(1)}, u32[]{:S(2)}, u32[]{:S(2)}) collective-permute-start(f32[8,128]{1,0:T(8,128)S(1)} %add.14.refs_0_), channel_id=1, source_target_pairs={{0,1},{1,0},{2,3},{3,2},{4,5},{5,4},{6,7},{7,6},{8,9},{9,8},{10,11... | collective-permute-start | bytes 12296 | tf_op jit(solution)/shard_map/ppermute | solution.py:274
  37.8 1.2 %collective-permute-start.15 = (f32[8,128]{1,0:T(8,128)S(1)}, f32[8,128]{1,0:T(8,128)S(1)}, u32[]{:S(2)}, u32[]{:S(2)}) collective-permute-start(f32[8,128]{1,0:T(8,128)S(1)} %get-tuple-element.61.own_ref), channel_id=1, source_target_pairs={{0,1},{1,0},{2,3},{3,2},{4,5},{5,4},{6,7},{7,6},{8,9},{9,8},{10,11... | collective-permute-start | bytes 12296 | tf_op jit(solution)/shard_map/ppermute | solution.py:274

commit v5 on v4

--- a/solution.py
+++ b/solution.py
@@ -16,14 +16,13 @@
 CHUNK = 256
 HIDDEN = 1e9
 GRANT = 16 << 20
-WIDE = 54_000_000
+WIDE = 53_000_000
 F32 = jnp.float32
 BF16 = jnp.bfloat16
 
 VMEM = pl.BlockSpec(memory_space=pltpu.VMEM)
 HBM = pl.BlockSpec(memory_space=pltpu.HBM)
 
-NT = (((1,), (1,)), ((), ()))
 NN = (((1,), (0,)), ((), ()))
 TN = (((0,), (0,)), ((), ()))
 
@@ -96,7 +95,7 @@
 def prepare_kernel(stratum, share, *refs):
     with_strip = stratum == 0
     sources = refs[: 2 + with_strip]
-    outs = refs[len(sources) : len(sources) + 1 + 3 * with_strip]
+    outs = refs[len(sources) : len(sources) + 1 + 5 * with_strip]
     buffers, sem = refs[len(sources) + len(outs) : -1], refs[-1]
     pixels, dates = buffers[0].shape
     nx = dates // share // CORES
@@ -124,10 +123,11 @@
             strip = buffers[2][chunk, :]
             outs[1][chunk, :] = strip
             outs[2][chunk, :], outs[3][chunk, :] = split(strip)
+            outs[4][:, chunk], outs[5][:, chunk] = split(strip.T)
 
 
 def errors_and_part(side, problem, block, high_ref, low_ref):
-    values_ref, h_ref, l_ref = problem
+    values_ref, h_ref, l_ref, th_ref, tl_ref = problem
     half = block.shape[0]
     rows = slice(side * half, (side + 1) * half)
     block = split(block)
@@ -135,7 +135,8 @@
     for chunk in chunks_of(values_ref.shape[1]):
         strip = (h_ref[chunk, :], l_ref[chunk, :])
         values = values_ref[rows, chunk]
-        errors = jnp.where(values < HIDDEN, values - product(block, strip, NT), 0.0)
+        predicted = product(block, (th_ref[:, chunk], tl_ref[:, chunk]), NN)
+        errors = jnp.where(values < HIDDEN, values - predicted, 0.0)
         errors = split(errors)
         high_ref[:, chunk], low_ref[:, chunk] = errors
         part = product(errors, strip, NN)
@@ -157,14 +158,15 @@
 
 
 def first_send_kernel(nx, *refs):
-    problem, (send_ref, high_ref, low_ref, block_ref) = refs[nx : nx + 3], refs[nx + 3 :]
-    assemble(refs[:nx], block_ref)
-    send_ref[...] = errors_and_part(0, problem, block_ref[...], high_ref, low_ref)
-
-
-def first_keep_kernel(nx, *refs):
-    problem, (keep_ref, high_ref, low_ref, block_ref) = refs[nx : nx + 3], refs[nx + 3 :]
-    assemble(refs[:nx], block_ref)
+    problem, outs = refs[2 * nx : 2 * nx + 5], refs[2 * nx + 5 :]
+    send_ref, high_ref, low_ref, other_ref, own_ref = outs
+    assemble(refs[nx : 2 * nx], own_ref)
+    assemble(refs[:nx], other_ref)
+    send_ref[...] = errors_and_part(0, problem, other_ref[...], high_ref, low_ref)
+
+
+def first_keep_kernel(block_ref, *refs):
+    problem, (keep_ref, high_ref, low_ref) = refs[:5], refs[5:]
     block = block_ref[...]
     part = errors_and_part(1, problem, block, high_ref, low_ref)
     keep_ref[...] = with_ridge(part, block)
@@ -174,18 +176,18 @@
     return step_of([tile_squares(own_ref[...]), tile_squares(other_ref[...])], count)
 
 
-def later_send_kernel(count, own_ref, other_ref, message_ref, *refs):
-    problem, (send_ref, high_ref, low_ref, block_ref) = refs[:3], refs[3:]
+def later_send_kernel(count, own_ref, other_ref, old_ref, *refs):
+    problem, (send_ref, high_ref, low_ref, block_ref) = refs[:5], refs[5:]
     step = later_step(count, own_ref, other_ref)
-    block = message_ref[: other_ref.shape[0], :] - step * other_ref[...]
+    block = old_ref[...] - step * other_ref[...]
     block_ref[...] = block
     send_ref[...] = errors_and_part(0, problem, block, high_ref, low_ref)
 
 
-def later_keep_kernel(count, share, own_ref, other_ref, message_ref, *refs):
-    problem, (keep_ref, high_ref, low_ref, block_ref, share_ref) = refs[:3], refs[3:]
+def later_keep_kernel(count, share, own_ref, other_ref, old_ref, *refs):
+    problem, (keep_ref, high_ref, low_ref, block_ref, share_ref) = refs[:5], refs[5:]
     step = later_step(count, own_ref, other_ref)
-    block = message_ref[: own_ref.shape[0], :] - step * own_ref[...]
+    block = old_ref[...] - step * own_ref[...]
     block_ref[...] = block
     chip, _ = place()
     share_ref[...] = block_ref[aligned(chip, share), :]
@@ -202,33 +204,16 @@
 def gradient_kernel(strip_ref, h0, l0, h1, l1, b0, b1, grad_ref, tile_ref):
     grad = pixel_gradient(strip_ref, ((h0, h1), (l0, l1)), (b0, b1))
     grad_ref[...] = grad
-    tile = tile_squares(grad)
-    columns = tile_ref.shape[1]
-    tile_ref[:, :128] = tile
-    if columns > 128:
-        tile_ref[:, 128:] = jnp.zeros((8, columns - 128), F32)
-
-
-def join_kernel(*refs):
-    messages, out_ref = refs[:-1], refs[-1]
-    nx = len(messages)
-    share = messages[0].shape[0] - 8
-    chip, _ = place()
-    total = None
-    for dx, ref in enumerate(messages):
-        out_ref[aligned(lax.rem(chip - dx + nx, nx), share), :] = ref[:share, :]
-        tile = ref[share:, :]
-        total = tile if total is None else total + tile
-    out_ref[nx * share :, :] = total
-
-
-def first_step_kernel(count, own_ref, other_ref, strip_ref, grad_ref, *outs):
-    strip_out, h_ref, l_ref = outs
-    half = own_ref.shape[0] - 8
-    step = step_of([own_ref[half:, :128], other_ref[half:, :128]], count)
+    tile_ref[...] = tile_squares(grad)
+
+
+def first_step_kernel(count, strip_ref, grad_ref, own_ref, other_ref, *outs):
+    strip_out, h_ref, l_ref, th_ref, tl_ref = outs
+    step = step_of([own_ref[...], other_ref[...]], count)
     strip = strip_ref[...] - step * grad_ref[...]
     strip_out[...] = strip
     h_ref[...], l_ref[...] = split(strip)
+    th_ref[...], tl_ref[...] = split(strip.T)
 
 
 def step_kernel(count, held_ref, grad_ref, *refs):
@@ -284,8 +269,8 @@
         return [value] + [within(value, dx, 0) for dx in range(1, nx)]
 
     strip_shapes = [shape(pixels, rank)] + [shape(pixels, rank, BF16)] * 2
+    strip_shapes += [shape(rank, pixels, BF16)] * 2
     part_shapes = [shape(half, rank)] + [shape(half, pixels, BF16)] * 2
-    part_shapes += [shape(half, rank)]
 
     def prepared(stratum, grant, *args):
         kinds = [F32, jnp.int32, F32][: len(args)]
@@ -301,43 +286,45 @@
 
     others = [within(date_factors, dx, 1) for dx in range(nx)]
     owns = chips(date_factors)
-    old = onward(date_factors, 0)
     values, strip, *halves = prepared(0, WIDE, readings, coverage, pixel_factors)
     values_1, = prepared(1, GRANT, readings, coverage)
-    send, h0, l0, b0 = call(
-        functools.partial(first_send_kernel, nx), part_shapes,
-        *others, values, *halves, flops=6 * work,
+    send, h0, l0, b0, b1 = call(
+        functools.partial(first_send_kernel, nx),
+        part_shapes + [shape(half, rank)] * 2,
+        *others, *owns, values, *halves, flops=6 * work,
     )
     got = within(send, 0, 1)
-    keep, h1, l1, b1 = call(
-        functools.partial(first_keep_kernel, nx), part_shapes,
-        *owns, values, *halves, flops=6 * work,
+    old_half = onward(b1, 0)
+    keep, h1, l1 = call(
+        first_keep_kernel, part_shapes, b1, values, *halves, flops=6 * work
     )
     mine = keep + got
     came = [onward(mine, dx) for dx in range(nx)]
     grad, tile = call(
-        gradient_kernel, [shape(pixels, rank), shape(8, rank)],
+        gradient_kernel, [shape(pixels, rank), shape(8, 128)],
         strip, h0, l0, h1, l1, b0, b1, flops=6 * work,
     )
-    messages = chips(jnp.concatenate([old, tile], 0))
-    own_message, = call(join_kernel, [shape(half + 8, rank)], *messages)
-    other_message = within(own_message, 0, 1)
+    tiles = chips(tile)
+    tile = sum(tiles[1:], tiles[0])
+    other_tile = within(tile, 0, 1)
+    old_other = within(old_half, 0, 1)
     strip, *halves = call(
         functools.partial(first_step_kernel, pixel_count), strip_shapes,
-        own_message, other_message, strip, grad,
+        strip, grad, tile, other_tile,
     )
     own_grad = sum(came[1:], came[0])
     other_grad = within(own_grad, 0, 1)
 
     send, h0, l0, b0 = call(
-        functools.partial(later_send_kernel, date_count), part_shapes,
-        own_grad, other_grad, other_message, values_1, *halves, flops=6 * work,
+        functools.partial(later_send_kernel, date_count),
+        part_shapes + [shape(half, rank)],
+        own_grad, other_grad, old_other, values_1, *halves, flops=6 * work,
     )
     got = within(send, 0, 1)
     keep, h1, l1, b1, own = call(
         functools.partial(later_keep_kernel, date_count, share),
-        part_shapes + [shape(share, rank)],
-        own_grad, other_grad, own_message, values_1, *halves, flops=6 * work,
+        part_shapes + [shape(half, rank), shape(share, rank)],
+        own_grad, other_grad, old_half, values_1, *halves, flops=6 * work,
     )
     mine = keep + got
     came = [onward(jnp.concatenate([mine, own], 0), 0)]

time: 40 us -> 45.3 us (1.13)
  waiting for transfers between devices: 14.4 us -> 22.6 us
  Pallas kernels: 10.2 us -> 8.77 us
  starting transfers between devices: 14.2 us -> 12.9 us
    ppermute x5, waiting for transfers between devices: 7.81 us -> 13.9 us  [onward(): return lax.ppermute(value, ('blk', 'sub'), pairs)]
    ppermute x11 -> x12, waiting for transfers between devices: 6.56 us -> 8.69 us  [within(): return lax.ppermute(value, 'sub', pairs)]
    pallas_call x13 -> x12, Pallas kernels: 10.2 us -> 8.77 us  [call(): pl.pallas_call(kernel, out_shape=outs, in_specs=[where] * len(args), out_...]
    ppermute x5, starting transfers between devices: 8.31 us -> 7.08 us  [onward(): return lax.ppermute(value, ('blk', 'sub'), pairs)]
    ppermute x11 -> x12, starting transfers between devices: 5.93 us -> 5.79 us  [within(): return lax.ppermute(value, 'sub', pairs)]
  transfers between devices with their start and end apart: 16 -> 17, of which waited for: 5 -> 10; matrix products, arithmetic and copies ran while one was open for 0% -> 0% of each run, Pallas kernels for 21% -> 15%
where the time goes in v5:
time: 45.3 us; the launch traced here: 45.2 us
  waiting for transfers between devices  22.6 us (50%)
  starting transfers between devices  12.9 us (28%)
  Pallas kernels  8.77 us (19%)
  between operations  0.83 us (2%)
    ppermute x5, waiting for transfers between devices, onward(): return lax.ppermute(value, ('blk', 'sub'), pairs)  13.9 us
    pallas_call x12, Pallas kernels, call(): pl.pallas_call(kernel, out_shape=outs, in_specs=[where] * len(args), out_...  8.77 us
    ppermute x12, waiting for transfers between devices, within(): return lax.ppermute(value, 'sub', pairs)  8.69 us
    ppermute x5, starting transfers between devices, onward(): return lax.ppermute(value, ('blk', 'sub'), pairs)  7.08 us
    ppermute x12, starting transfers between devices, within(): return lax.ppermute(value, 'sub', pairs)  5.79 us
  transfers between devices with their start and end apart: 17, of which 10 were waited for; matrix products, arithmetic and copies ran while one was open for 0% of the time, Pallas kernels for 15%

profile of v5, /device:TPU:0, one launch (start us, length us, event | category | flops | bytes accessed | tf_op | source)
XLA Modules:
  0.0 45.2 jit_solution(913388065764160268)
XLA Ops:
  0.6 0.6 %collective-permute-start = (f32[64,256]{1,0:T(8,128)}, f32[64,256]{1,0:T(8,128)S(1)}, u32[]{:S(2)}, u32[]{:S(2)}) collective-permute-start(f32[64,256]{1,0:T(8,128)} %refs_2_.3), channel_id=1, source_target_pairs={{0,1},{1,0},{2,3},{3,2},{4,5},{5,4},{6,7},{7,6},{8,9},{9,8},{10,11... | collective-permute-start | bytes 196616 | tf_op jit(solution)/shard_map/ppermute | solution.py:259
  1.2 2.6 %collective-permute-start.1 = (f32[64,256]{1,0:T(8,128)}, f32[64,256]{1,0:T(8,128)S(1)}, u32[]{:S(2)}, u32[]{:S(2)}) collective-permute-start(f32[64,256]{1,0:T(8,128)} %refs_2_.3), channel_id=1, source_target_pairs={{0,3},{1,2},{2,1},{3,0},{4,7},{5,6},{6,5},{7,4},{8,11},{9,10},{10,... | collective-permute-start | bytes 196616 | tf_op jit(solution)/shard_map/ppermute | solution.py:259
  3.8 1.9 %shard_map.59 = (f32[256,768]{1,0:T(8,128)S(1)}, f32[768,256]{1,0:T(8,128)S(1)}, bf16[768,256]{1,0:T(8,128)(2,1)S(1)}, bf16[768,256]{1,0:T(8,128)(2,1)S(1)}, bf1...) custom-call(f32[2,768,256]{2,1,0:T(8,128)} %refs_0_.3, s32[2,768,256]{2,1,0:T(8,128)} %refs_1_.3, f32[768,256]{1,0:T(8,128)} %refs_2_.2), custom_call_target="tpu_custom_call" | custom-call | bytes 7077888 | tf_op jit(solution)/shard_map/pallas_call | solution.py:64
  5.7 0.9 %collective-permute-done.1.refs_1_ = f32[64,256]{1,0:T(8,128)S(1)} collective-permute-done((f32[64,256]{1,0:T(8,128)}, f32[64,256]{1,0:T(8,128)S(1)}, u32[]{:S(2)}, u32[]{:S(2)}) %collective-permute-start.1) | collective-permute-done | bytes 65568 | tf_op jit(solution)/shard_map/ppermute | solution.py:259
  6.6 1.7 %collective-permute-done.2.refs_3_ = f32[64,256]{1,0:T(8,128)S(1)} collective-permute-done((f32[64,256]{1,0:T(8,128)}, f32[64,256]{1,0:T(8,128)S(1)}, u32[]{:S(2)}, u32[]{:S(2)}) %collective-permute-start.2) | collective-permute-done | bytes 65568 | tf_op jit(solution)/shard_map/ppermute | solution.py:259
  8.3 0.7 %shard_map.60 = (f32[128,256]{1,0:T(8,128)S(1)}, bf16[128,768]{1,0:T(8,128)(2,1)S(1)}, bf16[128,768]{1,0:T(8,128)(2,1)S(1)}, f32[128,256]{1,0:T(8,128)S(1)}, f32[128,256]{1,0:T(8,128)S(1)}) custom-call(f32[64,256]{1,0:T(8,128)S(1)} %collective-permute-done.refs_0_, f32[64,256]{1,0:T(8,128)S(1)} %collective-permute-done.1.refs_1_, f32[64,256]{1,0:T(8,128)S(1)} %copy-done.2, ...), custom_call_target="tpu_custom_call" | custom-call | flops 301989888 | bytes 3407872 | tf_op jit(solution)/shard_map/pallas_call | solution.py:64
  9.0 1.6 %collective-permute-start.9 = (f32[128,256]{1,0:T(8,128)S(1)}, f32[128,256]{1,0:T(8,128)S(1)}, u32[]{:S(2)}, u32[]{:S(2)}) collective-permute-start(f32[128,256]{1,0:T(8,128)S(1)} %get-tuple-element.44.block_ref.b1), channel_id=1, source_target_pairs={{0,4},{1,5},{2,6},{3,7},{4,8},{5,9},{6,10},{7,11},{8,12},{9,13},{1... | collective-permute-start | bytes 393224 | tf_op jit(solution)/shard_map/ppermute | solution.py:266
  10.6 0.6 %shard_map.61 = (f32[128,256]{1,0:T(8,128)S(1)}, bf16[128,768]{1,0:T(8,128)(2,1)S(1)}, bf16[128,768]{1,0:T(8,128)(2,1)S(1)}) custom-call(f32[128,256]{1,0:T(8,128)S(1)} %get-tuple-element.44.block_ref.b1, f32[256,768]{1,0:T(8,128)S(1)} %get-tuple-element.37.refs_4_.refs_0_, bf16[768,256]{1,0:T(8,128)(2,1)S(1)} %get-tuple-element.38.refs_5_.refs_1_, ...), custom_call_target="tpu_custom_call" | custom-call | flops 301989888 | bytes 3014656 | tf_op jit(solution)/shard_map/pallas_call | solution.py:64
  11.3 1.6 %collective-permute-start.6 = (f32[128,256]{1,0:T(8,128)S(1)}, f32[128,256]{1,0:T(8,128)S(1)}, u32[]{:S(2)}, u32[]{:S(2)}) collective-permute-start(f32[128,256]{1,0:T(8,128)S(1)} %add.16), channel_id=1, source_target_pairs={{0,4},{1,5},{2,6},{3,7},{4,8},{5,9},{6,10},{7,11},{8,12},{9,13},{1... | collective-permute-start | bytes 393224 | tf_op jit(solution)/shard_map/ppermute | solution.py:266
  13.0 2.5 %collective-permute-start.7 = (f32[128,256]{1,0:T(8,128)S(1)}, f32[128,256]{1,0:T(8,128)S(1)}, u32[]{:S(2)}, u32[]{:S(2)}) collective-permute-start(f32[128,256]{1,0:T(8,128)S(1)} %add.16), channel_id=1, source_target_pairs={{0,6},{1,7},{2,4},{3,5},{4,10},{5,11},{6,8},{7,9},{8,14},{9,15},{1... | collective-permute-start | bytes 393224 | tf_op jit(solution)/shard_map/ppermute | solution.py:266
  15.5 1.8 %collective-permute-done.9.old_ref = f32[128,256]{1,0:T(8,128)S(1)} collective-permute-done((f32[128,256]{1,0:T(8,128)S(1)}, f32[128,256]{1,0:T(8,128)S(1)}, u32[]{:S(2)}, u32[]{:S(2)}) %collective-permute-start.9) | collective-permute-done | bytes 131104 | tf_op jit(solution)/shard_map/ppermute | solution.py:266
  17.2 2.8 %collective-permute-done.6 = f32[128,256]{1,0:T(8,128)S(1)} collective-permute-done((f32[128,256]{1,0:T(8,128)S(1)}, f32[128,256]{1,0:T(8,128)S(1)}, u32[]{:S(2)}, u32[]{:S(2)}) %collective-permute-start.6) | collective-permute-done | bytes 131104 | tf_op jit(solution)/shard_map/ppermute | solution.py:266
  20.0 3.3 %collective-permute-done.7 = f32[128,256]{1,0:T(8,128)S(1)} collective-permute-done((f32[128,256]{1,0:T(8,128)S(1)}, f32[128,256]{1,0:T(8,128)S(1)}, u32[]{:S(2)}, u32[]{:S(2)}) %collective-permute-start.7) | collective-permute-done | bytes 131104 | tf_op jit(solution)/shard_map/ppermute | solution.py:266
  23.9 0.6 %collective-permute-start.3 = (f32[8,128]{1,0:T(8,128)S(1)}, f32[8,128]{1,0:T(8,128)S(1)}, u32[]{:S(2)}, u32[]{:S(2)}) collective-permute-start(f32[8,128]{1,0:T(8,128)S(1)} %get-tuple-element.49), channel_id=1, source_target_pairs={{0,2},{1,3},{2,0},{3,1},{4,6},{5,7},{6,4},{7,5},{8,10},{9,11},{10,... | collective-permute-start | bytes 12296 | tf_op jit(solution)/shard_map/ppermute | solution.py:259
  24.5 3.1 %collective-permute-done.3 = f32[8,128]{1,0:T(8,128)S(1)} collective-permute-done((f32[8,128]{1,0:T(8,128)S(1)}, f32[8,128]{1,0:T(8,128)S(1)}, u32[]{:S(2)}, u32[]{:S(2)}) %collective-permute-start.3) | collective-permute-done | bytes 4128 | tf_op jit(solution)/shard_map/ppermute | solution.py:259
  27.6 0.6 %shard_map.64.refs_0_ = f32[256,768]{1,0:T(8,128)S(1)} custom-call(f32[2,768,256]{2,1,0:T(8,128)S(1)} %copy-done, s32[2,768,256]{2,1,0:T(8,128)S(1)} %copy-done.1), custom_call_target="tpu_custom_call" | custom-call | bytes 3932160 | tf_op jit(solution)/shard_map/pallas_call | solution.py:64
  29.3 0.8 %shard_map.65 = (f32[128,256]{1,0:T(8,128)S(1)}, bf16[128,768]{1,0:T(8,128)(2,1)S(1)}, bf16[128,768]{1,0:T(8,128)(2,1)S(1)}, f32[128,256]{1,0:T(8,128)S(1)}) custom-call(f32[128,256]{1,0:T(8,128)S(1)} %add.17.own_ref, f32[128,256]{1,0:T(8,128)S(1)} %collective-permute-done.8.other_ref, f32[128,256]{1,0:T(8,128)S(1)} %collective-permute-done.10.old_ref, ...), custom_call_target="tpu_custom_call" | custom-call | flops 301989888 | bytes 3407872 | tf_op jit(solution)/shard_map/pallas_call | solution.py:64
  30.3 0.8 %shard_map.66 = (f32[128,256]{1,0:T(8,128)S(1)}, bf16[128,768]{1,0:T(8,128)(2,1)S(1)}, bf16[128,768]{1,0:T(8,128)(2,1)S(1)}, f32[128,256]{1,0:T(8,128)S(1)}, f32[64,256]{1,0:T(8,128)S(1)}) custom-call(f32[128,256]{1,0:T(8,128)S(1)} %add.17.own_ref, f32[128,256]{1,0:T(8,128)S(1)} %collective-permute-done.8.other_ref, ...), custom_call_target="tpu_custom_call" | custom-call | flops 301989888 | bytes 3473408 | tf_op jit(solution)/shard_map/pallas_call | solution.py:64
  31.6 1.3 %collective-permute-start.15 = (f32[128,256]{1,0:T(8,128)S(1)}, f32[128,256]{1,0:T(8,128)S(1)}, u32[]{:S(2)}, u32[]{:S(2)}) collective-permute-start(f32[128,256]{1,0:T(8,128)S(1)} %add.19), channel_id=1, source_target_pairs={{0,6},{1,7},{2,4},{3,5},{4,10},{5,11},{6,8},{7,9},{8,14},{9,15},{1... | collective-permute-start | bytes 393224 | tf_op jit(solution)/shard_map/ppermute | solution.py:266
  33.3 1.6 %collective-permute-start.11 = (f32[8,128]{1,0:T(8,128)S(1)}, f32[8,128]{1,0:T(8,128)S(1)}, u32[]{:S(2)}, u32[]{:S(2)}) collective-permute-start(f32[8,128]{1,0:T(8,128)S(1)} %get-tuple-element.64), channel_id=1, source_target_pairs={{0,2},{1,3},{2,0},{3,1},{4,6},{5,7},{6,4},{7,5},{8,10},{9,11},{10,... | collective-permute-start | bytes 12296 | tf_op jit(solution)/shard_map/ppermute | solution.py:259
  34.9 2.1 %collective-permute-done.11 = f32[8,128]{1,0:T(8,128)S(1)} collective-permute-done((f32[8,128]{1,0:T(8,128)S(1)}, f32[8,128]{1,0:T(8,128)S(1)}, u32[]{:S(2)}, u32[]{:S(2)}) %collective-permute-start.11) | collective-permute-done | bytes 4128 | tf_op jit(solution)/shard_map/ppermute | solution.py:259
  37.0 6.1 %collective-permute-done.15.refs_1_ = f32[128,256]{1,0:T(8,128)S(1)} collective-permute-done((f32[128,256]{1,0:T(8,128)S(1)}, f32[128,256]{1,0:T(8,128)S(1)}, u32[]{:S(2)}, u32[]{:S(2)}) %collective-permute-start.15) | collective-permute-done | bytes 131104 | tf_op jit(solution)/shard_map/ppermute | solution.py:266
  43.2 1.2 %shard_map.68 = f32[768,256]{1,0:T(8,128)} custom-call(f32[768,256]{1,0:T(8,128)S(1)} %get-tuple-element.50.strip_ref.held_ref, f32[768,256]{1,0:T(8,128)S(1)} %get-tuple-element.63.grad_ref, f32[8,128]{1,0:T(8,128)S(1)} %add.18.refs_0_, f32[8,128]{1,0:T(8,128)S(1)} %collective-permute-done.12.refs_1_), custom_call_target="tpu_custom_call" | custom-call | bytes 2367488 | tf_op jit(solution)/shard_map/pallas_call | solution.py:64
  44.4 0.8 %shard_map.70 = f32[64,256]{1,0:T(8,128)} custom-call(f32[192,256]{1,0:T(8,128)S(1)} %collective-permute-done.14.refs_0_.message_ref, f32[64,256]{1,0:T(8,128)S(1)} %get-tuple-element.68.grad_ref, f32[8,128]{1,0:T(8,128)S(1)} %get-tuple-element.69.own_ref, f32[8,128]{1,0:T(8,128)S(1)} %collective-permute-done.16.other_ref), custom_call_target="tpu_custom_call" | custom-call | bytes 335872 | tf_op jit(solution)/shard_map/pallas_call | solution.py:64
  (34 shorter events, 3.1 us)
Async XLA Ops:
  0.6 7.6 %copy-start.2 = (f32[64,256]{1,0:T(8,128)S(1)}, f32[64,256]{1,0:T(8,128)}, u32[]{:S(2)}) copy-start(f32[64,256]{1,0:T(8,128)} %refs_2_.3) | copy-start | bytes 196612
  0.6 5.1 %collective-permute-start = (f32[64,256]{1,0:T(8,128)}, f32[64,256]{1,0:T(8,128)S(1)}, u32[]{:S(2)}, u32[]{:S(2)}) collective-permute-start(f32[64,256]{1,0:T(8,128)} %refs_2_.3), channel_id=1, source_target_pairs={{0,1},{1,0},{2,3},{3,2},{4,5},{5,4},{6,7},{7,6},{8,9},{9,8},{10,11... | collective-permute-start | bytes 196616 | tf_op jit(solution)/shard_map/ppermute | solution.py:259
  1.2 5.4 %collective-permute-start.1 = (f32[64,256]{1,0:T(8,128)}, f32[64,256]{1,0:T(8,128)S(1)}, u32[]{:S(2)}, u32[]{:S(2)}) collective-permute-start(f32[64,256]{1,0:T(8,128)} %refs_2_.3), channel_id=1, source_target_pairs={{0,3},{1,2},{2,1},{3,0},{4,7},{5,6},{6,5},{7,4},{8,11},{9,10},{10,... | collective-permute-start | bytes 196616 | tf_op jit(solution)/shard_map/ppermute | solution.py:259
  3.8 4.5 %collective-permute-start.2 = (f32[64,256]{1,0:T(8,128)}, f32[64,256]{1,0:T(8,128)S(1)}, u32[]{:S(2)}, u32[]{:S(2)}) collective-permute-start(f32[64,256]{1,0:T(8,128)} %refs_2_.3), channel_id=1, source_target_pairs={{0,2},{1,3},{2,0},{3,1},{4,6},{5,7},{6,4},{7,5},{8,10},{9,11},{10,... | collective-permute-start | bytes 196616 | tf_op jit(solution)/shard_map/ppermute | solution.py:259
  8.9 2.4 %collective-permute-start.5 = (f32[128,256]{1,0:T(8,128)S(1)}, f32[128,256]{1,0:T(8,128)S(1)}, u32[]{:S(2)}, u32[]{:S(2)}) collective-permute-start(f32[128,256]{1,0:T(8,128)S(1)} %get-tuple-element.52), channel_id=1, source_target_pairs={{0,1},{1,0},{2,3},{3,2},{4,5},{5,4},{6,7},{7,6},{8,9},{9,8},{10,11... | collective-permute-start | bytes 393224 | tf_op jit(solution)/shard_map/ppermute | solution.py:259
  9.0 8.2 %collective-permute-start.9 = (f32[128,256]{1,0:T(8,128)S(1)}, f32[128,256]{1,0:T(8,128)S(1)}, u32[]{:S(2)}, u32[]{:S(2)}) collective-permute-start(f32[128,256]{1,0:T(8,128)S(1)} %get-tuple-element.44.block_ref.b1), channel_id=1, source_target_pairs={{0,4},{1,5},{2,6},{3,7},{4,8},{5,9},{6,10},{7,11},{8,12},{9,13},{1... | collective-permute-start | bytes 393224 | tf_op jit(solution)/shard_map/ppermute | solution.py:266
  10.6 17.0 %copy-start.1 = (s32[2,768,256]{2,1,0:T(8,128)S(1)}, s32[2,768,256]{2,1,0:T(8,128)}, u32[]{:S(2)}) copy-start(s32[2,768,256]{2,1,0:T(8,128)} %refs_1_.3) | copy-start | bytes 4718596
  11.3 16.3 %copy-start = (f32[2,768,256]{2,1,0:T(8,128)S(1)}, f32[2,768,256]{2,1,0:T(8,128)}, u32[]{:S(2)}) copy-start(f32[2,768,256]{2,1,0:T(8,128)} %refs_0_.3) | copy-start | bytes 4718596
  11.3 8.7 %collective-permute-start.6 = (f32[128,256]{1,0:T(8,128)S(1)}, f32[128,256]{1,0:T(8,128)S(1)}, u32[]{:S(2)}, u32[]{:S(2)}) collective-permute-start(f32[128,256]{1,0:T(8,128)S(1)} %add.16), channel_id=1, source_target_pairs={{0,4},{1,5},{2,6},{3,7},{4,8},{5,9},{6,10},{7,11},{8,12},{9,13},{1... | collective-permute-start | bytes 393224 | tf_op jit(solution)/shard_map/ppermute | solution.py:266
  13.0 10.3 %collective-permute-start.7 = (f32[128,256]{1,0:T(8,128)S(1)}, f32[128,256]{1,0:T(8,128)S(1)}, u32[]{:S(2)}, u32[]{:S(2)}) collective-permute-start(f32[128,256]{1,0:T(8,128)S(1)} %add.16), channel_id=1, source_target_pairs={{0,6},{1,7},{2,4},{3,5},{4,10},{5,11},{6,8},{7,9},{8,14},{9,15},{1... | collective-permute-start | bytes 393224 | tf_op jit(solution)/shard_map/ppermute | solution.py:266
  17.2 12.0 %collective-permute-start.10 = (f32[128,256]{1,0:T(8,128)S(1)}, f32[128,256]{1,0:T(8,128)S(1)}, u32[]{:S(2)}, u32[]{:S(2)}) collective-permute-start(f32[128,256]{1,0:T(8,128)S(1)} %collective-permute-done.9.old_ref), channel_id=1, source_target_pairs={{0,1},{1,0},{2,3},{3,2},{4,5},{5,4},{6,7},{7,6},{8,9},{9,8},{10,11... | collective-permute-start | bytes 393224 | tf_op jit(solution)/shard_map/ppermute | solution.py:259
  23.3 5.9 %collective-permute-start.8 = (f32[128,256]{1,0:T(8,128)S(1)}, f32[128,256]{1,0:T(8,128)S(1)}, u32[]{:S(2)}, u32[]{:S(2)}) collective-permute-start(f32[128,256]{1,0:T(8,128)S(1)} %add.17.own_ref), channel_id=1, source_target_pairs={{0,1},{1,0},{2,3},{3,2},{4,5},{5,4},{6,7},{7,6},{8,9},{9,8},{10,11... | collective-permute-start | bytes 393224 | tf_op jit(solution)/shard_map/ppermute | solution.py:259
  23.9 3.7 %collective-permute-start.3 = (f32[8,128]{1,0:T(8,128)S(1)}, f32[8,128]{1,0:T(8,128)S(1)}, u32[]{:S(2)}, u32[]{:S(2)}) collective-permute-start(f32[8,128]{1,0:T(8,128)S(1)} %get-tuple-element.49), channel_id=1, source_target_pairs={{0,2},{1,3},{2,0},{3,1},{4,6},{5,7},{6,4},{7,5},{8,10},{9,11},{10,... | collective-permute-start | bytes 12296 | tf_op jit(solution)/shard_map/ppermute | solution.py:259
  27.6 1.2 %collective-permute-start.4 = (f32[8,128]{1,0:T(8,128)S(1)}, f32[8,128]{1,0:T(8,128)S(1)}, u32[]{:S(2)}, u32[]{:S(2)}) collective-permute-start(f32[8,128]{1,0:T(8,128)S(1)} %add.15.own_ref), channel_id=1, source_target_pairs={{0,1},{1,0},{2,3},{3,2},{4,5},{5,4},{6,7},{7,6},{8,9},{9,8},{10,11... | collective-permute-start | bytes 12296 | tf_op jit(solution)/shard_map/ppermute | solution.py:259
  30.0 1.4 %collective-permute-start.13 = (f32[128,256]{1,0:T(8,128)S(1)}, f32[128,256]{1,0:T(8,128)S(1)}, u32[]{:S(2)}, u32[]{:S(2)}) collective-permute-start(f32[128,256]{1,0:T(8,128)S(1)} %get-tuple-element.66), channel_id=1, source_target_pairs={{0,1},{1,0},{2,3},{3,2},{4,5},{5,4},{6,7},{7,6},{8,9},{9,8},{10,11... | collective-permute-start | bytes 393224 | tf_op jit(solution)/shard_map/ppermute | solution.py:259
  31.5 11.6 %collective-permute-start.14 = (f32[192,256]{1,0:T(8,128)S(1)}, f32[192,256]{1,0:T(8,128)S(1)}, u32[]{:S(2)}, u32[]{:S(2)}) collective-permute-start(f32[192,256]{1,0:T(8,128)S(1)} %pad_maximum_fusion), channel_id=1, source_target_pairs={{0,4},{1,5},{2,6},{3,7},{4,8},{5,9},{6,10},{7,11},{8,12},{9,13},{1... | collective-permute-start | bytes 589832 | tf_op jit(solution)/shard_map/ppermute | solution.py:266
  31.6 11.5 %collective-permute-start.15 = (f32[128,256]{1,0:T(8,128)S(1)}, f32[128,256]{1,0:T(8,128)S(1)}, u32[]{:S(2)}, u32[]{:S(2)}) collective-permute-start(f32[128,256]{1,0:T(8,128)S(1)} %add.19), channel_id=1, source_target_pairs={{0,6},{1,7},{2,4},{3,5},{4,10},{5,11},{6,8},{7,9},{8,14},{9,15},{1... | collective-permute-start | bytes 393224 | tf_op jit(solution)/shard_map/ppermute | solution.py:266
  33.3 3.7 %collective-permute-start.11 = (f32[8,128]{1,0:T(8,128)S(1)}, f32[8,128]{1,0:T(8,128)S(1)}, u32[]{:S(2)}, u32[]{:S(2)}) collective-permute-start(f32[8,128]{1,0:T(8,128)S(1)} %get-tuple-element.64), channel_id=1, source_target_pairs={{0,2},{1,3},{2,0},{3,1},{4,6},{5,7},{6,4},{7,5},{8,10},{9,11},{10,... | collective-permute-start | bytes 12296 | tf_op jit(solution)/shard_map/ppermute | solution.py:259
  37.0 6.2 %collective-permute-start.12 = (f32[8,128]{1,0:T(8,128)S(1)}, f32[8,128]{1,0:T(8,128)S(1)}, u32[]{:S(2)}, u32[]{:S(2)}) collective-permute-start(f32[8,128]{1,0:T(8,128)S(1)} %add.18.refs_0_), channel_id=1, source_target_pairs={{0,1},{1,0},{2,3},{3,2},{4,5},{5,4},{6,7},{7,6},{8,9},{9,8},{10,11... | collective-permute-start | bytes 12296 | tf_op jit(solution)/shard_map/ppermute | solution.py:259
  43.1 1.2 %collective-permute-start.16 = (f32[8,128]{1,0:T(8,128)S(1)}, f32[8,128]{1,0:T(8,128)S(1)}, u32[]{:S(2)}, u32[]{:S(2)}) collective-permute-start(f32[8,128]{1,0:T(8,128)S(1)} %get-tuple-element.69.own_ref), channel_id=1, source_target_pairs={{0,1},{1,0},{2,3},{3,2},{4,5},{5,4},{6,7},{7,6},{8,9},{9,8},{10,11... | collective-permute-start | bytes 12296 | tf_op jit(solution)/shard_map/ppermute | solution.py:259

commit v6 on v5

--- a/solution.py
+++ b/solution.py
@@ -158,18 +158,21 @@
 
 
 def first_send_kernel(nx, *refs):
-    problem, outs = refs[2 * nx : 2 * nx + 5], refs[2 * nx + 5 :]
-    send_ref, high_ref, low_ref, other_ref, own_ref = outs
-    assemble(refs[nx : 2 * nx], own_ref)
-    assemble(refs[:nx], other_ref)
-    send_ref[...] = errors_and_part(0, problem, other_ref[...], high_ref, low_ref)
-
-
-def first_keep_kernel(block_ref, *refs):
-    problem, (keep_ref, high_ref, low_ref) = refs[:5], refs[5:]
+    problem, (send_ref, high_ref, low_ref, block_ref) = refs[nx : nx + 5], refs[nx + 5 :]
+    assemble(refs[:nx], block_ref)
+    send_ref[...] = errors_and_part(0, problem, block_ref[...], high_ref, low_ref)
+
+
+def first_keep_kernel(nx, *refs):
+    problem, (keep_ref, high_ref, low_ref, block_ref) = refs[nx : nx + 5], refs[nx + 5 :]
+    assemble(refs[:nx], block_ref)
     block = block_ref[...]
     part = errors_and_part(1, problem, block, high_ref, low_ref)
     keep_ref[...] = with_ridge(part, block)
+
+
+def join_kernel(*refs):
+    assemble(refs[:-1], refs[-1])
 
 
 def later_step(count, own_ref, other_ref):
@@ -223,20 +226,13 @@
 
 def last_gradient_kernel(share, *refs):
     parts, (grad_ref, tile_ref), sum_ref = refs[:-3], refs[-3:-1], refs[-1]
-    half = sum_ref.shape[0]
-    total = parts[0][:half, :]
+    total = parts[0][...]
     for ref in parts[1:]:
         total = total + ref[...]
     sum_ref[...] = total
     tile_ref[...] = tile_squares(total)
     chip, _ = place()
     grad_ref[...] = sum_ref[aligned(chip, share), :]
-
-
-def last_step_kernel(count, message_ref, grad_ref, own_ref, other_ref, out_ref):
-    step = step_of([own_ref[...], other_ref[...]], count)
-    held = message_ref[message_ref.shape[0] - grad_ref.shape[0] :, :]
-    out_ref[...] = held - step * grad_ref[...]
 
 
 def on_device(readings, coverage, pixel_factors, date_factors):
@@ -286,17 +282,17 @@
 
     others = [within(date_factors, dx, 1) for dx in range(nx)]
     owns = chips(date_factors)
+    old = onward(date_factors, 0)
     values, strip, *halves = prepared(0, WIDE, readings, coverage, pixel_factors)
     values_1, = prepared(1, GRANT, readings, coverage)
-    send, h0, l0, b0, b1 = call(
-        functools.partial(first_send_kernel, nx),
-        part_shapes + [shape(half, rank)] * 2,
-        *others, *owns, values, *halves, flops=6 * work,
+    send, h0, l0, b0 = call(
+        functools.partial(first_send_kernel, nx), part_shapes + [shape(half, rank)],
+        *others, values, *halves, flops=6 * work,
     )
     got = within(send, 0, 1)
-    old_half = onward(b1, 0)
-    keep, h1, l1 = call(
-        first_keep_kernel, part_shapes, b1, values, *halves, flops=6 * work
+    keep, h1, l1, b1 = call(
+        functools.partial(first_keep_kernel, nx), part_shapes + [shape(half, rank)],
+        *owns, values, *halves, flops=6 * work,
     )
     mine = keep + got
     came = [onward(mine, dx) for dx in range(nx)]
@@ -307,6 +303,8 @@
     tiles = chips(tile)
     tile = sum(tiles[1:], tiles[0])
     other_tile = within(tile, 0, 1)
+    olds = chips(old)
+    old_half, = call(join_kernel, [shape(half, rank)], *olds)
     old_other = within(old_half, 0, 1)
     strip, *halves = call(
         functools.partial(first_step_kernel, pixel_count), strip_shapes,
@@ -327,8 +325,8 @@
         own_grad, other_grad, old_half, values_1, *halves, flops=6 * work,
     )
     mine = keep + got
-    came = [onward(jnp.concatenate([mine, own], 0), 0)]
-    came += [onward(mine, dx) for dx in range(1, nx)]
+    came = [onward(mine, dx) for dx in range(nx)]
+    held = onward(own, 0)
     grad, tile = call(
         gradient_kernel, [shape(pixels, rank), shape(8, 128)],
         strip, h0, l0, h1, l1, b0, b1, flops=6 * work,
@@ -347,8 +345,8 @@
     )
     other_tile = within(tile, 0, 1)
     date_out, = call(
-        functools.partial(last_step_kernel, date_count), [shape(share, rank)],
-        came[0], date_grad, tile, other_tile,
+        functools.partial(step_kernel, date_count), [shape(share, rank)],
+        held, date_grad, tile, other_tile,
     )
     return strip, date_out
 

time: 45.3 us -> 44.8 us (0.989)
  waiting for transfers between devices: 22.6 us -> 16.1 us
  starting transfers between devices: 12.9 us -> 19 us
    ppermute x5 -> x6, waiting for transfers between devices: 13.9 us -> 5.4 us  [onward(): return lax.ppermute(value, ('blk', 'sub'), pairs)]
    ppermute x12 -> x13, starting transfers between devices: 5.79 us -> 9.37 us  [within(): return lax.ppermute(value, 'sub', pairs)]
    ppermute x5 -> x6, starting transfers between devices: 7.08 us -> 9.58 us  [onward(): return lax.ppermute(value, ('blk', 'sub'), pairs)]
    ppermute x12 -> x13, waiting for transfers between devices: 8.69 us -> 10.7 us  [within(): return lax.ppermute(value, 'sub', pairs)]
    pallas_call x12 -> x13, Pallas kernels: 8.77 us -> 8.77 us  [call(): pl.pallas_call(kernel, out_shape=outs, in_specs=[where] * len(args), out_...]
  transfers between devices with their start and end apart: 17 -> 19, of which waited for: 10 -> 10; matrix products, arithmetic and copies ran while one was open for 0% -> 0% of each run, Pallas kernels for 15% -> 15%
where the time goes in v6:
time: 44.8 us; the launch traced here: 44.7 us
  starting transfers between devices  19 us (42%)
  waiting for transfers between devices  16.1 us (36%)
  Pallas kernels  8.77 us (20%)
  between operations  0.83 us (2%)
    ppermute x13, waiting for transfers between devices, within(): return lax.ppermute(value, 'sub', pairs)  10.7 us
    ppermute x6, starting transfers between devices, onward(): return lax.ppermute(value, ('blk', 'sub'), pairs)  9.58 us
    ppermute x13, starting transfers between devices, within(): return lax.ppermute(value, 'sub', pairs)  9.37 us
    pallas_call x13, Pallas kernels, call(): pl.pallas_call(kernel, out_shape=outs, in_specs=[where] * len(args), out_...  8.77 us
    ppermute x6, waiting for transfers between devices, onward(): return lax.ppermute(value, ('blk', 'sub'), pairs)  5.4 us
  transfers between devices with their start and end apart: 19, of which 10 were waited for; matrix products, arithmetic and copies ran while one was open for 0% of the time, Pallas kernels for 15%

profile of v6, /device:TPU:0, one launch (start us, length us, event | category | flops | bytes accessed | tf_op | source)
XLA Modules:
  0.0 44.7 jit_solution(2908817734521317093)
XLA Ops:
  1.2 2.6 %collective-permute-start.1 = (f32[64,256]{1,0:T(8,128)}, f32[64,256]{1,0:T(8,128)S(1)}, u32[]{:S(2)}, u32[]{:S(2)}) collective-permute-start(f32[64,256]{1,0:T(8,128)} %refs_0_.4), channel_id=1, source_target_pairs={{0,3},{1,2},{2,1},{3,0},{4,7},{5,6},{6,5},{7,4},{8,11},{9,10},{10,... | collective-permute-start | bytes 196616 | tf_op jit(solution)/shard_map/ppermute | solution.py:255
  3.8 1.9 %shard_map.59 = (f32[256,768]{1,0:T(8,128)S(1)}, f32[768,256]{1,0:T(8,128)S(1)}, bf16[768,256]{1,0:T(8,128)(2,1)S(1)}, bf16[768,256]{1,0:T(8,128)(2,1)S(1)}, bf1...) custom-call(f32[2,768,256]{2,1,0:T(8,128)} %refs_0_.5, s32[2,768,256]{2,1,0:T(8,128)} %refs_1_.3, f32[768,256]{1,0:T(8,128)} %refs_2_.1), custom_call_target="tpu_custom_call" | custom-call | bytes 7077888 | tf_op jit(solution)/shard_map/pallas_call | solution.py:64
  5.7 0.7 %collective-permute-done.1.refs_1_ = f32[64,256]{1,0:T(8,128)S(1)} collective-permute-done((f32[64,256]{1,0:T(8,128)}, f32[64,256]{1,0:T(8,128)S(1)}, u32[]{:S(2)}, u32[]{:S(2)}) %collective-permute-start.1) | collective-permute-done | bytes 65568 | tf_op jit(solution)/shard_map/ppermute | solution.py:255
  6.4 0.6 %shard_map.60 = (f32[128,256]{1,0:T(8,128)S(1)}, bf16[128,768]{1,0:T(8,128)(2,1)S(1)}, bf16[128,768]{1,0:T(8,128)(2,1)S(1)}, f32[128,256]{1,0:T(8,128)S(1)}) custom-call(f32[64,256]{1,0:T(8,128)S(1)} %collective-permute-done.refs_0_, f32[64,256]{1,0:T(8,128)S(1)} %collective-permute-done.1.refs_1_, f32[256,768]{1,0:T(8,128)S(1)} %get-tuple-element.37.refs_2_, ...), custom_call_target="tpu_custom_call" | custom-call | flops 301989888 | bytes 3145728 | tf_op jit(solution)/shard_map/pallas_call | solution.py:64
  7.2 1.7 %collective-permute-start.2 = (f32[64,256]{1,0:T(8,128)S(1)}, f32[64,256]{1,0:T(8,128)S(1)}, u32[]{:S(2)}, u32[]{:S(2)}) collective-permute-start(f32[64,256]{1,0:T(8,128)S(1)} %copy-done.2), channel_id=1, source_target_pairs={{0,2},{1,3},{2,0},{3,1},{4,6},{5,7},{6,4},{7,5},{8,10},{9,11},{10,... | collective-permute-start | bytes 196616 | tf_op jit(solution)/shard_map/ppermute | solution.py:255
  8.9 1.6 %collective-permute-start.9 = (f32[64,256]{1,0:T(8,128)S(1)}, f32[64,256]{1,0:T(8,128)S(1)}, u32[]{:S(2)}, u32[]{:S(2)}) collective-permute-start(f32[64,256]{1,0:T(8,128)S(1)} %copy-done.2), channel_id=1, source_target_pairs={{0,4},{1,5},{2,6},{3,7},{4,8},{5,9},{6,10},{7,11},{8,12},{9,13},{1... | collective-permute-start | bytes 196616 | tf_op jit(solution)/shard_map/ppermute | solution.py:262
  10.5 1.1 %collective-permute-done.2.refs_1_ = f32[64,256]{1,0:T(8,128)S(1)} collective-permute-done((f32[64,256]{1,0:T(8,128)S(1)}, f32[64,256]{1,0:T(8,128)S(1)}, u32[]{:S(2)}, u32[]{:S(2)}) %collective-permute-start.2) | collective-permute-done | bytes 65568 | tf_op jit(solution)/shard_map/ppermute | solution.py:255
  11.6 0.6 %shard_map.61 = (f32[128,256]{1,0:T(8,128)S(1)}, bf16[128,768]{1,0:T(8,128)(2,1)S(1)}, bf16[128,768]{1,0:T(8,128)(2,1)S(1)}, f32[128,256]{1,0:T(8,128)S(1)}) custom-call(f32[64,256]{1,0:T(8,128)S(1)} %copy-done.2, f32[64,256]{1,0:T(8,128)S(1)} %collective-permute-done.2.refs_1_, f32[256,768]{1,0:T(8,128)S(1)} %get-tuple-element.37.refs_2_, ...), custom_call_target="tpu_custom_call" | custom-call | flops 301989888 | bytes 3145728 | tf_op jit(solution)/shard_map/pallas_call | solution.py:64
  12.3 1.7 %collective-permute-start.6 = (f32[128,256]{1,0:T(8,128)S(1)}, f32[128,256]{1,0:T(8,128)S(1)}, u32[]{:S(2)}, u32[]{:S(2)}) collective-permute-start(f32[128,256]{1,0:T(8,128)S(1)} %add.16), channel_id=1, source_target_pairs={{0,4},{1,5},{2,6},{3,7},{4,8},{5,9},{6,10},{7,11},{8,12},{9,13},{1... | collective-permute-start | bytes 393224 | tf_op jit(solution)/shard_map/ppermute | solution.py:262
  14.0 2.5 %collective-permute-start.7 = (f32[128,256]{1,0:T(8,128)S(1)}, f32[128,256]{1,0:T(8,128)S(1)}, u32[]{:S(2)}, u32[]{:S(2)}) collective-permute-start(f32[128,256]{1,0:T(8,128)S(1)} %add.16), channel_id=1, source_target_pairs={{0,6},{1,7},{2,4},{3,5},{4,10},{5,11},{6,8},{7,9},{8,14},{9,15},{1... | collective-permute-start | bytes 393224 | tf_op jit(solution)/shard_map/ppermute | solution.py:262
  17.0 3.9 %collective-permute-done.10.refs_1_ = f32[64,256]{1,0:T(8,128)S(1)} collective-permute-done((f32[64,256]{1,0:T(8,128)S(1)}, f32[64,256]{1,0:T(8,128)S(1)}, u32[]{:S(2)}, u32[]{:S(2)}) %collective-permute-start.10) | collective-permute-done | bytes 65568 | tf_op jit(solution)/shard_map/ppermute | solution.py:255
  21.0 1.3 %collective-permute-done.7 = f32[128,256]{1,0:T(8,128)S(1)} collective-permute-done((f32[128,256]{1,0:T(8,128)S(1)}, f32[128,256]{1,0:T(8,128)S(1)}, u32[]{:S(2)}, u32[]{:S(2)}) %collective-permute-start.7) | collective-permute-done | bytes 131104 | tf_op jit(solution)/shard_map/ppermute | solution.py:262
  23.0 1.8 %collective-permute-start.3 = (f32[8,128]{1,0:T(8,128)S(1)}, f32[8,128]{1,0:T(8,128)S(1)}, u32[]{:S(2)}, u32[]{:S(2)}) collective-permute-start(f32[8,128]{1,0:T(8,128)S(1)} %get-tuple-element.49), channel_id=1, source_target_pairs={{0,2},{1,3},{2,0},{3,1},{4,6},{5,7},{6,4},{7,5},{8,10},{9,11},{10,... | collective-permute-start | bytes 12296 | tf_op jit(solution)/shard_map/ppermute | solution.py:255
  24.8 1.9 %collective-permute-done.3 = f32[8,128]{1,0:T(8,128)S(1)} collective-permute-done((f32[8,128]{1,0:T(8,128)S(1)}, f32[8,128]{1,0:T(8,128)S(1)}, u32[]{:S(2)}, u32[]{:S(2)}) %collective-permute-start.3) | collective-permute-done | bytes 4128 | tf_op jit(solution)/shard_map/ppermute | solution.py:255
  28.3 0.8 %shard_map.66 = (f32[128,256]{1,0:T(8,128)S(1)}, bf16[128,768]{1,0:T(8,128)(2,1)S(1)}, bf16[128,768]{1,0:T(8,128)(2,1)S(1)}, f32[128,256]{1,0:T(8,128)S(1)}) custom-call(f32[128,256]{1,0:T(8,128)S(1)} %add.17.own_ref, f32[128,256]{1,0:T(8,128)S(1)} %collective-permute-done.8.other_ref, f32[128,256]{1,0:T(8,128)S(1)} %collective-permute-done.11.old_ref, ...), custom_call_target="tpu_custom_call" | custom-call | flops 301989888 | bytes 3407872 | tf_op jit(solution)/shard_map/pallas_call | solution.py:64
  29.3 0.8 %shard_map.67 = (f32[128,256]{1,0:T(8,128)S(1)}, bf16[128,768]{1,0:T(8,128)(2,1)S(1)}, bf16[128,768]{1,0:T(8,128)(2,1)S(1)}, f32[128,256]{1,0:T(8,128)S(1)}, f32[64,256]{1,0:T(8,128)S(1)}) custom-call(f32[128,256]{1,0:T(8,128)S(1)} %add.17.own_ref, f32[128,256]{1,0:T(8,128)S(1)} %collective-permute-done.8.other_ref, f32[128,256]{1,0:T(8,128)S(1)} %shard_map.64.old_ref, ...), custom_call_target="tpu_custom_call" | custom-call | flops 301989888 | bytes 3473408 | tf_op jit(solution)/shard_map/pallas_call | solution.py:64
  30.5 1.1 %collective-permute-start.16 = (f32[128,256]{1,0:T(8,128)S(1)}, f32[128,256]{1,0:T(8,128)S(1)}, u32[]{:S(2)}, u32[]{:S(2)}) collective-permute-start(f32[128,256]{1,0:T(8,128)S(1)} %add.19), channel_id=1, source_target_pairs={{0,4},{1,5},{2,6},{3,7},{4,8},{5,9},{6,10},{7,11},{8,12},{9,13},{1... | collective-permute-start | bytes 393224 | tf_op jit(solution)/shard_map/ppermute | solution.py:262
  31.6 1.7 %collective-permute-start.17 = (f32[128,256]{1,0:T(8,128)S(1)}, f32[128,256]{1,0:T(8,128)S(1)}, u32[]{:S(2)}, u32[]{:S(2)}) collective-permute-start(f32[128,256]{1,0:T(8,128)S(1)} %add.19), channel_id=1, source_target_pairs={{0,6},{1,7},{2,4},{3,5},{4,10},{5,11},{6,8},{7,9},{8,14},{9,15},{1... | collective-permute-start | bytes 393224 | tf_op jit(solution)/shard_map/ppermute | solution.py:262
  33.3 1.0 %collective-permute-start.14 = (f32[64,256]{1,0:T(8,128)S(1)}, f32[64,256]{1,0:T(8,128)S(1)}, u32[]{:S(2)}, u32[]{:S(2)}) collective-permute-start(f32[64,256]{1,0:T(8,128)S(1)} %get-tuple-element.65), channel_id=1, source_target_pairs={{0,4},{1,5},{2,6},{3,7},{4,8},{5,9},{6,10},{7,11},{8,12},{9,13},{1... | collective-permute-start | bytes 196616 | tf_op jit(solution)/shard_map/ppermute | solution.py:262
  34.9 1.6 %collective-permute-start.12 = (f32[8,128]{1,0:T(8,128)S(1)}, f32[8,128]{1,0:T(8,128)S(1)}, u32[]{:S(2)}, u32[]{:S(2)}) collective-permute-start(f32[8,128]{1,0:T(8,128)S(1)} %get-tuple-element.64), channel_id=1, source_target_pairs={{0,2},{1,3},{2,0},{3,1},{4,6},{5,7},{6,4},{7,5},{8,10},{9,11},{10,... | collective-permute-start | bytes 12296 | tf_op jit(solution)/shard_map/ppermute | solution.py:255
  36.4 2.2 %collective-permute-done.12 = f32[8,128]{1,0:T(8,128)S(1)} collective-permute-done((f32[8,128]{1,0:T(8,128)S(1)}, f32[8,128]{1,0:T(8,128)S(1)}, u32[]{:S(2)}, u32[]{:S(2)}) %collective-permute-start.12) | collective-permute-done | bytes 4128 | tf_op jit(solution)/shard_map/ppermute | solution.py:255
  38.7 3.9 %collective-permute-done.17.refs_1_ = f32[128,256]{1,0:T(8,128)S(1)} collective-permute-done((f32[128,256]{1,0:T(8,128)S(1)}, f32[128,256]{1,0:T(8,128)S(1)}, u32[]{:S(2)}, u32[]{:S(2)}) %collective-permute-start.17) | collective-permute-done | bytes 131104 | tf_op jit(solution)/shard_map/ppermute | solution.py:262
  42.8 1.2 %shard_map.69 = f32[768,256]{1,0:T(8,128)} custom-call(f32[768,256]{1,0:T(8,128)S(1)} %get-tuple-element.50.strip_ref.held_ref, f32[768,256]{1,0:T(8,128)S(1)} %get-tuple-element.63.grad_ref, f32[8,128]{1,0:T(8,128)S(1)} %add.18.refs_0_, f32[8,128]{1,0:T(8,128)S(1)} %collective-permute-done.13.refs_1_), custom_call_target="tpu_custom_call" | custom-call | bytes 2367488 | tf_op jit(solution)/shard_map/pallas_call | solution.py:64
  43.9 0.8 %shard_map.71 = f32[64,256]{1,0:T(8,128)} custom-call(f32[64,256]{1,0:T(8,128)S(1)} %collective-permute-done.14.held_ref, f32[64,256]{1,0:T(8,128)S(1)} %get-tuple-element.68.grad_ref, f32[8,128]{1,0:T(8,128)S(1)} %get-tuple-element.69.refs_0_, f32[8,128]{1,0:T(8,128)S(1)} %collective-permute-done.18.refs_1_), custom_call_target="tpu_custom_call" | custom-call | bytes 204800 | tf_op jit(solution)/shard_map/pallas_call | solution.py:64
  (38 shorter events, 5.0 us)
Async XLA Ops:
  0.6 5.0 %collective-permute-start = (f32[64,256]{1,0:T(8,128)}, f32[64,256]{1,0:T(8,128)S(1)}, u32[]{:S(2)}, u32[]{:S(2)}) collective-permute-start(f32[64,256]{1,0:T(8,128)} %refs_0_.4), channel_id=1, source_target_pairs={{0,1},{1,0},{2,3},{3,2},{4,5},{5,4},{6,7},{7,6},{8,9},{9,8},{10,11... | collective-permute-start | bytes 196616 | tf_op jit(solution)/shard_map/ppermute | solution.py:255
  1.2 5.2 %collective-permute-start.1 = (f32[64,256]{1,0:T(8,128)}, f32[64,256]{1,0:T(8,128)S(1)}, u32[]{:S(2)}, u32[]{:S(2)}) collective-permute-start(f32[64,256]{1,0:T(8,128)} %refs_0_.4), channel_id=1, source_target_pairs={{0,3},{1,2},{2,1},{3,0},{4,7},{5,6},{6,5},{7,4},{8,11},{9,10},{10,... | collective-permute-start | bytes 196616 | tf_op jit(solution)/shard_map/ppermute | solution.py:255
  5.6 1.6 %copy-start.2 = (f32[64,256]{1,0:T(8,128)S(1)}, f32[64,256]{1,0:T(8,128)}, u32[]{:S(2)}) copy-start(f32[64,256]{1,0:T(8,128)} %refs_0_.4) | copy-start | bytes 196612
  7.0 5.2 %collective-permute-start.5 = (f32[128,256]{1,0:T(8,128)S(1)}, f32[128,256]{1,0:T(8,128)S(1)}, u32[]{:S(2)}, u32[]{:S(2)}) collective-permute-start(f32[128,256]{1,0:T(8,128)S(1)} %get-tuple-element.52), channel_id=1, source_target_pairs={{0,1},{1,0},{2,3},{3,2},{4,5},{5,4},{6,7},{7,6},{8,9},{9,8},{10,11... | collective-permute-start | bytes 393224 | tf_op jit(solution)/shard_map/ppermute | solution.py:255
  7.2 4.4 %collective-permute-start.2 = (f32[64,256]{1,0:T(8,128)S(1)}, f32[64,256]{1,0:T(8,128)S(1)}, u32[]{:S(2)}, u32[]{:S(2)}) collective-permute-start(f32[64,256]{1,0:T(8,128)S(1)} %copy-done.2), channel_id=1, source_target_pairs={{0,2},{1,3},{2,0},{3,1},{4,6},{5,7},{6,4},{7,5},{8,10},{9,11},{10,... | collective-permute-start | bytes 196616 | tf_op jit(solution)/shard_map/ppermute | solution.py:255
  8.9 7.6 %collective-permute-start.9 = (f32[64,256]{1,0:T(8,128)S(1)}, f32[64,256]{1,0:T(8,128)S(1)}, u32[]{:S(2)}, u32[]{:S(2)}) collective-permute-start(f32[64,256]{1,0:T(8,128)S(1)} %copy-done.2), channel_id=1, source_target_pairs={{0,4},{1,5},{2,6},{3,7},{4,8},{5,9},{6,10},{7,11},{8,12},{9,13},{1... | collective-permute-start | bytes 196616 | tf_op jit(solution)/shard_map/ppermute | solution.py:262
  11.6 15.1 %copy-start.1 = (s32[2,768,256]{2,1,0:T(8,128)S(1)}, s32[2,768,256]{2,1,0:T(8,128)}, u32[]{:S(2)}) copy-start(s32[2,768,256]{2,1,0:T(8,128)} %refs_1_.3) | copy-start | bytes 4718596
  12.3 14.4 %copy-start = (f32[2,768,256]{2,1,0:T(8,128)S(1)}, f32[2,768,256]{2,1,0:T(8,128)}, u32[]{:S(2)}) copy-start(f32[2,768,256]{2,1,0:T(8,128)} %refs_0_.5) | copy-start | bytes 4718596
  12.3 8.7 %collective-permute-start.6 = (f32[128,256]{1,0:T(8,128)S(1)}, f32[128,256]{1,0:T(8,128)S(1)}, u32[]{:S(2)}, u32[]{:S(2)}) collective-permute-start(f32[128,256]{1,0:T(8,128)S(1)} %add.16), channel_id=1, source_target_pairs={{0,4},{1,5},{2,6},{3,7},{4,8},{5,9},{6,10},{7,11},{8,12},{9,13},{1... | collective-permute-start | bytes 393224 | tf_op jit(solution)/shard_map/ppermute | solution.py:262
  14.0 8.4 %collective-permute-start.7 = (f32[128,256]{1,0:T(8,128)S(1)}, f32[128,256]{1,0:T(8,128)S(1)}, u32[]{:S(2)}, u32[]{:S(2)}) collective-permute-start(f32[128,256]{1,0:T(8,128)S(1)} %add.16), channel_id=1, source_target_pairs={{0,6},{1,7},{2,4},{3,5},{4,10},{5,11},{6,8},{7,9},{8,14},{9,15},{1... | collective-permute-start | bytes 393224 | tf_op jit(solution)/shard_map/ppermute | solution.py:262
  16.5 4.4 %collective-permute-start.10 = (f32[64,256]{1,0:T(8,128)S(1)}, f32[64,256]{1,0:T(8,128)S(1)}, u32[]{:S(2)}, u32[]{:S(2)}) collective-permute-start(f32[64,256]{1,0:T(8,128)S(1)} %collective-permute-done.9.refs_0_), channel_id=1, source_target_pairs={{0,2},{1,3},{2,0},{3,1},{4,6},{5,7},{6,4},{7,5},{8,10},{9,11},{10,... | collective-permute-start | bytes 196616 | tf_op jit(solution)/shard_map/ppermute | solution.py:255
  20.9 7.3 %collective-permute-start.11 = (f32[128,256]{1,0:T(8,128)S(1)}, f32[128,256]{1,0:T(8,128)S(1)}, u32[]{:S(2)}, u32[]{:S(2)}) collective-permute-start(f32[128,256]{1,0:T(8,128)S(1)} %shard_map.64.old_ref), channel_id=1, source_target_pairs={{0,1},{1,0},{2,3},{3,2},{4,5},{5,4},{6,7},{7,6},{8,9},{9,8},{10,11... | collective-permute-start | bytes 393224 | tf_op jit(solution)/shard_map/ppermute | solution.py:255
  22.4 5.9 %collective-permute-start.8 = (f32[128,256]{1,0:T(8,128)S(1)}, f32[128,256]{1,0:T(8,128)S(1)}, u32[]{:S(2)}, u32[]{:S(2)}) collective-permute-start(f32[128,256]{1,0:T(8,128)S(1)} %add.17.own_ref), channel_id=1, source_target_pairs={{0,1},{1,0},{2,3},{3,2},{4,5},{5,4},{6,7},{7,6},{8,9},{9,8},{10,11... | collective-permute-start | bytes 393224 | tf_op jit(solution)/shard_map/ppermute | solution.py:255
  23.0 3.7 %collective-permute-start.3 = (f32[8,128]{1,0:T(8,128)S(1)}, f32[8,128]{1,0:T(8,128)S(1)}, u32[]{:S(2)}, u32[]{:S(2)}) collective-permute-start(f32[8,128]{1,0:T(8,128)S(1)} %get-tuple-element.49), channel_id=1, source_target_pairs={{0,2},{1,3},{2,0},{3,1},{4,6},{5,7},{6,4},{7,5},{8,10},{9,11},{10,... | collective-permute-start | bytes 12296 | tf_op jit(solution)/shard_map/ppermute | solution.py:255
  26.7 1.2 %collective-permute-start.4 = (f32[8,128]{1,0:T(8,128)S(1)}, f32[8,128]{1,0:T(8,128)S(1)}, u32[]{:S(2)}, u32[]{:S(2)}) collective-permute-start(f32[8,128]{1,0:T(8,128)S(1)} %add.15.own_ref), channel_id=1, source_target_pairs={{0,1},{1,0},{2,3},{3,2},{4,5},{5,4},{6,7},{7,6},{8,9},{9,8},{10,11... | collective-permute-start | bytes 12296 | tf_op jit(solution)/shard_map/ppermute | solution.py:255
  29.1 1.4 %collective-permute-start.15 = (f32[128,256]{1,0:T(8,128)S(1)}, f32[128,256]{1,0:T(8,128)S(1)}, u32[]{:S(2)}, u32[]{:S(2)}) collective-permute-start(f32[128,256]{1,0:T(8,128)S(1)} %get-tuple-element.67), channel_id=1, source_target_pairs={{0,1},{1,0},{2,3},{3,2},{4,5},{5,4},{6,7},{7,6},{8,9},{9,8},{10,11... | collective-permute-start | bytes 393224 | tf_op jit(solution)/shard_map/ppermute | solution.py:255
  30.5 8.2 %collective-permute-start.16 = (f32[128,256]{1,0:T(8,128)S(1)}, f32[128,256]{1,0:T(8,128)S(1)}, u32[]{:S(2)}, u32[]{:S(2)}) collective-permute-start(f32[128,256]{1,0:T(8,128)S(1)} %add.19), channel_id=1, source_target_pairs={{0,4},{1,5},{2,6},{3,7},{4,8},{5,9},{6,10},{7,11},{8,12},{9,13},{1... | collective-permute-start | bytes 393224 | tf_op jit(solution)/shard_map/ppermute | solution.py:262
  31.6 11.1 %collective-permute-start.17 = (f32[128,256]{1,0:T(8,128)S(1)}, f32[128,256]{1,0:T(8,128)S(1)}, u32[]{:S(2)}, u32[]{:S(2)}) collective-permute-start(f32[128,256]{1,0:T(8,128)S(1)} %add.19), channel_id=1, source_target_pairs={{0,6},{1,7},{2,4},{3,5},{4,10},{5,11},{6,8},{7,9},{8,14},{9,15},{1... | collective-permute-start | bytes 393224 | tf_op jit(solution)/shard_map/ppermute | solution.py:262
  33.3 10.6 %collective-permute-start.14 = (f32[64,256]{1,0:T(8,128)S(1)}, f32[64,256]{1,0:T(8,128)S(1)}, u32[]{:S(2)}, u32[]{:S(2)}) collective-permute-start(f32[64,256]{1,0:T(8,128)S(1)} %get-tuple-element.65), channel_id=1, source_target_pairs={{0,4},{1,5},{2,6},{3,7},{4,8},{5,9},{6,10},{7,11},{8,12},{9,13},{1... | collective-permute-start | bytes 196616 | tf_op jit(solution)/shard_map/ppermute | solution.py:262
  34.9 3.7 %collective-permute-start.12 = (f32[8,128]{1,0:T(8,128)S(1)}, f32[8,128]{1,0:T(8,128)S(1)}, u32[]{:S(2)}, u32[]{:S(2)}) collective-permute-start(f32[8,128]{1,0:T(8,128)S(1)} %get-tuple-element.64), channel_id=1, source_target_pairs={{0,2},{1,3},{2,0},{3,1},{4,6},{5,7},{6,4},{7,5},{8,10},{9,11},{10,... | collective-permute-start | bytes 12296 | tf_op jit(solution)/shard_map/ppermute | solution.py:255
  38.6 4.2 %collective-permute-start.13 = (f32[8,128]{1,0:T(8,128)S(1)}, f32[8,128]{1,0:T(8,128)S(1)}, u32[]{:S(2)}, u32[]{:S(2)}) collective-permute-start(f32[8,128]{1,0:T(8,128)S(1)} %add.18.refs_0_), channel_id=1, source_target_pairs={{0,1},{1,0},{2,3},{3,2},{4,5},{5,4},{6,7},{7,6},{8,9},{9,8},{10,11... | collective-permute-start | bytes 12296 | tf_op jit(solution)/shard_map/ppermute | solution.py:255
  42.7 1.2 %collective-permute-start.18 = (f32[8,128]{1,0:T(8,128)S(1)}, f32[8,128]{1,0:T(8,128)S(1)}, u32[]{:S(2)}, u32[]{:S(2)}) collective-permute-start(f32[8,128]{1,0:T(8,128)S(1)} %get-tuple-element.69.refs_0_), channel_id=1, source_target_pairs={{0,1},{1,0},{2,3},{3,2},{4,5},{5,4},{6,7},{7,6},{8,9},{9,8},{10,11... | collective-permute-start | bytes 12296 | tf_op jit(solution)/shard_map/ppermute | solution.py:255

commit v7 on v6

--- a/solution.py
+++ b/solution.py
@@ -38,6 +38,10 @@
         lax.dot_general, dimension_numbers=dims, preferred_element_type=F32
     )
     (a_high, a_low), (b_high, b_low) = a, b
+    if dims == NN:
+        rows = a_high.shape[0]
+        both = dot(jnp.concatenate([a_high, a_low], 0), b_high)
+        return both[:rows] + (dot(a_high, b_low) + both[rows:])
     return dot(a_high, b_high) + (dot(a_high, b_low) + dot(a_low, b_high))
 
 
@@ -116,7 +120,7 @@
         seen = jnp.where(buffers[1][chunk, :] != 0, buffers[0][chunk, :], HIDDEN)
         turned = seen.T
         for at in range(nx * CORES):
-            own = jnp.where(core == at % CORES, nx, 0)
+            own = jnp.where(core == (at + stratum) % CORES, nx, 0)
             rows = aligned(own + at // CORES, share)
             outs[0][rows, chunk] = turned[at * share : (at + 1) * share]
         if with_strip:
@@ -256,7 +260,7 @@
 
     def onward(value, dx):
         pairs = [
-            (b * n + a, (b + 1) % blocks * n + moved(a, dx, 0))
+            (b * n + a, (b + 1) % blocks * n + moved(a, dx, 1))
             for b in range(blocks) for a in range(n)
         ]
         return lax.ppermute(value, ("blk", "sub"), pairs)
@@ -273,7 +277,9 @@
         outs = [shape(dates, pixels)]
         if len(args) == 3:
             outs += strip_shapes
-        scratch = [pltpu.VMEM((pixels, args[0].shape[2]), kind) for kind in kinds]
+        scratch = [
+            pltpu.VMEM((pixels, a.shape[-1]), kind) for a, kind in zip(args, kinds)
+        ]
         scratch.append(pltpu.SemaphoreType.DMA((len(chunks_of(pixels)), len(args))))
         return call(
             functools.partial(prepare_kernel, stratum, share), outs, *args,
@@ -300,7 +306,7 @@
         gradient_kernel, [shape(pixels, rank), shape(8, 128)],
         strip, h0, l0, h1, l1, b0, b1, flops=6 * work,
     )
-    tiles = chips(tile)
+    tiles = [tile] + [within(tile, dx, 1) for dx in range(1, nx)]
     tile = sum(tiles[1:], tiles[0])
     other_tile = within(tile, 0, 1)
     olds = chips(old)
@@ -331,7 +337,7 @@
         gradient_kernel, [shape(pixels, rank), shape(8, 128)],
         strip, h0, l0, h1, l1, b0, b1, flops=6 * work,
     )
-    tiles = chips(tile)
+    tiles = [tile] + [within(tile, dx, 1) for dx in range(1, nx)]
     tile = sum(tiles[1:], tiles[0])
     other_tile = within(tile, 0, 1)
     strip, = call(

time: 44.8 us -> 44 us (0.982)
  starting transfers between devices: 19 us -> 17.5 us
  waiting for transfers between devices: 16.1 us -> 16.7 us
    ppermute x6, starting transfers between devices: 9.58 us -> 7.8 us  [onward(): return lax.ppermute(value, ('blk', 'sub'), pairs)]
  transfers between devices with their start and end apart: 19 -> 19, of which waited for: 10 -> 9; matrix products, arithmetic and copies ran while one was open for 0% -> 0% of each run, Pallas kernels for 15% -> 15%
where the time goes in v7:
time: 44 us; the launch traced here: 43.8 us
  starting transfers between devices  17.5 us (40%)
  waiting for transfers between devices  16.7 us (38%)
  Pallas kernels  8.77 us (20%)
  between operations  0.8 us (2%)
    ppermute x13, waiting for transfers between devices, within(): return lax.ppermute(value, 'sub', pairs)  11.1 us
    ppermute x13, starting transfers between devices, within(): return lax.ppermute(value, 'sub', pairs)  9.7 us
    pallas_call x13, Pallas kernels, call(): pl.pallas_call(kernel, out_shape=outs, in_specs=[where] * len(args), out_...  8.77 us
    ppermute x6, starting transfers between devices, onward(): return lax.ppermute(value, ('blk', 'sub'), pairs)  7.8 us
    ppermute x6, waiting for transfers between devices, onward(): return lax.ppermute(value, ('blk', 'sub'), pairs)  5.56 us
  transfers between devices with their start and end apart: 19, of which 9 were waited for; matrix products, arithmetic and copies ran while one was open for 0% of the time, Pallas kernels for 15%

profile of v7, /device:TPU:0, one launch (start us, length us, event | category | flops | bytes accessed | tf_op | source)
XLA Modules:
  0.0 43.8 jit_solution(1150829170809169865)
XLA Ops:
  1.2 2.6 %collective-permute-start.1 = (f32[64,256]{1,0:T(8,128)}, f32[64,256]{1,0:T(8,128)S(1)}, u32[]{:S(2)}, u32[]{:S(2)}) collective-permute-start(f32[64,256]{1,0:T(8,128)} %refs_0_.4), channel_id=1, source_target_pairs={{0,3},{1,2},{2,1},{3,0},{4,7},{5,6},{6,5},{7,4},{8,11},{9,10},{10,... | collective-permute-start | bytes 196616 | tf_op jit(solution)/shard_map/ppermute | solution.py:259
  3.8 1.9 %shard_map.59 = (f32[256,768]{1,0:T(8,128)S(1)}, f32[768,256]{1,0:T(8,128)S(1)}, bf16[768,256]{1,0:T(8,128)(2,1)S(1)}, bf16[768,256]{1,0:T(8,128)(2,1)S(1)}, bf1...) custom-call(f32[2,768,256]{2,1,0:T(8,128)} %refs_0_.5, s32[2,768,256]{2,1,0:T(8,128)} %refs_1_.3, f32[768,256]{1,0:T(8,128)} %refs_2_.1), custom_call_target="tpu_custom_call" | custom-call | bytes 7077888 | tf_op jit(solution)/shard_map/pallas_call | solution.py:68
  5.7 0.7 %collective-permute-done.1.refs_1_ = f32[64,256]{1,0:T(8,128)S(1)} collective-permute-done((f32[64,256]{1,0:T(8,128)}, f32[64,256]{1,0:T(8,128)S(1)}, u32[]{:S(2)}, u32[]{:S(2)}) %collective-permute-start.1) | collective-permute-done | bytes 65568 | tf_op jit(solution)/shard_map/ppermute | solution.py:259
  6.4 0.6 %shard_map.60 = (f32[128,256]{1,0:T(8,128)S(1)}, bf16[128,768]{1,0:T(8,128)(2,1)S(1)}, bf16[128,768]{1,0:T(8,128)(2,1)S(1)}, f32[128,256]{1,0:T(8,128)S(1)}) custom-call(f32[64,256]{1,0:T(8,128)S(1)} %collective-permute-done.refs_0_, f32[64,256]{1,0:T(8,128)S(1)} %collective-permute-done.1.refs_1_, f32[256,768]{1,0:T(8,128)S(1)} %get-tuple-element.37.refs_2_, ...), custom_call_target="tpu_custom_call" | custom-call | flops 301989888 | bytes 3145728 | tf_op jit(solution)/shard_map/pallas_call | solution.py:68
  7.2 1.7 %collective-permute-start.2 = (f32[64,256]{1,0:T(8,128)S(1)}, f32[64,256]{1,0:T(8,128)S(1)}, u32[]{:S(2)}, u32[]{:S(2)}) collective-permute-start(f32[64,256]{1,0:T(8,128)S(1)} %copy-done.2), channel_id=1, source_target_pairs={{0,2},{1,3},{2,0},{3,1},{4,6},{5,7},{6,4},{7,5},{8,10},{9,11},{10,... | collective-permute-start | bytes 196616 | tf_op jit(solution)/shard_map/ppermute | solution.py:259
  8.9 1.0 %collective-permute-start.9 = (f32[64,256]{1,0:T(8,128)S(1)}, f32[64,256]{1,0:T(8,128)S(1)}, u32[]{:S(2)}, u32[]{:S(2)}) collective-permute-start(f32[64,256]{1,0:T(8,128)S(1)} %copy-done.2), channel_id=1, source_target_pairs={{0,5},{1,4},{2,7},{3,6},{4,9},{5,8},{6,11},{7,10},{8,13},{9,12},{1... | collective-permute-start | bytes 196616 | tf_op jit(solution)/shard_map/ppermute | solution.py:266
  9.9 1.7 %collective-permute-done.2.refs_1_ = f32[64,256]{1,0:T(8,128)S(1)} collective-permute-done((f32[64,256]{1,0:T(8,128)S(1)}, f32[64,256]{1,0:T(8,128)S(1)}, u32[]{:S(2)}, u32[]{:S(2)}) %collective-permute-start.2) | collective-permute-done | bytes 65568 | tf_op jit(solution)/shard_map/ppermute | solution.py:259
  11.6 0.6 %shard_map.61 = (f32[128,256]{1,0:T(8,128)S(1)}, bf16[128,768]{1,0:T(8,128)(2,1)S(1)}, bf16[128,768]{1,0:T(8,128)(2,1)S(1)}, f32[128,256]{1,0:T(8,128)S(1)}) custom-call(f32[64,256]{1,0:T(8,128)S(1)} %copy-done.2, f32[64,256]{1,0:T(8,128)S(1)} %collective-permute-done.2.refs_1_, f32[256,768]{1,0:T(8,128)S(1)} %get-tuple-element.37.refs_2_, ...), custom_call_target="tpu_custom_call" | custom-call | flops 301989888 | bytes 3145728 | tf_op jit(solution)/shard_map/pallas_call | solution.py:68
  12.5 3.7 %collective-permute-start.7 = (f32[128,256]{1,0:T(8,128)S(1)}, f32[128,256]{1,0:T(8,128)S(1)}, u32[]{:S(2)}, u32[]{:S(2)}) collective-permute-start(f32[128,256]{1,0:T(8,128)S(1)} %add.16), channel_id=1, source_target_pairs={{0,7},{1,6},{2,5},{3,4},{4,11},{5,10},{6,9},{7,8},{8,15},{9,14},{1... | collective-permute-start | bytes 393224 | tf_op jit(solution)/shard_map/ppermute | solution.py:266
  16.8 3.7 %collective-permute-done.10.refs_1_ = f32[64,256]{1,0:T(8,128)S(1)} collective-permute-done((f32[64,256]{1,0:T(8,128)S(1)}, f32[64,256]{1,0:T(8,128)S(1)}, u32[]{:S(2)}, u32[]{:S(2)}) %collective-permute-start.10) | collective-permute-done | bytes 65568 | tf_op jit(solution)/shard_map/ppermute | solution.py:259
  20.6 2.8 %collective-permute-done.7 = f32[128,256]{1,0:T(8,128)S(1)} collective-permute-done((f32[128,256]{1,0:T(8,128)S(1)}, f32[128,256]{1,0:T(8,128)S(1)}, u32[]{:S(2)}, u32[]{:S(2)}) %collective-permute-start.7) | collective-permute-done | bytes 131104 | tf_op jit(solution)/shard_map/ppermute | solution.py:266
  24.6 2.7 %collective-permute-done.3 = f32[8,128]{1,0:T(8,128)S(1)} collective-permute-done((f32[8,128]{1,0:T(8,128)S(1)}, f32[8,128]{1,0:T(8,128)S(1)}, u32[]{:S(2)}, u32[]{:S(2)}) %collective-permute-start.3) | collective-permute-done | bytes 4128 | tf_op jit(solution)/shard_map/ppermute | solution.py:259
  27.6 0.6 %shard_map.65.refs_0_ = f32[256,768]{1,0:T(8,128)S(1)} custom-call(f32[2,768,256]{2,1,0:T(8,128)S(1)} %copy-done, s32[2,768,256]{2,1,0:T(8,128)S(1)} %copy-done.1), custom_call_target="tpu_custom_call" | custom-call | bytes 3932160 | tf_op jit(solution)/shard_map/pallas_call | solution.py:68
  28.9 0.8 %shard_map.66 = (f32[128,256]{1,0:T(8,128)S(1)}, bf16[128,768]{1,0:T(8,128)(2,1)S(1)}, bf16[128,768]{1,0:T(8,128)(2,1)S(1)}, f32[128,256]{1,0:T(8,128)S(1)}) custom-call(f32[128,256]{1,0:T(8,128)S(1)} %add.17.own_ref, f32[128,256]{1,0:T(8,128)S(1)} %collective-permute-done.8.other_ref, f32[128,256]{1,0:T(8,128)S(1)} %collective-permute-done.11.old_ref, ...), custom_call_target="tpu_custom_call" | custom-call | flops 301989888 | bytes 3407872 | tf_op jit(solution)/shard_map/pallas_call | solution.py:68
  30.1 0.8 %shard_map.67 = (f32[128,256]{1,0:T(8,128)S(1)}, bf16[128,768]{1,0:T(8,128)(2,1)S(1)}, bf16[128,768]{1,0:T(8,128)(2,1)S(1)}, f32[128,256]{1,0:T(8,128)S(1)}, f32[64,256]{1,0:T(8,128)S(1)}) custom-call(f32[128,256]{1,0:T(8,128)S(1)} %add.17.own_ref, f32[128,256]{1,0:T(8,128)S(1)} %collective-permute-done.8.other_ref, f32[128,256]{1,0:T(8,128)S(1)} %shard_map.64.old_ref, ...), custom_call_target="tpu_custom_call" | custom-call | flops 301989888 | bytes 3473408 | tf_op jit(solution)/shard_map/pallas_call | solution.py:68
  31.6 1.4 %collective-permute-start.17 = (f32[128,256]{1,0:T(8,128)S(1)}, f32[128,256]{1,0:T(8,128)S(1)}, u32[]{:S(2)}, u32[]{:S(2)}) collective-permute-start(f32[128,256]{1,0:T(8,128)S(1)} %add.19), channel_id=1, source_target_pairs={{0,7},{1,6},{2,5},{3,4},{4,11},{5,10},{6,9},{7,8},{8,15},{9,14},{1... | collective-permute-start | bytes 393224 | tf_op jit(solution)/shard_map/ppermute | solution.py:266
  33.0 1.0 %collective-permute-start.14 = (f32[64,256]{1,0:T(8,128)S(1)}, f32[64,256]{1,0:T(8,128)S(1)}, u32[]{:S(2)}, u32[]{:S(2)}) collective-permute-start(f32[64,256]{1,0:T(8,128)S(1)} %get-tuple-element.65), channel_id=1, source_target_pairs={{0,5},{1,4},{2,7},{3,6},{4,9},{5,8},{6,11},{7,10},{8,13},{9,12},{1... | collective-permute-start | bytes 196616 | tf_op jit(solution)/shard_map/ppermute | solution.py:266
  34.6 1.3 %collective-permute-start.12 = (f32[8,128]{1,0:T(8,128)S(1)}, f32[8,128]{1,0:T(8,128)S(1)}, u32[]{:S(2)}, u32[]{:S(2)}) collective-permute-start(f32[8,128]{1,0:T(8,128)S(1)} %get-tuple-element.64), channel_id=1, source_target_pairs={{0,3},{1,2},{2,1},{3,0},{4,7},{5,6},{6,5},{7,4},{8,11},{9,10},{10,... | collective-permute-start | bytes 12296 | tf_op jit(solution)/shard_map/ppermute | solution.py:259
  35.9 1.8 %collective-permute-done.12 = f32[8,128]{1,0:T(8,128)S(1)} collective-permute-done((f32[8,128]{1,0:T(8,128)S(1)}, f32[8,128]{1,0:T(8,128)S(1)}, u32[]{:S(2)}, u32[]{:S(2)}) %collective-permute-start.12) | collective-permute-done | bytes 4128 | tf_op jit(solution)/shard_map/ppermute | solution.py:259
  37.7 0.6 %collective-permute-start.13 = (f32[8,128]{1,0:T(8,128)S(1)}, f32[8,128]{1,0:T(8,128)S(1)}, u32[]{:S(2)}, u32[]{:S(2)}) collective-permute-start(f32[8,128]{1,0:T(8,128)S(1)} %add.18.refs_0_), channel_id=1, source_target_pairs={{0,1},{1,0},{2,3},{3,2},{4,5},{5,4},{6,7},{7,6},{8,9},{9,8},{10,11... | collective-permute-start | bytes 12296 | tf_op jit(solution)/shard_map/ppermute | solution.py:259
  38.3 2.8 %collective-permute-done.17.refs_1_ = f32[128,256]{1,0:T(8,128)S(1)} collective-permute-done((f32[128,256]{1,0:T(8,128)S(1)}, f32[128,256]{1,0:T(8,128)S(1)}, u32[]{:S(2)}, u32[]{:S(2)}) %collective-permute-start.17) | collective-permute-done | bytes 131104 | tf_op jit(solution)/shard_map/ppermute | solution.py:266
  41.1 0.8 %collective-permute-start.18 = (f32[8,128]{1,0:T(8,128)S(1)}, f32[8,128]{1,0:T(8,128)S(1)}, u32[]{:S(2)}, u32[]{:S(2)}) collective-permute-start(f32[8,128]{1,0:T(8,128)S(1)} %get-tuple-element.69.refs_0_), channel_id=1, source_target_pairs={{0,1},{1,0},{2,3},{3,2},{4,5},{5,4},{6,7},{7,6},{8,9},{9,8},{10,11... | collective-permute-start | bytes 12296 | tf_op jit(solution)/shard_map/ppermute | solution.py:259
  41.9 1.2 %shard_map.69 = f32[768,256]{1,0:T(8,128)} custom-call(f32[768,256]{1,0:T(8,128)S(1)} %get-tuple-element.50.strip_ref.held_ref, f32[768,256]{1,0:T(8,128)S(1)} %get-tuple-element.63.grad_ref, f32[8,128]{1,0:T(8,128)S(1)} %add.18.refs_0_, f32[8,128]{1,0:T(8,128)S(1)} %collective-permute-done.13.refs_1_), custom_call_target="tpu_custom_call" | custom-call | bytes 2367488 | tf_op jit(solution)/shard_map/pallas_call | solution.py:68
  43.0 0.8 %shard_map.71 = f32[64,256]{1,0:T(8,128)} custom-call(f32[64,256]{1,0:T(8,128)S(1)} %collective-permute-done.14.held_ref, f32[64,256]{1,0:T(8,128)S(1)} %get-tuple-element.68.grad_ref, f32[8,128]{1,0:T(8,128)S(1)} %get-tuple-element.69.refs_0_, f32[8,128]{1,0:T(8,128)S(1)} %collective-permute-done.18.refs_1_), custom_call_target="tpu_custom_call" | custom-call | bytes 204800 | tf_op jit(solution)/shard_map/pallas_call | solution.py:68
  (38 shorter events, 5.4 us)
Async XLA Ops:
  0.6 5.0 %collective-permute-start = (f32[64,256]{1,0:T(8,128)}, f32[64,256]{1,0:T(8,128)S(1)}, u32[]{:S(2)}, u32[]{:S(2)}) collective-permute-start(f32[64,256]{1,0:T(8,128)} %refs_0_.4), channel_id=1, source_target_pairs={{0,1},{1,0},{2,3},{3,2},{4,5},{5,4},{6,7},{7,6},{8,9},{9,8},{10,11... | collective-permute-start | bytes 196616 | tf_op jit(solution)/shard_map/ppermute | solution.py:259
  1.2 5.2 %collective-permute-start.1 = (f32[64,256]{1,0:T(8,128)}, f32[64,256]{1,0:T(8,128)S(1)}, u32[]{:S(2)}, u32[]{:S(2)}) collective-permute-start(f32[64,256]{1,0:T(8,128)} %refs_0_.4), channel_id=1, source_target_pairs={{0,3},{1,2},{2,1},{3,0},{4,7},{5,6},{6,5},{7,4},{8,11},{9,10},{10,... | collective-permute-start | bytes 196616 | tf_op jit(solution)/shard_map/ppermute | solution.py:259
  5.6 1.6 %copy-start.2 = (f32[64,256]{1,0:T(8,128)S(1)}, f32[64,256]{1,0:T(8,128)}, u32[]{:S(2)}) copy-start(f32[64,256]{1,0:T(8,128)} %refs_0_.4) | copy-start | bytes 196612
  7.0 5.3 %collective-permute-start.5 = (f32[128,256]{1,0:T(8,128)S(1)}, f32[128,256]{1,0:T(8,128)S(1)}, u32[]{:S(2)}, u32[]{:S(2)}) collective-permute-start(f32[128,256]{1,0:T(8,128)S(1)} %get-tuple-element.52), channel_id=1, source_target_pairs={{0,1},{1,0},{2,3},{3,2},{4,5},{5,4},{6,7},{7,6},{8,9},{9,8},{10,11... | collective-permute-start | bytes 393224 | tf_op jit(solution)/shard_map/ppermute | solution.py:259
  7.2 4.4 %collective-permute-start.2 = (f32[64,256]{1,0:T(8,128)S(1)}, f32[64,256]{1,0:T(8,128)S(1)}, u32[]{:S(2)}, u32[]{:S(2)}) collective-permute-start(f32[64,256]{1,0:T(8,128)S(1)} %copy-done.2), channel_id=1, source_target_pairs={{0,2},{1,3},{2,0},{3,1},{4,6},{5,7},{6,4},{7,5},{8,10},{9,11},{10,... | collective-permute-start | bytes 196616 | tf_op jit(solution)/shard_map/ppermute | solution.py:259
  8.9 7.3 %collective-permute-start.9 = (f32[64,256]{1,0:T(8,128)S(1)}, f32[64,256]{1,0:T(8,128)S(1)}, u32[]{:S(2)}, u32[]{:S(2)}) collective-permute-start(f32[64,256]{1,0:T(8,128)S(1)} %copy-done.2), channel_id=1, source_target_pairs={{0,5},{1,4},{2,7},{3,6},{4,9},{5,8},{6,11},{7,10},{8,13},{9,12},{1... | collective-permute-start | bytes 196616 | tf_op jit(solution)/shard_map/ppermute | solution.py:266
  11.6 16.0 %copy-start.1 = (s32[2,768,256]{2,1,0:T(8,128)S(1)}, s32[2,768,256]{2,1,0:T(8,128)}, u32[]{:S(2)}) copy-start(s32[2,768,256]{2,1,0:T(8,128)} %refs_1_.3) | copy-start | bytes 4718596
  12.3 15.4 %copy-start = (f32[2,768,256]{2,1,0:T(8,128)S(1)}, f32[2,768,256]{2,1,0:T(8,128)}, u32[]{:S(2)}) copy-start(f32[2,768,256]{2,1,0:T(8,128)} %refs_0_.5) | copy-start | bytes 4718596
  12.3 8.3 %collective-permute-start.6 = (f32[128,256]{1,0:T(8,128)S(1)}, f32[128,256]{1,0:T(8,128)S(1)}, u32[]{:S(2)}, u32[]{:S(2)}) collective-permute-start(f32[128,256]{1,0:T(8,128)S(1)} %add.16), channel_id=1, source_target_pairs={{0,5},{1,4},{2,7},{3,6},{4,9},{5,8},{6,11},{7,10},{8,13},{9,12},{1... | collective-permute-start | bytes 393224 | tf_op jit(solution)/shard_map/ppermute | solution.py:266
  12.5 10.9 %collective-permute-start.7 = (f32[128,256]{1,0:T(8,128)S(1)}, f32[128,256]{1,0:T(8,128)S(1)}, u32[]{:S(2)}, u32[]{:S(2)}) collective-permute-start(f32[128,256]{1,0:T(8,128)S(1)} %add.16), channel_id=1, source_target_pairs={{0,7},{1,6},{2,5},{3,4},{4,11},{5,10},{6,9},{7,8},{8,15},{9,14},{1... | collective-permute-start | bytes 393224 | tf_op jit(solution)/shard_map/ppermute | solution.py:266
  16.2 4.3 %collective-permute-start.10 = (f32[64,256]{1,0:T(8,128)S(1)}, f32[64,256]{1,0:T(8,128)S(1)}, u32[]{:S(2)}, u32[]{:S(2)}) collective-permute-start(f32[64,256]{1,0:T(8,128)S(1)} %collective-permute-done.9.refs_0_), channel_id=1, source_target_pairs={{0,2},{1,3},{2,0},{3,1},{4,6},{5,7},{6,4},{7,5},{8,10},{9,11},{10,... | collective-permute-start | bytes 196616 | tf_op jit(solution)/shard_map/ppermute | solution.py:259
  20.5 8.4 %collective-permute-start.11 = (f32[128,256]{1,0:T(8,128)S(1)}, f32[128,256]{1,0:T(8,128)S(1)}, u32[]{:S(2)}, u32[]{:S(2)}) collective-permute-start(f32[128,256]{1,0:T(8,128)S(1)} %shard_map.64.old_ref), channel_id=1, source_target_pairs={{0,1},{1,0},{2,3},{3,2},{4,5},{5,4},{6,7},{7,6},{8,9},{9,8},{10,11... | collective-permute-start | bytes 393224 | tf_op jit(solution)/shard_map/ppermute | solution.py:259
  23.4 5.5 %collective-permute-start.8 = (f32[128,256]{1,0:T(8,128)S(1)}, f32[128,256]{1,0:T(8,128)S(1)}, u32[]{:S(2)}, u32[]{:S(2)}) collective-permute-start(f32[128,256]{1,0:T(8,128)S(1)} %add.17.own_ref), channel_id=1, source_target_pairs={{0,1},{1,0},{2,3},{3,2},{4,5},{5,4},{6,7},{7,6},{8,9},{9,8},{10,11... | collective-permute-start | bytes 393224 | tf_op jit(solution)/shard_map/ppermute | solution.py:259
  24.2 3.1 %collective-permute-start.3 = (f32[8,128]{1,0:T(8,128)S(1)}, f32[8,128]{1,0:T(8,128)S(1)}, u32[]{:S(2)}, u32[]{:S(2)}) collective-permute-start(f32[8,128]{1,0:T(8,128)S(1)} %get-tuple-element.49), channel_id=1, source_target_pairs={{0,3},{1,2},{2,1},{3,0},{4,7},{5,6},{6,5},{7,4},{8,11},{9,10},{10,... | collective-permute-start | bytes 12296 | tf_op jit(solution)/shard_map/ppermute | solution.py:259
  27.3 1.2 %collective-permute-start.4 = (f32[8,128]{1,0:T(8,128)S(1)}, f32[8,128]{1,0:T(8,128)S(1)}, u32[]{:S(2)}, u32[]{:S(2)}) collective-permute-start(f32[8,128]{1,0:T(8,128)S(1)} %add.15.own_ref), channel_id=1, source_target_pairs={{0,1},{1,0},{2,3},{3,2},{4,5},{5,4},{6,7},{7,6},{8,9},{9,8},{10,11... | collective-permute-start | bytes 12296 | tf_op jit(solution)/shard_map/ppermute | solution.py:259
  29.7 1.4 %collective-permute-start.15 = (f32[128,256]{1,0:T(8,128)S(1)}, f32[128,256]{1,0:T(8,128)S(1)}, u32[]{:S(2)}, u32[]{:S(2)}) collective-permute-start(f32[128,256]{1,0:T(8,128)S(1)} %get-tuple-element.67), channel_id=1, source_target_pairs={{0,1},{1,0},{2,3},{3,2},{4,5},{5,4},{6,7},{7,6},{8,9},{9,8},{10,11... | collective-permute-start | bytes 393224 | tf_op jit(solution)/shard_map/ppermute | solution.py:259
  31.2 7.2 %collective-permute-start.16 = (f32[128,256]{1,0:T(8,128)S(1)}, f32[128,256]{1,0:T(8,128)S(1)}, u32[]{:S(2)}, u32[]{:S(2)}) collective-permute-start(f32[128,256]{1,0:T(8,128)S(1)} %add.19), channel_id=1, source_target_pairs={{0,5},{1,4},{2,7},{3,6},{4,9},{5,8},{6,11},{7,10},{8,13},{9,12},{1... | collective-permute-start | bytes 393224 | tf_op jit(solution)/shard_map/ppermute | solution.py:266
  31.6 9.5 %collective-permute-start.17 = (f32[128,256]{1,0:T(8,128)S(1)}, f32[128,256]{1,0:T(8,128)S(1)}, u32[]{:S(2)}, u32[]{:S(2)}) collective-permute-start(f32[128,256]{1,0:T(8,128)S(1)} %add.19), channel_id=1, source_target_pairs={{0,7},{1,6},{2,5},{3,4},{4,11},{5,10},{6,9},{7,8},{8,15},{9,14},{1... | collective-permute-start | bytes 393224 | tf_op jit(solution)/shard_map/ppermute | solution.py:266
  33.0 10.0 %collective-permute-start.14 = (f32[64,256]{1,0:T(8,128)S(1)}, f32[64,256]{1,0:T(8,128)S(1)}, u32[]{:S(2)}, u32[]{:S(2)}) collective-permute-start(f32[64,256]{1,0:T(8,128)S(1)} %get-tuple-element.65), channel_id=1, source_target_pairs={{0,5},{1,4},{2,7},{3,6},{4,9},{5,8},{6,11},{7,10},{8,13},{9,12},{1... | collective-permute-start | bytes 196616 | tf_op jit(solution)/shard_map/ppermute | solution.py:266
  34.6 3.1 %collective-permute-start.12 = (f32[8,128]{1,0:T(8,128)S(1)}, f32[8,128]{1,0:T(8,128)S(1)}, u32[]{:S(2)}, u32[]{:S(2)}) collective-permute-start(f32[8,128]{1,0:T(8,128)S(1)} %get-tuple-element.64), channel_id=1, source_target_pairs={{0,3},{1,2},{2,1},{3,0},{4,7},{5,6},{6,5},{7,4},{8,11},{9,10},{10,... | collective-permute-start | bytes 12296 | tf_op jit(solution)/shard_map/ppermute | solution.py:259
  37.7 4.2 %collective-permute-start.13 = (f32[8,128]{1,0:T(8,128)S(1)}, f32[8,128]{1,0:T(8,128)S(1)}, u32[]{:S(2)}, u32[]{:S(2)}) collective-permute-start(f32[8,128]{1,0:T(8,128)S(1)} %add.18.refs_0_), channel_id=1, source_target_pairs={{0,1},{1,0},{2,3},{3,2},{4,5},{5,4},{6,7},{7,6},{8,9},{9,8},{10,11... | collective-permute-start | bytes 12296 | tf_op jit(solution)/shard_map/ppermute | solution.py:259
  41.1 1.9 %collective-permute-start.18 = (f32[8,128]{1,0:T(8,128)S(1)}, f32[8,128]{1,0:T(8,128)S(1)}, u32[]{:S(2)}, u32[]{:S(2)}) collective-permute-start(f32[8,128]{1,0:T(8,128)S(1)} %get-tuple-element.69.refs_0_), channel_id=1, source_target_pairs={{0,1},{1,0},{2,3},{3,2},{4,5},{5,4},{6,7},{7,6},{8,9},{9,8},{10,11... | collective-permute-start | bytes 12296 | tf_op jit(solution)/shard_map/ppermute | solution.py:259

commit v8 on v7

--- a/solution.py
+++ b/solution.py
@@ -38,10 +38,6 @@
         lax.dot_general, dimension_numbers=dims, preferred_element_type=F32
     )
     (a_high, a_low), (b_high, b_low) = a, b
-    if dims == NN:
-        rows = a_high.shape[0]
-        both = dot(jnp.concatenate([a_high, a_low], 0), b_high)
-        return both[:rows] + (dot(a_high, b_low) + both[rows:])
     return dot(a_high, b_high) + (dot(a_high, b_low) + dot(a_low, b_high))
 
 
@@ -183,21 +179,22 @@
     return step_of([tile_squares(own_ref[...]), tile_squares(other_ref[...])], count)
 
 
-def later_send_kernel(count, own_ref, other_ref, old_ref, *refs):
-    problem, (send_ref, high_ref, low_ref, block_ref) = refs[:5], refs[5:]
+def later_send_kernel(count, share, own_ref, other_ref, old_own_ref, old_ref, *refs):
+    problem, (send_ref, high_ref, low_ref, block_ref, share_ref) = refs[:5], refs[5:]
     step = later_step(count, own_ref, other_ref)
+    chip, _ = place()
+    rows = aligned(chip, share)
+    share_ref[...] = old_own_ref[rows, :] - step * own_ref[rows, :]
     block = old_ref[...] - step * other_ref[...]
     block_ref[...] = block
     send_ref[...] = errors_and_part(0, problem, block, high_ref, low_ref)
 
 
-def later_keep_kernel(count, share, own_ref, other_ref, old_ref, *refs):
-    problem, (keep_ref, high_ref, low_ref, block_ref, share_ref) = refs[:5], refs[5:]
+def later_keep_kernel(count, own_ref, other_ref, old_ref, *refs):
+    problem, (keep_ref, high_ref, low_ref, block_ref) = refs[:5], refs[5:]
     step = later_step(count, own_ref, other_ref)
     block = old_ref[...] - step * own_ref[...]
     block_ref[...] = block
-    chip, _ = place()
-    share_ref[...] = block_ref[aligned(chip, share), :]
     part = errors_and_part(1, problem, block, high_ref, low_ref)
     keep_ref[...] = with_ridge(part, block)
 
@@ -319,20 +316,21 @@
     own_grad = sum(came[1:], came[0])
     other_grad = within(own_grad, 0, 1)
 
-    send, h0, l0, b0 = call(
-        functools.partial(later_send_kernel, date_count),
+    send, h0, l0, b0, own = call(
+        functools.partial(later_send_kernel, date_count, share),
+        part_shapes + [shape(half, rank), shape(share, rank)],
+        own_grad, other_grad, old_half, old_other, values_1, *halves,
+        flops=6 * work,
+    )
+    got = within(send, 0, 1)
+    held = onward(own, 0)
+    keep, h1, l1, b1 = call(
+        functools.partial(later_keep_kernel, date_count),
         part_shapes + [shape(half, rank)],
-        own_grad, other_grad, old_other, values_1, *halves, flops=6 * work,
-    )
-    got = within(send, 0, 1)
-    keep, h1, l1, b1, own = call(
-        functools.partial(later_keep_kernel, date_count, share),
-        part_shapes + [shape(half, rank), shape(share, rank)],
         own_grad, other_grad, old_half, values_1, *halves, flops=6 * work,
     )
     mine = keep + got
     came = [onward(mine, dx) for dx in range(nx)]
-    held = onward(own, 0)
     grad, tile = call(
         gradient_kernel, [shape(pixels, rank), shape(8, 128)],
         strip, h0, l0, h1, l1, b0, b1, flops=6 * work,

time: 44 us -> 43.9 us (level)
  no operation moved by 1% of the time
where the time goes in v8:
time: 43.9 us; the launch traced here: 43.8 us
  starting transfers between devices  17.5 us (40%)
  waiting for transfers between devices  16.7 us (38%)
  Pallas kernels  8.75 us (20%)
  between operations  0.8 us (2%)
    ppermute x13, waiting for transfers between devices, within(): return lax.ppermute(value, 'sub', pairs)  11.1 us
    ppermute x13, starting transfers between devices, within(): return lax.ppermute(value, 'sub', pairs)  9.68 us
    pallas_call x13, Pallas kernels, call(): pl.pallas_call(kernel, out_shape=outs, in_specs=[where] * len(args), out_...  8.75 us
    ppermute x6, starting transfers between devices, onward(): return lax.ppermute(value, ('blk', 'sub'), pairs)  7.8 us
    ppermute x6, waiting for transfers between devices, onward(): return lax.ppermute(value, ('blk', 'sub'), pairs)  5.56 us
  transfers between devices with their start and end apart: 19, of which 9 were waited for; matrix products, arithmetic and copies ran while one was open for 0% of the time, Pallas kernels for 15%

profile of v8, /device:TPU:0, one launch (start us, length us, event | category | flops | bytes accessed | tf_op | source)
XLA Modules:
  0.0 43.8 jit_solution(8054380774025383184)
XLA Ops:
  1.2 2.6 %collective-permute-start.1 = (f32[64,256]{1,0:T(8,128)}, f32[64,256]{1,0:T(8,128)S(1)}, u32[]{:S(2)}, u32[]{:S(2)}) collective-permute-start(f32[64,256]{1,0:T(8,128)} %refs_0_.4), channel_id=1, source_target_pairs={{0,3},{1,2},{2,1},{3,0},{4,7},{5,6},{6,5},{7,4},{8,11},{9,10},{10,... | collective-permute-start | bytes 196616 | tf_op jit(solution)/shard_map/ppermute | solution.py:256
  3.8 1.9 %shard_map.59 = (f32[256,768]{1,0:T(8,128)S(1)}, f32[768,256]{1,0:T(8,128)S(1)}, bf16[768,256]{1,0:T(8,128)(2,1)S(1)}, bf16[768,256]{1,0:T(8,128)(2,1)S(1)}, bf1...) custom-call(f32[2,768,256]{2,1,0:T(8,128)} %refs_0_.5, s32[2,768,256]{2,1,0:T(8,128)} %refs_1_.3, f32[768,256]{1,0:T(8,128)} %refs_2_.1), custom_call_target="tpu_custom_call" | custom-call | bytes 7077888 | tf_op jit(solution)/shard_map/pallas_call | solution.py:64
  5.7 0.7 %collective-permute-done.1.refs_1_ = f32[64,256]{1,0:T(8,128)S(1)} collective-permute-done((f32[64,256]{1,0:T(8,128)}, f32[64,256]{1,0:T(8,128)S(1)}, u32[]{:S(2)}, u32[]{:S(2)}) %collective-permute-start.1) | collective-permute-done | bytes 65568 | tf_op jit(solution)/shard_map/ppermute | solution.py:256
  6.4 0.6 %shard_map.60 = (f32[128,256]{1,0:T(8,128)S(1)}, bf16[128,768]{1,0:T(8,128)(2,1)S(1)}, bf16[128,768]{1,0:T(8,128)(2,1)S(1)}, f32[128,256]{1,0:T(8,128)S(1)}) custom-call(f32[64,256]{1,0:T(8,128)S(1)} %collective-permute-done.refs_0_, f32[64,256]{1,0:T(8,128)S(1)} %collective-permute-done.1.refs_1_, f32[256,768]{1,0:T(8,128)S(1)} %get-tuple-element.37.refs_2_, ...), custom_call_target="tpu_custom_call" | custom-call | flops 301989888 | bytes 3145728 | tf_op jit(solution)/shard_map/pallas_call | solution.py:64
  7.2 1.7 %collective-permute-start.2 = (f32[64,256]{1,0:T(8,128)S(1)}, f32[64,256]{1,0:T(8,128)S(1)}, u32[]{:S(2)}, u32[]{:S(2)}) collective-permute-start(f32[64,256]{1,0:T(8,128)S(1)} %copy-done.2), channel_id=1, source_target_pairs={{0,2},{1,3},{2,0},{3,1},{4,6},{5,7},{6,4},{7,5},{8,10},{9,11},{10,... | collective-permute-start | bytes 196616 | tf_op jit(solution)/shard_map/ppermute | solution.py:256
  8.9 1.0 %collective-permute-start.9 = (f32[64,256]{1,0:T(8,128)S(1)}, f32[64,256]{1,0:T(8,128)S(1)}, u32[]{:S(2)}, u32[]{:S(2)}) collective-permute-start(f32[64,256]{1,0:T(8,128)S(1)} %copy-done.2), channel_id=1, source_target_pairs={{0,5},{1,4},{2,7},{3,6},{4,9},{5,8},{6,11},{7,10},{8,13},{9,12},{1... | collective-permute-start | bytes 196616 | tf_op jit(solution)/shard_map/ppermute | solution.py:263
  9.9 1.7 %collective-permute-done.2.refs_1_ = f32[64,256]{1,0:T(8,128)S(1)} collective-permute-done((f32[64,256]{1,0:T(8,128)S(1)}, f32[64,256]{1,0:T(8,128)S(1)}, u32[]{:S(2)}, u32[]{:S(2)}) %collective-permute-start.2) | collective-permute-done | bytes 65568 | tf_op jit(solution)/shard_map/ppermute | solution.py:256
  11.6 0.6 %shard_map.61 = (f32[128,256]{1,0:T(8,128)S(1)}, bf16[128,768]{1,0:T(8,128)(2,1)S(1)}, bf16[128,768]{1,0:T(8,128)(2,1)S(1)}, f32[128,256]{1,0:T(8,128)S(1)}) custom-call(f32[64,256]{1,0:T(8,128)S(1)} %copy-done.2, f32[64,256]{1,0:T(8,128)S(1)} %collective-permute-done.2.refs_1_, f32[256,768]{1,0:T(8,128)S(1)} %get-tuple-element.37.refs_2_, ...), custom_call_target="tpu_custom_call" | custom-call | flops 301989888 | bytes 3145728 | tf_op jit(solution)/shard_map/pallas_call | solution.py:64
  12.5 3.7 %collective-permute-start.7 = (f32[128,256]{1,0:T(8,128)S(1)}, f32[128,256]{1,0:T(8,128)S(1)}, u32[]{:S(2)}, u32[]{:S(2)}) collective-permute-start(f32[128,256]{1,0:T(8,128)S(1)} %add.16), channel_id=1, source_target_pairs={{0,7},{1,6},{2,5},{3,4},{4,11},{5,10},{6,9},{7,8},{8,15},{9,14},{1... | collective-permute-start | bytes 393224 | tf_op jit(solution)/shard_map/ppermute | solution.py:263
  16.8 3.7 %collective-permute-done.10.refs_1_ = f32[64,256]{1,0:T(8,128)S(1)} collective-permute-done((f32[64,256]{1,0:T(8,128)S(1)}, f32[64,256]{1,0:T(8,128)S(1)}, u32[]{:S(2)}, u32[]{:S(2)}) %collective-permute-start.10) | collective-permute-done | bytes 65568 | tf_op jit(solution)/shard_map/ppermute | solution.py:256
  20.6 2.8 %collective-permute-done.7 = f32[128,256]{1,0:T(8,128)S(1)} collective-permute-done((f32[128,256]{1,0:T(8,128)S(1)}, f32[128,256]{1,0:T(8,128)S(1)}, u32[]{:S(2)}, u32[]{:S(2)}) %collective-permute-start.7) | collective-permute-done | bytes 131104 | tf_op jit(solution)/shard_map/ppermute | solution.py:263
  24.6 2.7 %collective-permute-done.3 = f32[8,128]{1,0:T(8,128)S(1)} collective-permute-done((f32[8,128]{1,0:T(8,128)S(1)}, f32[8,128]{1,0:T(8,128)S(1)}, u32[]{:S(2)}, u32[]{:S(2)}) %collective-permute-start.3) | collective-permute-done | bytes 4128 | tf_op jit(solution)/shard_map/ppermute | solution.py:256
  27.6 0.6 %shard_map.65.refs_0_ = f32[256,768]{1,0:T(8,128)S(1)} custom-call(f32[2,768,256]{2,1,0:T(8,128)S(1)} %copy-done, s32[2,768,256]{2,1,0:T(8,128)S(1)} %copy-done.1), custom_call_target="tpu_custom_call" | custom-call | bytes 3932160 | tf_op jit(solution)/shard_map/pallas_call | solution.py:64
  28.9 0.8 %shard_map.66 = (f32[128,256]{1,0:T(8,128)S(1)}, bf16[128,768]{1,0:T(8,128)(2,1)S(1)}, bf16[128,768]{1,0:T(8,128)(2,1)S(1)}, f32[128,256]{1,0:T(8,128)S(1)}, f32[64,256]{1,0:T(8,128)S(1)}) custom-call(f32[128,256]{1,0:T(8,128)S(1)} %add.17.own_ref, f32[128,256]{1,0:T(8,128)S(1)} %collective-permute-done.8.other_ref, ...), custom_call_target="tpu_custom_call" | custom-call | flops 301989888 | bytes 3604480 | tf_op jit(solution)/shard_map/pallas_call | solution.py:64
  30.1 0.8 %shard_map.67 = (f32[128,256]{1,0:T(8,128)S(1)}, bf16[128,768]{1,0:T(8,128)(2,1)S(1)}, bf16[128,768]{1,0:T(8,128)(2,1)S(1)}, f32[128,256]{1,0:T(8,128)S(1)}) custom-call(f32[128,256]{1,0:T(8,128)S(1)} %add.17.own_ref, f32[128,256]{1,0:T(8,128)S(1)} %collective-permute-done.8.other_ref, f32[128,256]{1,0:T(8,128)S(1)} %shard_map.64.old_own_ref.old_ref, ...), custom_call_target="tpu_custom_call" | custom-call | flops 301989888 | bytes 3407872 | tf_op jit(solution)/shard_map/pallas_call | solution.py:64
  31.6 1.4 %collective-permute-start.17 = (f32[128,256]{1,0:T(8,128)S(1)}, f32[128,256]{1,0:T(8,128)S(1)}, u32[]{:S(2)}, u32[]{:S(2)}) collective-permute-start(f32[128,256]{1,0:T(8,128)S(1)} %add.19), channel_id=1, source_target_pairs={{0,7},{1,6},{2,5},{3,4},{4,11},{5,10},{6,9},{7,8},{8,15},{9,14},{1... | collective-permute-start | bytes 393224 | tf_op jit(solution)/shard_map/ppermute | solution.py:263
  33.0 1.0 %collective-permute-start.14 = (f32[64,256]{1,0:T(8,128)S(1)}, f32[64,256]{1,0:T(8,128)S(1)}, u32[]{:S(2)}, u32[]{:S(2)}) collective-permute-start(f32[64,256]{1,0:T(8,128)S(1)} %get-tuple-element.65), channel_id=1, source_target_pairs={{0,5},{1,4},{2,7},{3,6},{4,9},{5,8},{6,11},{7,10},{8,13},{9,12},{1... | collective-permute-start | bytes 196616 | tf_op jit(solution)/shard_map/ppermute | solution.py:263
  34.6 1.3 %collective-permute-start.12 = (f32[8,128]{1,0:T(8,128)S(1)}, f32[8,128]{1,0:T(8,128)S(1)}, u32[]{:S(2)}, u32[]{:S(2)}) collective-permute-start(f32[8,128]{1,0:T(8,128)S(1)} %get-tuple-element.64), channel_id=1, source_target_pairs={{0,3},{1,2},{2,1},{3,0},{4,7},{5,6},{6,5},{7,4},{8,11},{9,10},{10,... | collective-permute-start | bytes 12296 | tf_op jit(solution)/shard_map/ppermute | solution.py:256
  35.9 1.8 %collective-permute-done.12 = f32[8,128]{1,0:T(8,128)S(1)} collective-permute-done((f32[8,128]{1,0:T(8,128)S(1)}, f32[8,128]{1,0:T(8,128)S(1)}, u32[]{:S(2)}, u32[]{:S(2)}) %collective-permute-start.12) | collective-permute-done | bytes 4128 | tf_op jit(solution)/shard_map/ppermute | solution.py:256
  37.7 0.6 %collective-permute-start.13 = (f32[8,128]{1,0:T(8,128)S(1)}, f32[8,128]{1,0:T(8,128)S(1)}, u32[]{:S(2)}, u32[]{:S(2)}) collective-permute-start(f32[8,128]{1,0:T(8,128)S(1)} %add.18.refs_0_), channel_id=1, source_target_pairs={{0,1},{1,0},{2,3},{3,2},{4,5},{5,4},{6,7},{7,6},{8,9},{9,8},{10,11... | collective-permute-start | bytes 12296 | tf_op jit(solution)/shard_map/ppermute | solution.py:256
  38.3 2.8 %collective-permute-done.17.refs_1_ = f32[128,256]{1,0:T(8,128)S(1)} collective-permute-done((f32[128,256]{1,0:T(8,128)S(1)}, f32[128,256]{1,0:T(8,128)S(1)}, u32[]{:S(2)}, u32[]{:S(2)}) %collective-permute-start.17) | collective-permute-done | bytes 131104 | tf_op jit(solution)/shard_map/ppermute | solution.py:263
  41.1 0.8 %collective-permute-start.18 = (f32[8,128]{1,0:T(8,128)S(1)}, f32[8,128]{1,0:T(8,128)S(1)}, u32[]{:S(2)}, u32[]{:S(2)}) collective-permute-start(f32[8,128]{1,0:T(8,128)S(1)} %get-tuple-element.69.refs_0_), channel_id=1, source_target_pairs={{0,1},{1,0},{2,3},{3,2},{4,5},{5,4},{6,7},{7,6},{8,9},{9,8},{10,11... | collective-permute-start | bytes 12296 | tf_op jit(solution)/shard_map/ppermute | solution.py:256
  41.9 1.2 %shard_map.69 = f32[768,256]{1,0:T(8,128)} custom-call(f32[768,256]{1,0:T(8,128)S(1)} %get-tuple-element.50.strip_ref.held_ref, f32[768,256]{1,0:T(8,128)S(1)} %get-tuple-element.63.grad_ref, f32[8,128]{1,0:T(8,128)S(1)} %add.18.refs_0_, f32[8,128]{1,0:T(8,128)S(1)} %collective-permute-done.13.refs_1_), custom_call_target="tpu_custom_call" | custom-call | bytes 2367488 | tf_op jit(solution)/shard_map/pallas_call | solution.py:64
  43.0 0.8 %shard_map.71 = f32[64,256]{1,0:T(8,128)} custom-call(f32[64,256]{1,0:T(8,128)S(1)} %collective-permute-done.14.held_ref, f32[64,256]{1,0:T(8,128)S(1)} %get-tuple-element.68.grad_ref, f32[8,128]{1,0:T(8,128)S(1)} %get-tuple-element.69.refs_0_, f32[8,128]{1,0:T(8,128)S(1)} %collective-permute-done.18.refs_1_), custom_call_target="tpu_custom_call" | custom-call | bytes 204800 | tf_op jit(solution)/shard_map/pallas_call | solution.py:64
  (38 shorter events, 5.4 us)
Async XLA Ops:
  0.6 5.0 %collective-permute-start = (f32[64,256]{1,0:T(8,128)}, f32[64,256]{1,0:T(8,128)S(1)}, u32[]{:S(2)}, u32[]{:S(2)}) collective-permute-start(f32[64,256]{1,0:T(8,128)} %refs_0_.4), channel_id=1, source_target_pairs={{0,1},{1,0},{2,3},{3,2},{4,5},{5,4},{6,7},{7,6},{8,9},{9,8},{10,11... | collective-permute-start | bytes 196616 | tf_op jit(solution)/shard_map/ppermute | solution.py:256
  1.2 5.2 %collective-permute-start.1 = (f32[64,256]{1,0:T(8,128)}, f32[64,256]{1,0:T(8,128)S(1)}, u32[]{:S(2)}, u32[]{:S(2)}) collective-permute-start(f32[64,256]{1,0:T(8,128)} %refs_0_.4), channel_id=1, source_target_pairs={{0,3},{1,2},{2,1},{3,0},{4,7},{5,6},{6,5},{7,4},{8,11},{9,10},{10,... | collective-permute-start | bytes 196616 | tf_op jit(solution)/shard_map/ppermute | solution.py:256
  5.6 1.6 %copy-start.2 = (f32[64,256]{1,0:T(8,128)S(1)}, f32[64,256]{1,0:T(8,128)}, u32[]{:S(2)}) copy-start(f32[64,256]{1,0:T(8,128)} %refs_0_.4) | copy-start | bytes 196612
  7.0 5.2 %collective-permute-start.5 = (f32[128,256]{1,0:T(8,128)S(1)}, f32[128,256]{1,0:T(8,128)S(1)}, u32[]{:S(2)}, u32[]{:S(2)}) collective-permute-start(f32[128,256]{1,0:T(8,128)S(1)} %get-tuple-element.52), channel_id=1, source_target_pairs={{0,1},{1,0},{2,3},{3,2},{4,5},{5,4},{6,7},{7,6},{8,9},{9,8},{10,11... | collective-permute-start | bytes 393224 | tf_op jit(solution)/shard_map/ppermute | solution.py:256
  7.2 4.4 %collective-permute-start.2 = (f32[64,256]{1,0:T(8,128)S(1)}, f32[64,256]{1,0:T(8,128)S(1)}, u32[]{:S(2)}, u32[]{:S(2)}) collective-permute-start(f32[64,256]{1,0:T(8,128)S(1)} %copy-done.2), channel_id=1, source_target_pairs={{0,2},{1,3},{2,0},{3,1},{4,6},{5,7},{6,4},{7,5},{8,10},{9,11},{10,... | collective-permute-start | bytes 196616 | tf_op jit(solution)/shard_map/ppermute | solution.py:256
  8.9 7.3 %collective-permute-start.9 = (f32[64,256]{1,0:T(8,128)S(1)}, f32[64,256]{1,0:T(8,128)S(1)}, u32[]{:S(2)}, u32[]{:S(2)}) collective-permute-start(f32[64,256]{1,0:T(8,128)S(1)} %copy-done.2), channel_id=1, source_target_pairs={{0,5},{1,4},{2,7},{3,6},{4,9},{5,8},{6,11},{7,10},{8,13},{9,12},{1... | collective-permute-start | bytes 196616 | tf_op jit(solution)/shard_map/ppermute | solution.py:263
  11.6 16.0 %copy-start.1 = (s32[2,768,256]{2,1,0:T(8,128)S(1)}, s32[2,768,256]{2,1,0:T(8,128)}, u32[]{:S(2)}) copy-start(s32[2,768,256]{2,1,0:T(8,128)} %refs_1_.3) | copy-start | bytes 4718596
  12.3 15.4 %copy-start = (f32[2,768,256]{2,1,0:T(8,128)S(1)}, f32[2,768,256]{2,1,0:T(8,128)}, u32[]{:S(2)}) copy-start(f32[2,768,256]{2,1,0:T(8,128)} %refs_0_.5) | copy-start | bytes 4718596
  12.3 8.3 %collective-permute-start.6 = (f32[128,256]{1,0:T(8,128)S(1)}, f32[128,256]{1,0:T(8,128)S(1)}, u32[]{:S(2)}, u32[]{:S(2)}) collective-permute-start(f32[128,256]{1,0:T(8,128)S(1)} %add.16), channel_id=1, source_target_pairs={{0,5},{1,4},{2,7},{3,6},{4,9},{5,8},{6,11},{7,10},{8,13},{9,12},{1... | collective-permute-start | bytes 393224 | tf_op jit(solution)/shard_map/ppermute | solution.py:263
  12.5 10.9 %collective-permute-start.7 = (f32[128,256]{1,0:T(8,128)S(1)}, f32[128,256]{1,0:T(8,128)S(1)}, u32[]{:S(2)}, u32[]{:S(2)}) collective-permute-start(f32[128,256]{1,0:T(8,128)S(1)} %add.16), channel_id=1, source_target_pairs={{0,7},{1,6},{2,5},{3,4},{4,11},{5,10},{6,9},{7,8},{8,15},{9,14},{1... | collective-permute-start | bytes 393224 | tf_op jit(solution)/shard_map/ppermute | solution.py:263
  16.2 4.3 %collective-permute-start.10 = (f32[64,256]{1,0:T(8,128)S(1)}, f32[64,256]{1,0:T(8,128)S(1)}, u32[]{:S(2)}, u32[]{:S(2)}) collective-permute-start(f32[64,256]{1,0:T(8,128)S(1)} %collective-permute-done.9.refs_0_), channel_id=1, source_target_pairs={{0,2},{1,3},{2,0},{3,1},{4,6},{5,7},{6,4},{7,5},{8,10},{9,11},{10,... | collective-permute-start | bytes 196616 | tf_op jit(solution)/shard_map/ppermute | solution.py:256
  20.5 8.4 %collective-permute-start.11 = (f32[128,256]{1,0:T(8,128)S(1)}, f32[128,256]{1,0:T(8,128)S(1)}, u32[]{:S(2)}, u32[]{:S(2)}) collective-permute-start(f32[128,256]{1,0:T(8,128)S(1)} %shard_map.64.old_own_ref.old_ref), channel_id=1, source_target_pairs={{0,1},{1,0},{2,3},{3,2},{4,5},{5,4},{6,7},{7,6},{8,9},{9,8},{10,11... | collective-permute-start | bytes 393224 | tf_op jit(solution)/shard_map/ppermute | solution.py:256
  23.4 5.5 %collective-permute-start.8 = (f32[128,256]{1,0:T(8,128)S(1)}, f32[128,256]{1,0:T(8,128)S(1)}, u32[]{:S(2)}, u32[]{:S(2)}) collective-permute-start(f32[128,256]{1,0:T(8,128)S(1)} %add.17.own_ref), channel_id=1, source_target_pairs={{0,1},{1,0},{2,3},{3,2},{4,5},{5,4},{6,7},{7,6},{8,9},{9,8},{10,11... | collective-permute-start | bytes 393224 | tf_op jit(solution)/shard_map/ppermute | solution.py:256
  24.2 3.1 %collective-permute-start.3 = (f32[8,128]{1,0:T(8,128)S(1)}, f32[8,128]{1,0:T(8,128)S(1)}, u32[]{:S(2)}, u32[]{:S(2)}) collective-permute-start(f32[8,128]{1,0:T(8,128)S(1)} %get-tuple-element.49), channel_id=1, source_target_pairs={{0,3},{1,2},{2,1},{3,0},{4,7},{5,6},{6,5},{7,4},{8,11},{9,10},{10,... | collective-permute-start | bytes 12296 | tf_op jit(solution)/shard_map/ppermute | solution.py:256
  27.3 1.2 %collective-permute-start.4 = (f32[8,128]{1,0:T(8,128)S(1)}, f32[8,128]{1,0:T(8,128)S(1)}, u32[]{:S(2)}, u32[]{:S(2)}) collective-permute-start(f32[8,128]{1,0:T(8,128)S(1)} %add.15.own_ref), channel_id=1, source_target_pairs={{0,1},{1,0},{2,3},{3,2},{4,5},{5,4},{6,7},{7,6},{8,9},{9,8},{10,11... | collective-permute-start | bytes 12296 | tf_op jit(solution)/shard_map/ppermute | solution.py:256
  29.7 1.4 %collective-permute-start.15 = (f32[128,256]{1,0:T(8,128)S(1)}, f32[128,256]{1,0:T(8,128)S(1)}, u32[]{:S(2)}, u32[]{:S(2)}) collective-permute-start(f32[128,256]{1,0:T(8,128)S(1)} %get-tuple-element.67), channel_id=1, source_target_pairs={{0,1},{1,0},{2,3},{3,2},{4,5},{5,4},{6,7},{7,6},{8,9},{9,8},{10,11... | collective-permute-start | bytes 393224 | tf_op jit(solution)/shard_map/ppermute | solution.py:256
  31.2 7.2 %collective-permute-start.16 = (f32[128,256]{1,0:T(8,128)S(1)}, f32[128,256]{1,0:T(8,128)S(1)}, u32[]{:S(2)}, u32[]{:S(2)}) collective-permute-start(f32[128,256]{1,0:T(8,128)S(1)} %add.19), channel_id=1, source_target_pairs={{0,5},{1,4},{2,7},{3,6},{4,9},{5,8},{6,11},{7,10},{8,13},{9,12},{1... | collective-permute-start | bytes 393224 | tf_op jit(solution)/shard_map/ppermute | solution.py:263
  31.6 9.5 %collective-permute-start.17 = (f32[128,256]{1,0:T(8,128)S(1)}, f32[128,256]{1,0:T(8,128)S(1)}, u32[]{:S(2)}, u32[]{:S(2)}) collective-permute-start(f32[128,256]{1,0:T(8,128)S(1)} %add.19), channel_id=1, source_target_pairs={{0,7},{1,6},{2,5},{3,4},{4,11},{5,10},{6,9},{7,8},{8,15},{9,14},{1... | collective-permute-start | bytes 393224 | tf_op jit(solution)/shard_map/ppermute | solution.py:263
  33.0 10.0 %collective-permute-start.14 = (f32[64,256]{1,0:T(8,128)S(1)}, f32[64,256]{1,0:T(8,128)S(1)}, u32[]{:S(2)}, u32[]{:S(2)}) collective-permute-start(f32[64,256]{1,0:T(8,128)S(1)} %get-tuple-element.65), channel_id=1, source_target_pairs={{0,5},{1,4},{2,7},{3,6},{4,9},{5,8},{6,11},{7,10},{8,13},{9,12},{1... | collective-permute-start | bytes 196616 | tf_op jit(solution)/shard_map/ppermute | solution.py:263
  34.6 3.1 %collective-permute-start.12 = (f32[8,128]{1,0:T(8,128)S(1)}, f32[8,128]{1,0:T(8,128)S(1)}, u32[]{:S(2)}, u32[]{:S(2)}) collective-permute-start(f32[8,128]{1,0:T(8,128)S(1)} %get-tuple-element.64), channel_id=1, source_target_pairs={{0,3},{1,2},{2,1},{3,0},{4,7},{5,6},{6,5},{7,4},{8,11},{9,10},{10,... | collective-permute-start | bytes 12296 | tf_op jit(solution)/shard_map/ppermute | solution.py:256
  37.7 4.2 %collective-permute-start.13 = (f32[8,128]{1,0:T(8,128)S(1)}, f32[8,128]{1,0:T(8,128)S(1)}, u32[]{:S(2)}, u32[]{:S(2)}) collective-permute-start(f32[8,128]{1,0:T(8,128)S(1)} %add.18.refs_0_), channel_id=1, source_target_pairs={{0,1},{1,0},{2,3},{3,2},{4,5},{5,4},{6,7},{7,6},{8,9},{9,8},{10,11... | collective-permute-start | bytes 12296 | tf_op jit(solution)/shard_map/ppermute | solution.py:256
  41.1 1.9 %collective-permute-start.18 = (f32[8,128]{1,0:T(8,128)S(1)}, f32[8,128]{1,0:T(8,128)S(1)}, u32[]{:S(2)}, u32[]{:S(2)}) collective-permute-start(f32[8,128]{1,0:T(8,128)S(1)} %get-tuple-element.69.refs_0_), channel_id=1, source_target_pairs={{0,1},{1,0},{2,3},{3,2},{4,5},{5,4},{6,7},{7,6},{8,9},{9,8},{10,11... | collective-permute-start | bytes 12296 | tf_op jit(solution)/shard_map/ppermute | solution.py:256

commit v9 on v8

--- a/solution.py
+++ b/solution.py
@@ -179,6 +179,14 @@
     return step_of([tile_squares(own_ref[...]), tile_squares(other_ref[...])], count)
 
 
+def by_target(part, out_ref, share):
+    nx = part.shape[0] // share
+    chip, _ = place()
+    for at in range(nx):
+        rows = aligned(lax.rem(at - chip + nx, nx), share)
+        out_ref[rows, :] = part[at * share : (at + 1) * share]
+
+
 def later_send_kernel(count, share, own_ref, other_ref, old_own_ref, old_ref, *refs):
     problem, (send_ref, high_ref, low_ref, block_ref, share_ref) = refs[:5], refs[5:]
     step = later_step(count, own_ref, other_ref)
@@ -187,16 +195,16 @@
     share_ref[...] = old_own_ref[rows, :] - step * own_ref[rows, :]
     block = old_ref[...] - step * other_ref[...]
     block_ref[...] = block
-    send_ref[...] = errors_and_part(0, problem, block, high_ref, low_ref)
-
-
-def later_keep_kernel(count, own_ref, other_ref, old_ref, *refs):
+    by_target(errors_and_part(0, problem, block, high_ref, low_ref), send_ref, share)
+
+
+def later_keep_kernel(count, share, own_ref, other_ref, old_ref, *refs):
     problem, (keep_ref, high_ref, low_ref, block_ref) = refs[:5], refs[5:]
     step = later_step(count, own_ref, other_ref)
     block = old_ref[...] - step * own_ref[...]
     block_ref[...] = block
     part = errors_and_part(1, problem, block, high_ref, low_ref)
-    keep_ref[...] = with_ridge(part, block)
+    by_target(with_ridge(part, block), keep_ref, share)
 
 
 def pixel_gradient(strip_ref, errors, blocks):
@@ -225,15 +233,17 @@
     refs[-1][...] = held_ref[...] - step * grad_ref[...]
 
 
-def last_gradient_kernel(share, *refs):
-    parts, (grad_ref, tile_ref), sum_ref = refs[:-3], refs[-3:-1], refs[-1]
+def last_gradient_kernel(*refs):
+    parts, (grad_ref, tile_ref) = refs[:-2], refs[-2:]
     total = parts[0][...]
     for ref in parts[1:]:
         total = total + ref[...]
-    sum_ref[...] = total
+    grad_ref[...] = total
     tile_ref[...] = tile_squares(total)
-    chip, _ = place()
-    grad_ref[...] = sum_ref[aligned(chip, share), :]
+
+
+def orders(n):
+    return [(dx, dc) for dx in range(n // CORES) for dc in range(CORES)]
 
 
 def on_device(readings, coverage, pixel_factors, date_factors):
@@ -325,12 +335,12 @@
     got = within(send, 0, 1)
     held = onward(own, 0)
     keep, h1, l1, b1 = call(
-        functools.partial(later_keep_kernel, date_count),
+        functools.partial(later_keep_kernel, date_count, share),
         part_shapes + [shape(half, rank)],
         own_grad, other_grad, old_half, values_1, *halves, flops=6 * work,
     )
-    mine = keep + got
-    came = [onward(mine, dx) for dx in range(nx)]
+    rows = [slice(dx * share, (dx + 1) * share) for dx in range(nx)]
+    came = [onward(keep[r] + got[r], dx) for dx, r in enumerate(rows)]
     grad, tile = call(
         gradient_kernel, [shape(pixels, rank), shape(8, 128)],
         strip, h0, l0, h1, l1, b0, b1, flops=6 * work,
@@ -343,14 +353,12 @@
         strip, grad, tile, other_tile,
     )
     date_grad, tile = call(
-        functools.partial(last_gradient_kernel, share),
-        [shape(share, rank), shape(8, 128)], *came,
-        scratch=[pltpu.VMEM((half, rank), F32)],
-    )
-    other_tile = within(tile, 0, 1)
+        last_gradient_kernel, [shape(share, rank), shape(8, 128)], *came
+    )
+    tiles = [within(tile, *step) for step in orders(n)[1:]]
     date_out, = call(
         functools.partial(step_kernel, date_count), [shape(share, rank)],
-        held, date_grad, tile, other_tile,
+        held, date_grad, tile, *tiles,
     )
     return strip, date_out
 

time: 43.9 us -> 44.6 us (1.016)
  starting transfers between devices: 17.5 us -> 18.6 us
  waiting for transfers between devices: 16.7 us -> 16.2 us
    ppermute x6, waiting for transfers between devices: 5.56 us -> 2.8 us  [onward(): return lax.ppermute(value, ('blk', 'sub'), pairs)]
    ppermute x13 -> x15, waiting for transfers between devices: 11.1 us -> 13.4 us  [within(): return lax.ppermute(value, 'sub', pairs)]
    ppermute x13 -> x15, starting transfers between devices: 9.68 us -> 10.9 us  [within(): return lax.ppermute(value, 'sub', pairs)]
  transfers between devices with their start and end apart: 19 -> 21, of which waited for: 9 -> 10; matrix products, arithmetic and copies ran while one was open for 0% -> 0% of each run, Pallas kernels for 15% -> 15%
where the time goes in v9:
time: 44.6 us; the launch traced here: 44.5 us
  starting transfers between devices  18.6 us (42%)
  waiting for transfers between devices  16.2 us (36%)
  Pallas kernels  8.73 us (20%)
  between operations  0.8 us (2%)
    ppermute x15, waiting for transfers between devices, within(): return lax.ppermute(value, 'sub', pairs)  13.4 us
    ppermute x15, starting transfers between devices, within(): return lax.ppermute(value, 'sub', pairs)  10.9 us
    pallas_call x13, Pallas kernels, call(): pl.pallas_call(kernel, out_shape=outs, in_specs=[where] * len(args), out_...  8.73 us
    ppermute x6, starting transfers between devices, onward(): return lax.ppermute(value, ('blk', 'sub'), pairs)  7.8 us
    ppermute x6, waiting for transfers between devices, onward(): return lax.ppermute(value, ('blk', 'sub'), pairs)  2.8 us
  transfers between devices with their start and end apart: 21, of which 10 were waited for; matrix products, arithmetic and copies ran while one was open for 0% of the time, Pallas kernels for 15%

profile of v9, /device:TPU:0, one launch (start us, length us, event | category | flops | bytes accessed | tf_op | source)
XLA Modules:
  0.0 44.5 jit_solution(15881945355478226043)
XLA Ops:
  1.2 2.6 %collective-permute-start.1 = (f32[64,256]{1,0:T(8,128)}, f32[64,256]{1,0:T(8,128)S(1)}, u32[]{:S(2)}, u32[]{:S(2)}) collective-permute-start(f32[64,256]{1,0:T(8,128)} %refs_0_.4), channel_id=1, source_target_pairs={{0,3},{1,2},{2,1},{3,0},{4,7},{5,6},{6,5},{7,4},{8,11},{9,10},{10,... | collective-permute-start | bytes 196616 | tf_op jit(solution)/shard_map/ppermute | solution.py:266
  3.8 1.9 %shard_map.59 = (f32[256,768]{1,0:T(8,128)S(1)}, f32[768,256]{1,0:T(8,128)S(1)}, bf16[768,256]{1,0:T(8,128)(2,1)S(1)}, bf16[768,256]{1,0:T(8,128)(2,1)S(1)}, bf1...) custom-call(f32[2,768,256]{2,1,0:T(8,128)} %refs_0_.5, s32[2,768,256]{2,1,0:T(8,128)} %refs_1_.3, f32[768,256]{1,0:T(8,128)} %refs_2_.1), custom_call_target="tpu_custom_call" | custom-call | bytes 7077888 | tf_op jit(solution)/shard_map/pallas_call | solution.py:64
  5.7 0.7 %collective-permute-done.1.refs_1_ = f32[64,256]{1,0:T(8,128)S(1)} collective-permute-done((f32[64,256]{1,0:T(8,128)}, f32[64,256]{1,0:T(8,128)S(1)}, u32[]{:S(2)}, u32[]{:S(2)}) %collective-permute-start.1) | collective-permute-done | bytes 65568 | tf_op jit(solution)/shard_map/ppermute | solution.py:266
  6.4 0.6 %shard_map.60 = (f32[128,256]{1,0:T(8,128)S(1)}, bf16[128,768]{1,0:T(8,128)(2,1)S(1)}, bf16[128,768]{1,0:T(8,128)(2,1)S(1)}, f32[128,256]{1,0:T(8,128)S(1)}) custom-call(f32[64,256]{1,0:T(8,128)S(1)} %collective-permute-done.refs_0_, f32[64,256]{1,0:T(8,128)S(1)} %collective-permute-done.1.refs_1_, f32[256,768]{1,0:T(8,128)S(1)} %get-tuple-element.37.refs_2_, ...), custom_call_target="tpu_custom_call" | custom-call | flops 301989888 | bytes 3145728 | tf_op jit(solution)/shard_map/pallas_call | solution.py:64
  7.2 1.7 %collective-permute-start.2 = (f32[64,256]{1,0:T(8,128)S(1)}, f32[64,256]{1,0:T(8,128)S(1)}, u32[]{:S(2)}, u32[]{:S(2)}) collective-permute-start(f32[64,256]{1,0:T(8,128)S(1)} %copy-done.2), channel_id=1, source_target_pairs={{0,2},{1,3},{2,0},{3,1},{4,6},{5,7},{6,4},{7,5},{8,10},{9,11},{10,... | collective-permute-start | bytes 196616 | tf_op jit(solution)/shard_map/ppermute | solution.py:266
  8.9 1.0 %collective-permute-start.9 = (f32[64,256]{1,0:T(8,128)S(1)}, f32[64,256]{1,0:T(8,128)S(1)}, u32[]{:S(2)}, u32[]{:S(2)}) collective-permute-start(f32[64,256]{1,0:T(8,128)S(1)} %copy-done.2), channel_id=1, source_target_pairs={{0,5},{1,4},{2,7},{3,6},{4,9},{5,8},{6,11},{7,10},{8,13},{9,12},{1... | collective-permute-start | bytes 196616 | tf_op jit(solution)/shard_map/ppermute | solution.py:273
  9.9 1.7 %collective-permute-done.2.refs_1_ = f32[64,256]{1,0:T(8,128)S(1)} collective-permute-done((f32[64,256]{1,0:T(8,128)S(1)}, f32[64,256]{1,0:T(8,128)S(1)}, u32[]{:S(2)}, u32[]{:S(2)}) %collective-permute-start.2) | collective-permute-done | bytes 65568 | tf_op jit(solution)/shard_map/ppermute | solution.py:266
  11.6 0.6 %shard_map.61 = (f32[128,256]{1,0:T(8,128)S(1)}, bf16[128,768]{1,0:T(8,128)(2,1)S(1)}, bf16[128,768]{1,0:T(8,128)(2,1)S(1)}, f32[128,256]{1,0:T(8,128)S(1)}) custom-call(f32[64,256]{1,0:T(8,128)S(1)} %copy-done.2, f32[64,256]{1,0:T(8,128)S(1)} %collective-permute-done.2.refs_1_, f32[256,768]{1,0:T(8,128)S(1)} %get-tuple-element.37.refs_2_, ...), custom_call_target="tpu_custom_call" | custom-call | flops 301989888 | bytes 3145728 | tf_op jit(solution)/shard_map/pallas_call | solution.py:64
  12.5 3.7 %collective-permute-start.7 = (f32[128,256]{1,0:T(8,128)S(1)}, f32[128,256]{1,0:T(8,128)S(1)}, u32[]{:S(2)}, u32[]{:S(2)}) collective-permute-start(f32[128,256]{1,0:T(8,128)S(1)} %add.19), channel_id=1, source_target_pairs={{0,7},{1,6},{2,5},{3,4},{4,11},{5,10},{6,9},{7,8},{8,15},{9,14},{1... | collective-permute-start | bytes 393224 | tf_op jit(solution)/shard_map/ppermute | solution.py:273
  16.8 3.7 %collective-permute-done.10.refs_1_ = f32[64,256]{1,0:T(8,128)S(1)} collective-permute-done((f32[64,256]{1,0:T(8,128)S(1)}, f32[64,256]{1,0:T(8,128)S(1)}, u32[]{:S(2)}, u32[]{:S(2)}) %collective-permute-start.10) | collective-permute-done | bytes 65568 | tf_op jit(solution)/shard_map/ppermute | solution.py:266
  20.6 2.8 %collective-permute-done.7 = f32[128,256]{1,0:T(8,128)S(1)} collective-permute-done((f32[128,256]{1,0:T(8,128)S(1)}, f32[128,256]{1,0:T(8,128)S(1)}, u32[]{:S(2)}, u32[]{:S(2)}) %collective-permute-start.7) | collective-permute-done | bytes 131104 | tf_op jit(solution)/shard_map/ppermute | solution.py:273
  24.6 2.7 %collective-permute-done.3 = f32[8,128]{1,0:T(8,128)S(1)} collective-permute-done((f32[8,128]{1,0:T(8,128)S(1)}, f32[8,128]{1,0:T(8,128)S(1)}, u32[]{:S(2)}, u32[]{:S(2)}) %collective-permute-start.3) | collective-permute-done | bytes 4128 | tf_op jit(solution)/shard_map/ppermute | solution.py:266
  27.6 0.6 %shard_map.65.refs_0_ = f32[256,768]{1,0:T(8,128)S(1)} custom-call(f32[2,768,256]{2,1,0:T(8,128)S(1)} %copy-done, s32[2,768,256]{2,1,0:T(8,128)S(1)} %copy-done.1), custom_call_target="tpu_custom_call" | custom-call | bytes 3932160 | tf_op jit(solution)/shard_map/pallas_call | solution.py:64
  28.9 0.8 %shard_map.66 = (f32[128,256]{1,0:T(8,128)S(1)}, bf16[128,768]{1,0:T(8,128)(2,1)S(1)}, bf16[128,768]{1,0:T(8,128)(2,1)S(1)}, f32[128,256]{1,0:T(8,128)S(1)}, f32[64,256]{1,0:T(8,128)S(1)}) custom-call(f32[128,256]{1,0:T(8,128)S(1)} %add.20.own_ref, f32[128,256]{1,0:T(8,128)S(1)} %collective-permute-done.8.other_ref, ...), custom_call_target="tpu_custom_call" | custom-call | flops 301989888 | bytes 3604480 | tf_op jit(solution)/shard_map/pallas_call | solution.py:64
  30.1 0.8 %shard_map.67 = (f32[128,256]{1,0:T(8,128)S(1)}, bf16[128,768]{1,0:T(8,128)(2,1)S(1)}, bf16[128,768]{1,0:T(8,128)(2,1)S(1)}, f32[128,256]{1,0:T(8,128)S(1)}) custom-call(f32[128,256]{1,0:T(8,128)S(1)} %add.20.own_ref, f32[128,256]{1,0:T(8,128)S(1)} %collective-permute-done.8.other_ref, f32[128,256]{1,0:T(8,128)S(1)} %shard_map.64.old_own_ref.old_ref, ...), custom_call_target="tpu_custom_call" | custom-call | flops 301989888 | bytes 3407872 | tf_op jit(solution)/shard_map/pallas_call | solution.py:64
  31.5 1.4 %collective-permute-start.17 = (f32[64,256]{1,0:T(8,128)S(1)}, f32[64,256]{1,0:T(8,128)S(1)}, u32[]{:S(2)}, u32[]{:S(2)}) collective-permute-start(f32[64,256]{1,0:T(8,128)S(1)} %get-tuple-element.70), channel_id=1, source_target_pairs={{0,7},{1,6},{2,5},{3,4},{4,11},{5,10},{6,9},{7,8},{8,15},{9,14},{1... | collective-permute-start | bytes 196616 | tf_op jit(solution)/shard_map/ppermute | solution.py:273
  33.0 1.0 %collective-permute-start.14 = (f32[64,256]{1,0:T(8,128)S(1)}, f32[64,256]{1,0:T(8,128)S(1)}, u32[]{:S(2)}, u32[]{:S(2)}) collective-permute-start(f32[64,256]{1,0:T(8,128)S(1)} %get-tuple-element.65), channel_id=1, source_target_pairs={{0,5},{1,4},{2,7},{3,6},{4,9},{5,8},{6,11},{7,10},{8,13},{9,12},{1... | collective-permute-start | bytes 196616 | tf_op jit(solution)/shard_map/ppermute | solution.py:273
  34.6 1.3 %collective-permute-start.12 = (f32[8,128]{1,0:T(8,128)S(1)}, f32[8,128]{1,0:T(8,128)S(1)}, u32[]{:S(2)}, u32[]{:S(2)}) collective-permute-start(f32[8,128]{1,0:T(8,128)S(1)} %get-tuple-element.64), channel_id=1, source_target_pairs={{0,3},{1,2},{2,1},{3,0},{4,7},{5,6},{6,5},{7,4},{8,11},{9,10},{10,... | collective-permute-start | bytes 12296 | tf_op jit(solution)/shard_map/ppermute | solution.py:266
  35.9 2.2 %collective-permute-done.12 = f32[8,128]{1,0:T(8,128)S(1)} collective-permute-done((f32[8,128]{1,0:T(8,128)S(1)}, f32[8,128]{1,0:T(8,128)S(1)}, u32[]{:S(2)}, u32[]{:S(2)}) %collective-permute-start.12) | collective-permute-done | bytes 4128 | tf_op jit(solution)/shard_map/ppermute | solution.py:266
  38.8 1.9 %collective-permute-start.19 = (f32[8,128]{1,0:T(8,128)S(1)}, f32[8,128]{1,0:T(8,128)S(1)}, u32[]{:S(2)}, u32[]{:S(2)}) collective-permute-start(f32[8,128]{1,0:T(8,128)S(1)} %get-tuple-element.69.refs_0_), channel_id=1, source_target_pairs={{0,2},{1,3},{2,0},{3,1},{4,6},{5,7},{6,4},{7,5},{8,10},{9,11},{10,... | collective-permute-start | bytes 12296 | tf_op jit(solution)/shard_map/ppermute | solution.py:266
  40.7 1.2 %shard_map.69 = f32[768,256]{1,0:T(8,128)} custom-call(f32[768,256]{1,0:T(8,128)S(1)} %get-tuple-element.50.strip_ref.held_ref, f32[768,256]{1,0:T(8,128)S(1)} %get-tuple-element.63.grad_ref, f32[8,128]{1,0:T(8,128)S(1)} %add.21.refs_0_, f32[8,128]{1,0:T(8,128)S(1)} %collective-permute-done.13.refs_1_), custom_call_target="tpu_custom_call" | custom-call | bytes 2367488 | tf_op jit(solution)/shard_map/pallas_call | solution.py:64
  41.8 0.6 %collective-permute-done.19.refs_2_ = f32[8,128]{1,0:T(8,128)S(1)} collective-permute-done((f32[8,128]{1,0:T(8,128)S(1)}, f32[8,128]{1,0:T(8,128)S(1)}, u32[]{:S(2)}, u32[]{:S(2)}) %collective-permute-start.19) | collective-permute-done | bytes 4128 | tf_op jit(solution)/shard_map/ppermute | solution.py:266
  42.4 1.3 %collective-permute-done.20.refs_3_ = f32[8,128]{1,0:T(8,128)S(1)} collective-permute-done((f32[8,128]{1,0:T(8,128)S(1)}, f32[8,128]{1,0:T(8,128)S(1)}, u32[]{:S(2)}, u32[]{:S(2)}) %collective-permute-start.20) | collective-permute-done | bytes 4128 | tf_op jit(solution)/shard_map/ppermute | solution.py:266
  43.7 0.8 %shard_map.71 = f32[64,256]{1,0:T(8,128)} custom-call(f32[64,256]{1,0:T(8,128)S(1)} %collective-permute-done.14.held_ref, f32[64,256]{1,0:T(8,128)S(1)} %get-tuple-element.68.grad_ref, f32[8,128]{1,0:T(8,128)S(1)} %get-tuple-element.69.refs_0_, f32[8,128]{1,0:T(8,128)S(1)} %collective-permute-done.18.refs_1_, f32[8,128]{1,0:T(8,128)S(1)} %collective-permute-done.19.refs_2_, ...), custom_call_target="tpu_custom_call" | custom-call | bytes 212992 | tf_op jit(solution)/shard_map/pallas_call | solution.py:64
  (42 shorter events, 6.1 us)
Async XLA Ops:
  0.6 5.0 %collective-permute-start = (f32[64,256]{1,0:T(8,128)}, f32[64,256]{1,0:T(8,128)S(1)}, u32[]{:S(2)}, u32[]{:S(2)}) collective-permute-start(f32[64,256]{1,0:T(8,128)} %refs_0_.4), channel_id=1, source_target_pairs={{0,1},{1,0},{2,3},{3,2},{4,5},{5,4},{6,7},{7,6},{8,9},{9,8},{10,11... | collective-permute-start | bytes 196616 | tf_op jit(solution)/shard_map/ppermute | solution.py:266
  1.2 5.2 %collective-permute-start.1 = (f32[64,256]{1,0:T(8,128)}, f32[64,256]{1,0:T(8,128)S(1)}, u32[]{:S(2)}, u32[]{:S(2)}) collective-permute-start(f32[64,256]{1,0:T(8,128)} %refs_0_.4), channel_id=1, source_target_pairs={{0,3},{1,2},{2,1},{3,0},{4,7},{5,6},{6,5},{7,4},{8,11},{9,10},{10,... | collective-permute-start | bytes 196616 | tf_op jit(solution)/shard_map/ppermute | solution.py:266
  5.6 1.6 %copy-start.2 = (f32[64,256]{1,0:T(8,128)S(1)}, f32[64,256]{1,0:T(8,128)}, u32[]{:S(2)}) copy-start(f32[64,256]{1,0:T(8,128)} %refs_0_.4) | copy-start | bytes 196612
  7.0 5.2 %collective-permute-start.5 = (f32[128,256]{1,0:T(8,128)S(1)}, f32[128,256]{1,0:T(8,128)S(1)}, u32[]{:S(2)}, u32[]{:S(2)}) collective-permute-start(f32[128,256]{1,0:T(8,128)S(1)} %get-tuple-element.52), channel_id=1, source_target_pairs={{0,1},{1,0},{2,3},{3,2},{4,5},{5,4},{6,7},{7,6},{8,9},{9,8},{10,11... | collective-permute-start | bytes 393224 | tf_op jit(solution)/shard_map/ppermute | solution.py:266
  7.2 4.4 %collective-permute-start.2 = (f32[64,256]{1,0:T(8,128)S(1)}, f32[64,256]{1,0:T(8,128)S(1)}, u32[]{:S(2)}, u32[]{:S(2)}) collective-permute-start(f32[64,256]{1,0:T(8,128)S(1)} %copy-done.2), channel_id=1, source_target_pairs={{0,2},{1,3},{2,0},{3,1},{4,6},{5,7},{6,4},{7,5},{8,10},{9,11},{10,... | collective-permute-start | bytes 196616 | tf_op jit(solution)/shard_map/ppermute | solution.py:266
  8.9 7.3 %collective-permute-start.9 = (f32[64,256]{1,0:T(8,128)S(1)}, f32[64,256]{1,0:T(8,128)S(1)}, u32[]{:S(2)}, u32[]{:S(2)}) collective-permute-start(f32[64,256]{1,0:T(8,128)S(1)} %copy-done.2), channel_id=1, source_target_pairs={{0,5},{1,4},{2,7},{3,6},{4,9},{5,8},{6,11},{7,10},{8,13},{9,12},{1... | collective-permute-start | bytes 196616 | tf_op jit(solution)/shard_map/ppermute | solution.py:273
  11.6 16.0 %copy-start.1 = (s32[2,768,256]{2,1,0:T(8,128)S(1)}, s32[2,768,256]{2,1,0:T(8,128)}, u32[]{:S(2)}) copy-start(s32[2,768,256]{2,1,0:T(8,128)} %refs_1_.3) | copy-start | bytes 4718596
  12.3 15.4 %copy-start = (f32[2,768,256]{2,1,0:T(8,128)S(1)}, f32[2,768,256]{2,1,0:T(8,128)}, u32[]{:S(2)}) copy-start(f32[2,768,256]{2,1,0:T(8,128)} %refs_0_.5) | copy-start | bytes 4718596
  12.3 8.3 %collective-permute-start.6 = (f32[128,256]{1,0:T(8,128)S(1)}, f32[128,256]{1,0:T(8,128)S(1)}, u32[]{:S(2)}, u32[]{:S(2)}) collective-permute-start(f32[128,256]{1,0:T(8,128)S(1)} %add.19), channel_id=1, source_target_pairs={{0,5},{1,4},{2,7},{3,6},{4,9},{5,8},{6,11},{7,10},{8,13},{9,12},{1... | collective-permute-start | bytes 393224 | tf_op jit(solution)/shard_map/ppermute | solution.py:273
  12.5 10.9 %collective-permute-start.7 = (f32[128,256]{1,0:T(8,128)S(1)}, f32[128,256]{1,0:T(8,128)S(1)}, u32[]{:S(2)}, u32[]{:S(2)}) collective-permute-start(f32[128,256]{1,0:T(8,128)S(1)} %add.19), channel_id=1, source_target_pairs={{0,7},{1,6},{2,5},{3,4},{4,11},{5,10},{6,9},{7,8},{8,15},{9,14},{1... | collective-permute-start | bytes 393224 | tf_op jit(solution)/shard_map/ppermute | solution.py:273
  16.2 4.3 %collective-permute-start.10 = (f32[64,256]{1,0:T(8,128)S(1)}, f32[64,256]{1,0:T(8,128)S(1)}, u32[]{:S(2)}, u32[]{:S(2)}) collective-permute-start(f32[64,256]{1,0:T(8,128)S(1)} %collective-permute-done.9.refs_0_), channel_id=1, source_target_pairs={{0,2},{1,3},{2,0},{3,1},{4,6},{5,7},{6,4},{7,5},{8,10},{9,11},{10,... | collective-permute-start | bytes 196616 | tf_op jit(solution)/shard_map/ppermute | solution.py:266
  20.5 8.4 %collective-permute-start.11 = (f32[128,256]{1,0:T(8,128)S(1)}, f32[128,256]{1,0:T(8,128)S(1)}, u32[]{:S(2)}, u32[]{:S(2)}) collective-permute-start(f32[128,256]{1,0:T(8,128)S(1)} %shard_map.64.old_own_ref.old_ref), channel_id=1, source_target_pairs={{0,1},{1,0},{2,3},{3,2},{4,5},{5,4},{6,7},{7,6},{8,9},{9,8},{10,11... | collective-permute-start | bytes 393224 | tf_op jit(solution)/shard_map/ppermute | solution.py:266
  23.4 5.5 %collective-permute-start.8 = (f32[128,256]{1,0:T(8,128)S(1)}, f32[128,256]{1,0:T(8,128)S(1)}, u32[]{:S(2)}, u32[]{:S(2)}) collective-permute-start(f32[128,256]{1,0:T(8,128)S(1)} %add.20.own_ref), channel_id=1, source_target_pairs={{0,1},{1,0},{2,3},{3,2},{4,5},{5,4},{6,7},{7,6},{8,9},{9,8},{10,11... | collective-permute-start | bytes 393224 | tf_op jit(solution)/shard_map/ppermute | solution.py:266
  24.2 3.1 %collective-permute-start.3 = (f32[8,128]{1,0:T(8,128)S(1)}, f32[8,128]{1,0:T(8,128)S(1)}, u32[]{:S(2)}, u32[]{:S(2)}) collective-permute-start(f32[8,128]{1,0:T(8,128)S(1)} %get-tuple-element.49), channel_id=1, source_target_pairs={{0,3},{1,2},{2,1},{3,0},{4,7},{5,6},{6,5},{7,4},{8,11},{9,10},{10,... | collective-permute-start | bytes 12296 | tf_op jit(solution)/shard_map/ppermute | solution.py:266
  27.3 1.2 %collective-permute-start.4 = (f32[8,128]{1,0:T(8,128)S(1)}, f32[8,128]{1,0:T(8,128)S(1)}, u32[]{:S(2)}, u32[]{:S(2)}) collective-permute-start(f32[8,128]{1,0:T(8,128)S(1)} %add.18.own_ref), channel_id=1, source_target_pairs={{0,1},{1,0},{2,3},{3,2},{4,5},{5,4},{6,7},{7,6},{8,9},{9,8},{10,11... | collective-permute-start | bytes 12296 | tf_op jit(solution)/shard_map/ppermute | solution.py:266
  29.7 1.4 %collective-permute-start.15 = (f32[128,256]{1,0:T(8,128)S(1)}, f32[128,256]{1,0:T(8,128)S(1)}, u32[]{:S(2)}, u32[]{:S(2)}) collective-permute-start(f32[128,256]{1,0:T(8,128)S(1)} %get-tuple-element.67), channel_id=1, source_target_pairs={{0,1},{1,0},{2,3},{3,2},{4,5},{5,4},{6,7},{7,6},{8,9},{9,8},{10,11... | collective-permute-start | bytes 393224 | tf_op jit(solution)/shard_map/ppermute | solution.py:266
  31.1 7.5 %collective-permute-start.16 = (f32[64,256]{1,0:T(8,128)S(1)}, f32[64,256]{1,0:T(8,128)S(1)}, u32[]{:S(2)}, u32[]{:S(2)}) collective-permute-start(f32[64,256]{1,0:T(8,128)S(1)} %get-tuple-element.71), channel_id=1, source_target_pairs={{0,5},{1,4},{2,7},{3,6},{4,9},{5,8},{6,11},{7,10},{8,13},{9,12},{1... | collective-permute-start | bytes 196616 | tf_op jit(solution)/shard_map/ppermute | solution.py:273
  31.5 7.1 %collective-permute-start.17 = (f32[64,256]{1,0:T(8,128)S(1)}, f32[64,256]{1,0:T(8,128)S(1)}, u32[]{:S(2)}, u32[]{:S(2)}) collective-permute-start(f32[64,256]{1,0:T(8,128)S(1)} %get-tuple-element.70), channel_id=1, source_target_pairs={{0,7},{1,6},{2,5},{3,4},{4,11},{5,10},{6,9},{7,8},{8,15},{9,14},{1... | collective-permute-start | bytes 196616 | tf_op jit(solution)/shard_map/ppermute | solution.py:273
  33.0 8.8 %collective-permute-start.14 = (f32[64,256]{1,0:T(8,128)S(1)}, f32[64,256]{1,0:T(8,128)S(1)}, u32[]{:S(2)}, u32[]{:S(2)}) collective-permute-start(f32[64,256]{1,0:T(8,128)S(1)} %get-tuple-element.65), channel_id=1, source_target_pairs={{0,5},{1,4},{2,7},{3,6},{4,9},{5,8},{6,11},{7,10},{8,13},{9,12},{1... | collective-permute-start | bytes 196616 | tf_op jit(solution)/shard_map/ppermute | solution.py:273
  34.6 3.5 %collective-permute-start.12 = (f32[8,128]{1,0:T(8,128)S(1)}, f32[8,128]{1,0:T(8,128)S(1)}, u32[]{:S(2)}, u32[]{:S(2)}) collective-permute-start(f32[8,128]{1,0:T(8,128)S(1)} %get-tuple-element.64), channel_id=1, source_target_pairs={{0,3},{1,2},{2,1},{3,0},{4,7},{5,6},{6,5},{7,4},{8,11},{9,10},{10,... | collective-permute-start | bytes 12296 | tf_op jit(solution)/shard_map/ppermute | solution.py:266
  38.1 2.6 %collective-permute-start.13 = (f32[8,128]{1,0:T(8,128)S(1)}, f32[8,128]{1,0:T(8,128)S(1)}, u32[]{:S(2)}, u32[]{:S(2)}) collective-permute-start(f32[8,128]{1,0:T(8,128)S(1)} %add.21.refs_0_), channel_id=1, source_target_pairs={{0,1},{1,0},{2,3},{3,2},{4,5},{5,4},{6,7},{7,6},{8,9},{9,8},{10,11... | collective-permute-start | bytes 12296 | tf_op jit(solution)/shard_map/ppermute | solution.py:266
  38.7 3.2 %collective-permute-start.18 = (f32[8,128]{1,0:T(8,128)S(1)}, f32[8,128]{1,0:T(8,128)S(1)}, u32[]{:S(2)}, u32[]{:S(2)}) collective-permute-start(f32[8,128]{1,0:T(8,128)S(1)} %get-tuple-element.69.refs_0_), channel_id=1, source_target_pairs={{0,1},{1,0},{2,3},{3,2},{4,5},{5,4},{6,7},{7,6},{8,9},{9,8},{10,11... | collective-permute-start | bytes 12296 | tf_op jit(solution)/shard_map/ppermute | solution.py:266
  38.8 3.7 %collective-permute-start.19 = (f32[8,128]{1,0:T(8,128)S(1)}, f32[8,128]{1,0:T(8,128)S(1)}, u32[]{:S(2)}, u32[]{:S(2)}) collective-permute-start(f32[8,128]{1,0:T(8,128)S(1)} %get-tuple-element.69.refs_0_), channel_id=1, source_target_pairs={{0,2},{1,3},{2,0},{3,1},{4,6},{5,7},{6,4},{7,5},{8,10},{9,11},{10,... | collective-permute-start | bytes 12296 | tf_op jit(solution)/shard_map/ppermute | solution.py:266
  40.7 3.1 %collective-permute-start.20 = (f32[8,128]{1,0:T(8,128)S(1)}, f32[8,128]{1,0:T(8,128)S(1)}, u32[]{:S(2)}, u32[]{:S(2)}) collective-permute-start(f32[8,128]{1,0:T(8,128)S(1)} %get-tuple-element.69.refs_0_), channel_id=1, source_target_pairs={{0,3},{1,2},{2,1},{3,0},{4,7},{5,6},{6,5},{7,4},{8,11},{9,10},{10,... | collective-permute-start | bytes 12296 | tf_op jit(solution)/shard_map/ppermute | solution.py:266

commit v10 on v9

--- a/solution.py
+++ b/solution.py
@@ -242,10 +242,6 @@
     tile_ref[...] = tile_squares(total)
 
 
-def orders(n):
-    return [(dx, dc) for dx in range(n // CORES) for dc in range(CORES)]
-
-
 def on_device(readings, coverage, pixel_factors, date_factors):
     pixels, rank = pixel_factors.shape
     share = date_factors.shape[0]
@@ -294,7 +290,8 @@
         )
 
     others = [within(date_factors, dx, 1) for dx in range(nx)]
-    owns = chips(date_factors)
+    owns = [date_factors]
+    owns += [within(others[dx], 0, 1) for dx in range(1, nx)]
     old = onward(date_factors, 0)
     values, strip, *halves = prepared(0, WIDE, readings, coverage, pixel_factors)
     values_1, = prepared(1, GRANT, readings, coverage)
@@ -355,10 +352,11 @@
     date_grad, tile = call(
         last_gradient_kernel, [shape(share, rank), shape(8, 128)], *came
     )
-    tiles = [within(tile, *step) for step in orders(n)[1:]]
+    tile = sum([within(tile, dx, 1) for dx in range(1, nx)], tile)
+    other_tile = within(tile, 0, 1)
     date_out, = call(
         functools.partial(step_kernel, date_count), [shape(share, rank)],
-        held, date_grad, tile, *tiles,
+        held, date_grad, tile, other_tile,
     )
     return strip, date_out
 

time: 44.6 us -> 42.4 us (0.951)
  waiting for transfers between devices: 16.2 us -> 14.6 us
  starting transfers between devices: 18.6 us -> 18 us
    ppermute x15 -> x14, waiting for transfers between devices: 13.4 us -> 8.62 us  [within(): return lax.ppermute(value, 'sub', pairs)]
    ppermute x6, waiting for transfers between devices: 2.8 us -> 6.01 us  [onward(): return lax.ppermute(value, ('blk', 'sub'), pairs)]
    ppermute x15 -> x14, starting transfers between devices: 10.9 us -> 9.48 us  [within(): return lax.ppermute(value, 'sub', pairs)]
    ppermute x6, starting transfers between devices: 7.8 us -> 8.56 us  [onward(): return lax.ppermute(value, ('blk', 'sub'), pairs)]
  transfers between devices with their start and end apart: 21 -> 20, of which waited for: 10 -> 9; matrix products, arithmetic and copies ran while one was open for 0% -> 0% of each run, Pallas kernels for 15% -> 15%
where the time goes in v10:
time: 42.4 us; the launch traced here: 42.3 us
  starting transfers between devices  18 us (42%)
  waiting for transfers between devices  14.6 us (34%)
  Pallas kernels  8.73 us (21%)
  between operations  0.8 us (2%)
    ppermute x14, starting transfers between devices, within(): return lax.ppermute(value, 'sub', pairs)  9.48 us
    pallas_call x13, Pallas kernels, call(): pl.pallas_call(kernel, out_shape=outs, in_specs=[where] * len(args), out_...  8.73 us
    ppermute x14, waiting for transfers between devices, within(): return lax.ppermute(value, 'sub', pairs)  8.62 us
    ppermute x6, starting transfers between devices, onward(): return lax.ppermute(value, ('blk', 'sub'), pairs)  8.56 us
    ppermute x6, waiting for transfers between devices, onward(): return lax.ppermute(value, ('blk', 'sub'), pairs)  6.01 us
  transfers between devices with their start and end apart: 20, of which 9 were waited for; matrix products, arithmetic and copies ran while one was open for 0% of the time, Pallas kernels for 15%

profile of v10, /device:TPU:0, one launch (start us, length us, event | category | flops | bytes accessed | tf_op | source)
XLA Modules:
  0.0 42.3 jit_solution(11941255089440516736)
XLA Ops:
  1.2 2.6 %collective-permute-start.1 = (f32[64,256]{1,0:T(8,128)}, f32[64,256]{1,0:T(8,128)S(1)}, u32[]{:S(2)}, u32[]{:S(2)}) collective-permute-start(f32[64,256]{1,0:T(8,128)} %refs_0_.4), channel_id=1, source_target_pairs={{0,3},{1,2},{2,1},{3,0},{4,7},{5,6},{6,5},{7,4},{8,11},{9,10},{10,... | collective-permute-start | bytes 196616 | tf_op jit(solution)/shard_map/ppermute | solution.py:262
  3.8 1.9 %shard_map.59 = (f32[256,768]{1,0:T(8,128)S(1)}, f32[768,256]{1,0:T(8,128)S(1)}, bf16[768,256]{1,0:T(8,128)(2,1)S(1)}, bf16[768,256]{1,0:T(8,128)(2,1)S(1)}, bf1...) custom-call(f32[2,768,256]{2,1,0:T(8,128)} %refs_0_.5, s32[2,768,256]{2,1,0:T(8,128)} %refs_1_.3, f32[768,256]{1,0:T(8,128)} %refs_2_.1), custom_call_target="tpu_custom_call" | custom-call | bytes 7077888 | tf_op jit(solution)/shard_map/pallas_call | solution.py:64
  5.7 0.7 %collective-permute-done.1.refs_1_ = f32[64,256]{1,0:T(8,128)S(1)} collective-permute-done((f32[64,256]{1,0:T(8,128)}, f32[64,256]{1,0:T(8,128)S(1)}, u32[]{:S(2)}, u32[]{:S(2)}) %collective-permute-start.1) | collective-permute-done | bytes 65568 | tf_op jit(solution)/shard_map/ppermute | solution.py:262
  6.4 0.6 %shard_map.60 = (f32[128,256]{1,0:T(8,128)S(1)}, bf16[128,768]{1,0:T(8,128)(2,1)S(1)}, bf16[128,768]{1,0:T(8,128)(2,1)S(1)}, f32[128,256]{1,0:T(8,128)S(1)}) custom-call(f32[64,256]{1,0:T(8,128)S(1)} %collective-permute-done.refs_0_, f32[64,256]{1,0:T(8,128)S(1)} %collective-permute-done.1.refs_1_, f32[256,768]{1,0:T(8,128)S(1)} %get-tuple-element.37.refs_2_, ...), custom_call_target="tpu_custom_call" | custom-call | flops 301989888 | bytes 3145728 | tf_op jit(solution)/shard_map/pallas_call | solution.py:64
  7.6 1.5 %collective-permute-start.9 = (f32[64,256]{1,0:T(8,128)S(1)}, f32[64,256]{1,0:T(8,128)S(1)}, u32[]{:S(2)}, u32[]{:S(2)}) collective-permute-start(f32[64,256]{1,0:T(8,128)S(1)} %copy-done.2), channel_id=1, source_target_pairs={{0,5},{1,4},{2,7},{3,6},{4,9},{5,8},{6,11},{7,10},{8,13},{9,12},{1... | collective-permute-start | bytes 196616 | tf_op jit(solution)/shard_map/ppermute | solution.py:269
  9.1 0.6 %shard_map.61 = (f32[128,256]{1,0:T(8,128)S(1)}, bf16[128,768]{1,0:T(8,128)(2,1)S(1)}, bf16[128,768]{1,0:T(8,128)(2,1)S(1)}, f32[128,256]{1,0:T(8,128)S(1)}) custom-call(f32[64,256]{1,0:T(8,128)S(1)} %copy-done.2, f32[64,256]{1,0:T(8,128)S(1)} %collective-permute-done.2.refs_1_, f32[256,768]{1,0:T(8,128)S(1)} %get-tuple-element.37.refs_2_, ...), custom_call_target="tpu_custom_call" | custom-call | flops 301989888 | bytes 3145728 | tf_op jit(solution)/shard_map/pallas_call | solution.py:64
  9.8 1.3 %collective-permute-start.6 = (f32[128,256]{1,0:T(8,128)S(1)}, f32[128,256]{1,0:T(8,128)S(1)}, u32[]{:S(2)}, u32[]{:S(2)}) collective-permute-start(f32[128,256]{1,0:T(8,128)S(1)} %add.22), channel_id=1, source_target_pairs={{0,5},{1,4},{2,7},{3,6},{4,9},{5,8},{6,11},{7,10},{8,13},{9,12},{1... | collective-permute-start | bytes 393224 | tf_op jit(solution)/shard_map/ppermute | solution.py:269
  11.1 2.5 %collective-permute-start.7 = (f32[128,256]{1,0:T(8,128)S(1)}, f32[128,256]{1,0:T(8,128)S(1)}, u32[]{:S(2)}, u32[]{:S(2)}) collective-permute-start(f32[128,256]{1,0:T(8,128)S(1)} %add.22), channel_id=1, source_target_pairs={{0,7},{1,6},{2,5},{3,4},{4,11},{5,10},{6,9},{7,8},{8,15},{9,14},{1... | collective-permute-start | bytes 393224 | tf_op jit(solution)/shard_map/ppermute | solution.py:269
  13.7 1.1 %collective-permute-start.10 = (f32[64,256]{1,0:T(8,128)S(1)}, f32[64,256]{1,0:T(8,128)S(1)}, u32[]{:S(2)}, u32[]{:S(2)}) collective-permute-start(f32[64,256]{1,0:T(8,128)S(1)} %collective-permute-done.9.refs_0_), channel_id=1, source_target_pairs={{0,2},{1,3},{2,0},{3,1},{4,6},{5,7},{6,4},{7,5},{8,10},{9,11},{10,... | collective-permute-start | bytes 196616 | tf_op jit(solution)/shard_map/ppermute | solution.py:262
  14.7 3.2 %collective-permute-done.10.refs_1_ = f32[64,256]{1,0:T(8,128)S(1)} collective-permute-done((f32[64,256]{1,0:T(8,128)S(1)}, f32[64,256]{1,0:T(8,128)S(1)}, u32[]{:S(2)}, u32[]{:S(2)}) %collective-permute-start.10) | collective-permute-done | bytes 65568 | tf_op jit(solution)/shard_map/ppermute | solution.py:262
  18.0 2.9 %collective-permute-done.7 = f32[128,256]{1,0:T(8,128)S(1)} collective-permute-done((f32[128,256]{1,0:T(8,128)S(1)}, f32[128,256]{1,0:T(8,128)S(1)}, u32[]{:S(2)}, u32[]{:S(2)}) %collective-permute-start.7) | collective-permute-done | bytes 131104 | tf_op jit(solution)/shard_map/ppermute | solution.py:269
  21.6 1.2 %collective-permute-start.3 = (f32[8,128]{1,0:T(8,128)S(1)}, f32[8,128]{1,0:T(8,128)S(1)}, u32[]{:S(2)}, u32[]{:S(2)}) collective-permute-start(f32[8,128]{1,0:T(8,128)S(1)} %get-tuple-element.49), channel_id=1, source_target_pairs={{0,3},{1,2},{2,1},{3,0},{4,7},{5,6},{6,5},{7,4},{8,11},{9,10},{10,... | collective-permute-start | bytes 12296 | tf_op jit(solution)/shard_map/ppermute | solution.py:262
  22.8 1.9 %collective-permute-done.3 = f32[8,128]{1,0:T(8,128)S(1)} collective-permute-done((f32[8,128]{1,0:T(8,128)S(1)}, f32[8,128]{1,0:T(8,128)S(1)}, u32[]{:S(2)}, u32[]{:S(2)}) %collective-permute-start.3) | collective-permute-done | bytes 4128 | tf_op jit(solution)/shard_map/ppermute | solution.py:262
  26.4 0.8 %shard_map.66 = (f32[128,256]{1,0:T(8,128)S(1)}, bf16[128,768]{1,0:T(8,128)(2,1)S(1)}, bf16[128,768]{1,0:T(8,128)(2,1)S(1)}, f32[128,256]{1,0:T(8,128)S(1)}, f32[64,256]{1,0:T(8,128)S(1)}) custom-call(f32[128,256]{1,0:T(8,128)S(1)} %add.23.own_ref, f32[128,256]{1,0:T(8,128)S(1)} %collective-permute-done.8.other_ref, ...), custom_call_target="tpu_custom_call" | custom-call | flops 301989888 | bytes 3604480 | tf_op jit(solution)/shard_map/pallas_call | solution.py:64
  27.6 0.8 %shard_map.67 = (f32[128,256]{1,0:T(8,128)S(1)}, bf16[128,768]{1,0:T(8,128)(2,1)S(1)}, bf16[128,768]{1,0:T(8,128)(2,1)S(1)}, f32[128,256]{1,0:T(8,128)S(1)}) custom-call(f32[128,256]{1,0:T(8,128)S(1)} %add.23.own_ref, f32[128,256]{1,0:T(8,128)S(1)} %collective-permute-done.8.other_ref, f32[128,256]{1,0:T(8,128)S(1)} %shard_map.64.old_own_ref.old_ref, ...), custom_call_target="tpu_custom_call" | custom-call | flops 301989888 | bytes 3407872 | tf_op jit(solution)/shard_map/pallas_call | solution.py:64
  28.7 1.1 %collective-permute-start.16 = (f32[64,256]{1,0:T(8,128)S(1)}, f32[64,256]{1,0:T(8,128)S(1)}, u32[]{:S(2)}, u32[]{:S(2)}) collective-permute-start(f32[64,256]{1,0:T(8,128)S(1)} %get-tuple-element.71), channel_id=1, source_target_pairs={{0,5},{1,4},{2,7},{3,6},{4,9},{5,8},{6,11},{7,10},{8,13},{9,12},{1... | collective-permute-start | bytes 196616 | tf_op jit(solution)/shard_map/ppermute | solution.py:269
  29.8 2.0 %collective-permute-start.14 = (f32[64,256]{1,0:T(8,128)S(1)}, f32[64,256]{1,0:T(8,128)S(1)}, u32[]{:S(2)}, u32[]{:S(2)}) collective-permute-start(f32[64,256]{1,0:T(8,128)S(1)} %get-tuple-element.65), channel_id=1, source_target_pairs={{0,5},{1,4},{2,7},{3,6},{4,9},{5,8},{6,11},{7,10},{8,13},{9,12},{1... | collective-permute-start | bytes 196616 | tf_op jit(solution)/shard_map/ppermute | solution.py:269
  32.4 1.4 %collective-permute-start.12 = (f32[8,128]{1,0:T(8,128)S(1)}, f32[8,128]{1,0:T(8,128)S(1)}, u32[]{:S(2)}, u32[]{:S(2)}) collective-permute-start(f32[8,128]{1,0:T(8,128)S(1)} %get-tuple-element.64), channel_id=1, source_target_pairs={{0,3},{1,2},{2,1},{3,0},{4,7},{5,6},{6,5},{7,4},{8,11},{9,10},{10,... | collective-permute-start | bytes 12296 | tf_op jit(solution)/shard_map/ppermute | solution.py:262
  33.8 0.6 %collective-permute-done.16.refs_0_ = f32[64,256]{1,0:T(8,128)S(1)} collective-permute-done((f32[64,256]{1,0:T(8,128)S(1)}, f32[64,256]{1,0:T(8,128)S(1)}, u32[]{:S(2)}, u32[]{:S(2)}) %collective-permute-start.16) | collective-permute-done | bytes 65568 | tf_op jit(solution)/shard_map/ppermute | solution.py:269
  34.4 2.5 %collective-permute-done.17.refs_1_ = f32[64,256]{1,0:T(8,128)S(1)} collective-permute-done((f32[64,256]{1,0:T(8,128)S(1)}, f32[64,256]{1,0:T(8,128)S(1)}, u32[]{:S(2)}, u32[]{:S(2)}) %collective-permute-start.17) | collective-permute-done | bytes 65568 | tf_op jit(solution)/shard_map/ppermute | solution.py:269
  36.9 0.7 %collective-permute-start.18 = (f32[8,128]{1,0:T(8,128)S(1)}, f32[8,128]{1,0:T(8,128)S(1)}, u32[]{:S(2)}, u32[]{:S(2)}) collective-permute-start(f32[8,128]{1,0:T(8,128)S(1)} %get-tuple-element.69), channel_id=1, source_target_pairs={{0,3},{1,2},{2,1},{3,0},{4,7},{5,6},{6,5},{7,4},{8,11},{9,10},{10,... | collective-permute-start | bytes 12296 | tf_op jit(solution)/shard_map/ppermute | solution.py:262
  37.7 2.3 %collective-permute-done.18 = f32[8,128]{1,0:T(8,128)S(1)} collective-permute-done((f32[8,128]{1,0:T(8,128)S(1)}, f32[8,128]{1,0:T(8,128)S(1)}, u32[]{:S(2)}, u32[]{:S(2)}) %collective-permute-start.18) | collective-permute-done | bytes 4128 | tf_op jit(solution)/shard_map/ppermute | solution.py:262
  40.4 1.2 %shard_map.69 = f32[768,256]{1,0:T(8,128)} custom-call(f32[768,256]{1,0:T(8,128)S(1)} %get-tuple-element.50.strip_ref.held_ref, f32[768,256]{1,0:T(8,128)S(1)} %get-tuple-element.63.grad_ref, f32[8,128]{1,0:T(8,128)S(1)} %add.24.refs_0_, f32[8,128]{1,0:T(8,128)S(1)} %collective-permute-done.13.refs_1_), custom_call_target="tpu_custom_call" | custom-call | bytes 2367488 | tf_op jit(solution)/shard_map/pallas_call | solution.py:64
  41.5 0.8 %shard_map.71 = f32[64,256]{1,0:T(8,128)} custom-call(f32[64,256]{1,0:T(8,128)S(1)} %collective-permute-done.14.held_ref, f32[64,256]{1,0:T(8,128)S(1)} %get-tuple-element.68.grad_ref, f32[8,128]{1,0:T(8,128)S(1)} %add.27.refs_0_, f32[8,128]{1,0:T(8,128)S(1)} %collective-permute-done.19.refs_1_), custom_call_target="tpu_custom_call" | custom-call | bytes 204800 | tf_op jit(solution)/shard_map/pallas_call | solution.py:64
  (41 shorter events, 5.2 us)
Async XLA Ops:
  0.6 5.0 %collective-permute-start = (f32[64,256]{1,0:T(8,128)}, f32[64,256]{1,0:T(8,128)S(1)}, u32[]{:S(2)}, u32[]{:S(2)}) collective-permute-start(f32[64,256]{1,0:T(8,128)} %refs_0_.4), channel_id=1, source_target_pairs={{0,1},{1,0},{2,3},{3,2},{4,5},{5,4},{6,7},{7,6},{8,9},{9,8},{10,11... | collective-permute-start | bytes 196616 | tf_op jit(solution)/shard_map/ppermute | solution.py:262
  1.2 5.2 %collective-permute-start.1 = (f32[64,256]{1,0:T(8,128)}, f32[64,256]{1,0:T(8,128)S(1)}, u32[]{:S(2)}, u32[]{:S(2)}) collective-permute-start(f32[64,256]{1,0:T(8,128)} %refs_0_.4), channel_id=1, source_target_pairs={{0,3},{1,2},{2,1},{3,0},{4,7},{5,6},{6,5},{7,4},{8,11},{9,10},{10,... | collective-permute-start | bytes 196616 | tf_op jit(solution)/shard_map/ppermute | solution.py:262
  5.6 1.9 %copy-start.2 = (f32[64,256]{1,0:T(8,128)S(1)}, f32[64,256]{1,0:T(8,128)}, u32[]{:S(2)}) copy-start(f32[64,256]{1,0:T(8,128)} %refs_0_.4) | copy-start | bytes 196612
  7.0 2.7 %collective-permute-start.5 = (f32[128,256]{1,0:T(8,128)S(1)}, f32[128,256]{1,0:T(8,128)S(1)}, u32[]{:S(2)}, u32[]{:S(2)}) collective-permute-start(f32[128,256]{1,0:T(8,128)S(1)} %get-tuple-element.52), channel_id=1, source_target_pairs={{0,1},{1,0},{2,3},{3,2},{4,5},{5,4},{6,7},{7,6},{8,9},{9,8},{10,11... | collective-permute-start | bytes 393224 | tf_op jit(solution)/shard_map/ppermute | solution.py:262
  7.2 1.9 %collective-permute-start.2 = (f32[64,256]{1,0:T(8,128)S(1)}, f32[64,256]{1,0:T(8,128)S(1)}, u32[]{:S(2)}, u32[]{:S(2)}) collective-permute-start(f32[64,256]{1,0:T(8,128)S(1)} %collective-permute-done.1.refs_1_), channel_id=1, source_target_pairs={{0,1},{1,0},{2,3},{3,2},{4,5},{5,4},{6,7},{7,6},{8,9},{9,8},{10,11... | collective-permute-start | bytes 196616 | tf_op jit(solution)/shard_map/ppermute | solution.py:262
  7.6 6.1 %collective-permute-start.9 = (f32[64,256]{1,0:T(8,128)S(1)}, f32[64,256]{1,0:T(8,128)S(1)}, u32[]{:S(2)}, u32[]{:S(2)}) collective-permute-start(f32[64,256]{1,0:T(8,128)S(1)} %copy-done.2), channel_id=1, source_target_pairs={{0,5},{1,4},{2,7},{3,6},{4,9},{5,8},{6,11},{7,10},{8,13},{9,12},{1... | collective-permute-start | bytes 196616 | tf_op jit(solution)/shard_map/ppermute | solution.py:269
  9.1 16.1 %copy-start.1 = (s32[2,768,256]{2,1,0:T(8,128)S(1)}, s32[2,768,256]{2,1,0:T(8,128)}, u32[]{:S(2)}) copy-start(s32[2,768,256]{2,1,0:T(8,128)} %refs_1_.3) | copy-start | bytes 4718596
  9.7 15.4 %copy-start = (f32[2,768,256]{2,1,0:T(8,128)S(1)}, f32[2,768,256]{2,1,0:T(8,128)}, u32[]{:S(2)}) copy-start(f32[2,768,256]{2,1,0:T(8,128)} %refs_0_.5) | copy-start | bytes 4718596
  9.8 8.2 %collective-permute-start.6 = (f32[128,256]{1,0:T(8,128)S(1)}, f32[128,256]{1,0:T(8,128)S(1)}, u32[]{:S(2)}, u32[]{:S(2)}) collective-permute-start(f32[128,256]{1,0:T(8,128)S(1)} %add.22), channel_id=1, source_target_pairs={{0,5},{1,4},{2,7},{3,6},{4,9},{5,8},{6,11},{7,10},{8,13},{9,12},{1... | collective-permute-start | bytes 393224 | tf_op jit(solution)/shard_map/ppermute | solution.py:269
  11.1 9.8 %collective-permute-start.7 = (f32[128,256]{1,0:T(8,128)S(1)}, f32[128,256]{1,0:T(8,128)S(1)}, u32[]{:S(2)}, u32[]{:S(2)}) collective-permute-start(f32[128,256]{1,0:T(8,128)S(1)} %add.22), channel_id=1, source_target_pairs={{0,7},{1,6},{2,5},{3,4},{4,11},{5,10},{6,9},{7,8},{8,15},{9,14},{1... | collective-permute-start | bytes 393224 | tf_op jit(solution)/shard_map/ppermute | solution.py:269
  13.7 4.3 %collective-permute-start.10 = (f32[64,256]{1,0:T(8,128)S(1)}, f32[64,256]{1,0:T(8,128)S(1)}, u32[]{:S(2)}, u32[]{:S(2)}) collective-permute-start(f32[64,256]{1,0:T(8,128)S(1)} %collective-permute-done.9.refs_0_), channel_id=1, source_target_pairs={{0,2},{1,3},{2,0},{3,1},{4,6},{5,7},{6,4},{7,5},{8,10},{9,11},{10,... | collective-permute-start | bytes 196616 | tf_op jit(solution)/shard_map/ppermute | solution.py:262
  17.9 8.5 %collective-permute-start.11 = (f32[128,256]{1,0:T(8,128)S(1)}, f32[128,256]{1,0:T(8,128)S(1)}, u32[]{:S(2)}, u32[]{:S(2)}) collective-permute-start(f32[128,256]{1,0:T(8,128)S(1)} %shard_map.64.old_own_ref.old_ref), channel_id=1, source_target_pairs={{0,1},{1,0},{2,3},{3,2},{4,5},{5,4},{6,7},{7,6},{8,9},{9,8},{10,11... | collective-permute-start | bytes 393224 | tf_op jit(solution)/shard_map/ppermute | solution.py:262
  20.9 5.5 %collective-permute-start.8 = (f32[128,256]{1,0:T(8,128)S(1)}, f32[128,256]{1,0:T(8,128)S(1)}, u32[]{:S(2)}, u32[]{:S(2)}) collective-permute-start(f32[128,256]{1,0:T(8,128)S(1)} %add.23.own_ref), channel_id=1, source_target_pairs={{0,1},{1,0},{2,3},{3,2},{4,5},{5,4},{6,7},{7,6},{8,9},{9,8},{10,11... | collective-permute-start | bytes 393224 | tf_op jit(solution)/shard_map/ppermute | solution.py:262
  21.6 3.1 %collective-permute-start.3 = (f32[8,128]{1,0:T(8,128)S(1)}, f32[8,128]{1,0:T(8,128)S(1)}, u32[]{:S(2)}, u32[]{:S(2)}) collective-permute-start(f32[8,128]{1,0:T(8,128)S(1)} %get-tuple-element.49), channel_id=1, source_target_pairs={{0,3},{1,2},{2,1},{3,0},{4,7},{5,6},{6,5},{7,4},{8,11},{9,10},{10,... | collective-permute-start | bytes 12296 | tf_op jit(solution)/shard_map/ppermute | solution.py:262
  24.7 1.2 %collective-permute-start.4 = (f32[8,128]{1,0:T(8,128)S(1)}, f32[8,128]{1,0:T(8,128)S(1)}, u32[]{:S(2)}, u32[]{:S(2)}) collective-permute-start(f32[8,128]{1,0:T(8,128)S(1)} %add.21.own_ref), channel_id=1, source_target_pairs={{0,1},{1,0},{2,3},{3,2},{4,5},{5,4},{6,7},{7,6},{8,9},{9,8},{10,11... | collective-permute-start | bytes 12296 | tf_op jit(solution)/shard_map/ppermute | solution.py:262
  27.2 1.4 %collective-permute-start.15 = (f32[128,256]{1,0:T(8,128)S(1)}, f32[128,256]{1,0:T(8,128)S(1)}, u32[]{:S(2)}, u32[]{:S(2)}) collective-permute-start(f32[128,256]{1,0:T(8,128)S(1)} %get-tuple-element.67), channel_id=1, source_target_pairs={{0,1},{1,0},{2,3},{3,2},{4,5},{5,4},{6,7},{7,6},{8,9},{9,8},{10,11... | collective-permute-start | bytes 393224 | tf_op jit(solution)/shard_map/ppermute | solution.py:262
  28.7 5.7 %collective-permute-start.16 = (f32[64,256]{1,0:T(8,128)S(1)}, f32[64,256]{1,0:T(8,128)S(1)}, u32[]{:S(2)}, u32[]{:S(2)}) collective-permute-start(f32[64,256]{1,0:T(8,128)S(1)} %get-tuple-element.71), channel_id=1, source_target_pairs={{0,5},{1,4},{2,7},{3,6},{4,9},{5,8},{6,11},{7,10},{8,13},{9,12},{1... | collective-permute-start | bytes 196616 | tf_op jit(solution)/shard_map/ppermute | solution.py:269
  29.8 7.1 %collective-permute-start.17 = (f32[64,256]{1,0:T(8,128)S(1)}, f32[64,256]{1,0:T(8,128)S(1)}, u32[]{:S(2)}, u32[]{:S(2)}) collective-permute-start(f32[64,256]{1,0:T(8,128)S(1)} %get-tuple-element.70), channel_id=1, source_target_pairs={{0,7},{1,6},{2,5},{3,4},{4,11},{5,10},{6,9},{7,8},{8,15},{9,14},{1... | collective-permute-start | bytes 196616 | tf_op jit(solution)/shard_map/ppermute | solution.py:269
  29.8 11.7 %collective-permute-start.14 = (f32[64,256]{1,0:T(8,128)S(1)}, f32[64,256]{1,0:T(8,128)S(1)}, u32[]{:S(2)}, u32[]{:S(2)}) collective-permute-start(f32[64,256]{1,0:T(8,128)S(1)} %get-tuple-element.65), channel_id=1, source_target_pairs={{0,5},{1,4},{2,7},{3,6},{4,9},{5,8},{6,11},{7,10},{8,13},{9,12},{1... | collective-permute-start | bytes 196616 | tf_op jit(solution)/shard_map/ppermute | solution.py:269
  32.4 5.2 %collective-permute-start.12 = (f32[8,128]{1,0:T(8,128)S(1)}, f32[8,128]{1,0:T(8,128)S(1)}, u32[]{:S(2)}, u32[]{:S(2)}) collective-permute-start(f32[8,128]{1,0:T(8,128)S(1)} %get-tuple-element.64), channel_id=1, source_target_pairs={{0,3},{1,2},{2,1},{3,0},{4,7},{5,6},{6,5},{7,4},{8,11},{9,10},{10,... | collective-permute-start | bytes 12296 | tf_op jit(solution)/shard_map/ppermute | solution.py:262
  36.9 3.1 %collective-permute-start.18 = (f32[8,128]{1,0:T(8,128)S(1)}, f32[8,128]{1,0:T(8,128)S(1)}, u32[]{:S(2)}, u32[]{:S(2)}) collective-permute-start(f32[8,128]{1,0:T(8,128)S(1)} %get-tuple-element.69), channel_id=1, source_target_pairs={{0,3},{1,2},{2,1},{3,0},{4,7},{5,6},{6,5},{7,4},{8,11},{9,10},{10,... | collective-permute-start | bytes 12296 | tf_op jit(solution)/shard_map/ppermute | solution.py:262
  37.6 2.7 %collective-permute-start.13 = (f32[8,128]{1,0:T(8,128)S(1)}, f32[8,128]{1,0:T(8,128)S(1)}, u32[]{:S(2)}, u32[]{:S(2)}) collective-permute-start(f32[8,128]{1,0:T(8,128)S(1)} %add.24.refs_0_), channel_id=1, source_target_pairs={{0,1},{1,0},{2,3},{3,2},{4,5},{5,4},{6,7},{7,6},{8,9},{9,8},{10,11... | collective-permute-start | bytes 12296 | tf_op jit(solution)/shard_map/ppermute | solution.py:262
  40.0 1.5 %collective-permute-start.19 = (f32[8,128]{1,0:T(8,128)S(1)}, f32[8,128]{1,0:T(8,128)S(1)}, u32[]{:S(2)}, u32[]{:S(2)}) collective-permute-start(f32[8,128]{1,0:T(8,128)S(1)} %add.27.refs_0_), channel_id=1, source_target_pairs={{0,1},{1,0},{2,3},{3,2},{4,5},{5,4},{6,7},{7,6},{8,9},{9,8},{10,11... | collective-permute-start | bytes 12296 | tf_op jit(solution)/shard_map/ppermute | solution.py:262
